TPU v7x, 128 devices: a whole 4x4x4 slice. The times are simulated.
128 devices in a mesh: region: 4 (over x), block: 32 (over z, y, core).
Axes of the slice: x: 4, y: 4, z: 4, core: 2. Of those that a mesh axis runs over, the one named last changes fastest.
Arguments:
- env_left: float32 [4, 17, 32, 128, 128], P('region', None, 'block'), may hold values from -6 to 6
- env_right: float32 [4, 17, 32, 128, 128], P('region', None, 'block'), may hold values from -0.125 to 0.125
- site_tensors: float32 [4, 2, 4, 32, 128, 128], P('region', None, None, 'block'), may hold values from -0.5 to 0.5
- pair_state: float32 [4, 16, 32, 128, 128], P('region', None, 'block'), may hold values from -0.5 to 0.5
- mpo_sites: float32 [4, 2, 17, 17, 4, 4], P('region'), may hold values from -0.75 to 0.75
- mpo_pair: float32 [4, 2, 17, 17, 4, 4], P('region'), may hold values from -0.75 to 0.75
- channel_class: int32 [17], replicated, may hold values from 0 to 4, as said below
- live_rows: int32 [4, 3, 32], P('region'), may hold values from 64 to 128, as said below
- region_sites: int32 [4], P('region'), may hold values from 1 to 2, as said below
Outputs:
- new_env: float32 [4, 17, 32, 128, 128], P('region', None, 'block')
- pair_image: float32 [4, 16, 32, 128, 128], P('region', None, 'block')
Inputs may be any that keep to these rules, and one draw needn't show every extreme that they name: `channel_class`: each of the five classes is taken by at least 3 channels. `live_rows`: every bond of every region has a sector with exactly 128 live states. `region_sites`: some region updates exactly 2 sites.
All inputs are finite; a program needn't handle non-finite values.
Results may differ from a plain program's by a relative error of at most 0.0001.
Values sent between devices are 32-bit elements; how exact they have to be, the bound alone decides.
No kernel may reach another device: no remote copies, remote signals or barrier semaphores. Data moves between devices by JAX's collectives and lax.ppermute only.
A program may use at most 192 MiB of HBM per device.

v0:
```python
import functools
import jax
import jax.numpy as jnp
from jax import lax
from jax.experimental import pallas as pl
from jax.experimental.pallas import tpu as pltpu
from jax.sharding import PartitionSpec as P

NSEC = 32
TILE = 128
NW = 17
ND = 8
MAXLEN = 2
STATE_STEPS = (0, ND, 1, ND + 1)
CLASS_STEPS = (0, 1, -1, ND, -ND)
LONG = 11
SHORT = 5
RULE = NW * NW * 16
PADDED = RULE + NW * 16
F32 = jnp.float32
BF16 = jnp.bfloat16


def mix_tables(channel_class):
    steps = jnp.array(STATE_STEPS, dtype=jnp.int32)
    shifts = class_shift(channel_class)
    down = (jnp.arange(4) // 2)[:, None]
    up = (jnp.arange(4) % 2)[:, None]
    kind = channel_class[None, :]
    three = (
        (kind == 0)
        | ((kind == 1) & (down == 0))
        | ((kind == 2) & (down == 1))
        | ((kind == 3) & (up == 0))
        | ((kind == 4) & (up == 1))
    )
    channels = jnp.arange(NW, dtype=jnp.int32)
    key = jnp.where(three, 0, NW) + channels[None, :]
    place = (key[:, None, :] < key[:, :, None]).astype(jnp.int32).sum(-1)
    hot = place[:, None, :] == channels[None, :, None]
    out = jnp.where(hot, channels, 0).sum(-1)
    goal = jnp.where(hot, shifts, 0).sum(-1)
    source = shifts[:, None] + steps[None, :]
    allowed = (goal + steps[:, None])[:, :, None] == source.reshape(-1)[None, None, :]
    size = 4 * NW
    order = jnp.arange(size, dtype=jnp.int32)
    earlier = (order[:, None] < order[None, :]).astype(F32)
    rank = jnp.einsum("sim,mn->sin", allowed.astype(F32), earlier).astype(jnp.int32)
    term = allowed[:, :, None, :] & (rank[:, :, None, :] == jnp.arange(LONG)[:, None])
    count = allowed.astype(jnp.int32).sum(-1)
    block = jnp.where(term, order, 0).sum(-1)
    used = jnp.arange(LONG) < count[:, :, None]
    place = (block // 4) * (NW * 16) + block % 4
    place = jnp.where(used, place, RULE) + (out * 16 + 4 * jnp.arange(4)[:, None])[:, :, None]
    return out.reshape(-1), block.reshape(-1), place.reshape(-1)


def class_shift(kind):
    return jnp.where(kind == 1, 1, jnp.where(kind == 2, -1, jnp.where(kind == 3, ND, jnp.where(kind == 4, -ND, 0))))


def inside(sector):
    return ((sector >= 0) & (sector < NSEC)).astype(F32)


def split(x):
    high = x.astype(BF16)
    return high, (x - high.astype(F32)).astype(BF16)


def mix(blocks, base, block_ref, place_ref, rule_ref, rule, first, terms):
    total = None
    for k in range(terms):
        term = blocks[base + block_ref[first + k]] * rule_ref[rule * PADDED + place_ref[first + k]]
        total = term if total is None else total + term
    return total


def stacked(x):
    row = jnp.concatenate(split(x), axis=1)
    return jnp.concatenate([row, row], axis=0)


def folded(x):
    return x[:, :TILE] + x[:, TILE:]


def dot(a, b):
    return jnp.dot(a, b, preferred_element_type=F32)


def loop(start, stop, body, unroll):
    lax.fori_loop(start, stop, lambda i, c: (body(i), c)[1], 0, unroll=unroll)


def site_kernel(
    number, sector_ref, class_ref, live_ref, out_ref, block_ref, place_ref, rule_ref, *refs
):
    if number == 0:
        env_ref, *refs = refs
    else:
        low_ref, below_ref, above_ref, *refs = refs
    kets_refs, refs = refs[:5], refs[5:]
    closed_refs, refs = refs[:4], refs[4:]
    if number > 0:
        first_ref, *refs = refs
    kets, product, bras, _ = refs
    sector = sector_ref[0]

    for c, ref in enumerate(kets_refs):
        for t in range(4):
            keep = inside(sector + CLASS_STEPS[c] + STATE_STEPS[t])
            high, low = split(ref[0, t].T * keep)
            kets[c, t * TILE : (t + 1) * TILE, :TILE] = high
            kets[c, t * TILE : (t + 1) * TILE, TILE:] = low
    for s in range(4):
        bras[s] = stacked(kets_refs[0][0, s] * inside(sector + STATE_STEPS[s]))

    rows = lax.broadcasted_iota(jnp.int32, (TILE, TILE), 1)
    columns = lax.broadcasted_iota(jnp.int32, (TILE, TILE), 0)

    def environment(w):
        ket = sector + class_shift(class_ref[w])
        keep = inside(ket)
        if number == 0:
            return (env_ref[w] * keep).T
        count = jnp.where(keep > 0, live_ref[(number - 1) * NSEC + jnp.clip(ket, 0, NSEC - 1)], 0)
        own = live_ref[(number - 1) * NSEC + sector]
        total = low_ref[w] + below_ref[w] + above_ref[w]
        total = jnp.where((rows < own) & (columns < count), total, 0.0)
        first_ref[w] = total
        return total

    def form(w):
        result = folded(dot(kets[class_ref[w]], stacked(environment(w))))
        product[pl.ds(4 * w, 4)] = result.reshape(4, TILE, TILE)

    loop(0, NW, form, 1)

    for s in (3, 2, 1, 0):

        def close(terms, i):
            place = s * NW + i
            total = mix(product, 0, block_ref, place_ref, rule_ref, number, place * LONG, terms)
            result = folded(dot(jnp.concatenate(split(total), axis=1), bras[s]))
            closed_refs[s][out_ref[place]] = result

        loop(0, LONG, functools.partial(close, LONG), UNROLL_LONG)
        loop(LONG, NW, functools.partial(close, SHORT), UNROLL_SHORT)


UNROLL_LONG = 11
UNROLL_SHORT = 6
SMEM_SPEC = pl.BlockSpec(memory_space=pltpu.SMEM)
VMEM_SPEC = pl.BlockSpec(memory_space=pltpu.VMEM)
HBM_SPEC = pl.BlockSpec(memory_space=pl.ANY)


def site(number, scalars, envs, kets):
    block = jax.ShapeDtypeStruct((NW, TILE, TILE), F32)
    count = 4 if number == 0 else 5
    ket_spec = pl.BlockSpec((1, 4, TILE, TILE), lambda i: (number, 0, 0, 0))
    return pl.pallas_call(
        functools.partial(site_kernel, number),
        grid=(1,),
        out_shape=[block] * count,
        in_specs=[SMEM_SPEC] * 7 + [VMEM_SPEC] * len(envs) + [ket_spec] * 5,
        out_specs=[VMEM_SPEC] * count,
        scratch_shapes=[
            pltpu.VMEM((5, 4 * TILE, 2 * TILE), BF16),
            pltpu.VMEM((4 * NW, TILE, TILE), F32),
            pltpu.VMEM((4, 2 * TILE, 2 * TILE), BF16),
            pltpu.VMEM((2 * TILE, 2 * TILE), BF16),
        ],
        compiler_params=pltpu.CompilerParams(vmem_limit_bytes=40 * 2**20),
        cost_estimate=pl.CostEstimate(flops=4 * 10**9, bytes_accessed=10**7, transcendentals=0),
    )(*scalars, *envs, *kets)


def kets_kernel(sector_ref, k0, k1, k2, k3, k4, out_ref):
    t2 = pl.program_id(0)
    step2 = (t2 % 2) * ND + t2 // 2
    for c, ref in enumerate((k0, k1, k2, k3, k4)):
        for t1 in range(4):
            keep = inside(sector_ref[0] + CLASS_STEPS[c] + STATE_STEPS[t1] + step2)
            high, low = split(ref[t1, 0].T * keep)
            out_ref[0, c, t1 * TILE : (t1 + 1) * TILE, :TILE] = high
            out_ref[0, c, t1 * TILE : (t1 + 1) * TILE, TILE:] = low


def split_kets(sector, kets):
    return pl.pallas_call(
        kets_kernel,
        grid=(4,),
        out_shape=jax.ShapeDtypeStruct((4, 5, 4 * TILE, 2 * TILE), BF16),
        in_specs=[SMEM_SPEC] + [pl.BlockSpec((4, 1, TILE, TILE), lambda i: (0, i, 0, 0))] * 5,
        out_specs=pl.BlockSpec((1, 5, 4 * TILE, 2 * TILE), lambda i: (i, 0, 0, 0)),
        cost_estimate=pl.CostEstimate(flops=5 * 10**6, bytes_accessed=10**7, transcendentals=0),
        name="split_kets",
    )(sector, *[k.reshape(4, 4, TILE, TILE) for k in kets])


def pair_kernel(
    sector_ref, region_ref, class_ref, live_ref, out_ref, block_ref, place_ref, rule_ref, p_ref,
    start_ref, passed0_ref, passed1_ref, kets_hbm, *refs,
):
    rights_hbm, (image_ref, kets, rights, envs, product, middle, lhs, outer, sems) = refs[:9], refs[9:]
    sector = sector_ref[0]

    def kets_copy(t):
        return pltpu.make_async_copy(kets_hbm.at[t], kets.at[t], sems.at[t])

    rights_copies = [
        pltpu.make_async_copy(ref, rights.at[n], sems.at[4 + n]) for n, ref in enumerate(rights_hbm)
    ]
    for t in range(4):
        kets_copy(t).start()
    for copy in rights_copies:
        copy.start()

    @pl.when(region_ref[0] == 0)
    def _():
        def own(w):
            keep = inside(sector + class_shift(class_ref[w]))
            envs[w] = stacked((start_ref[w] * keep).T)

        loop(0, NW, own, 1)

    @pl.when(region_ref[0] != 0)
    def _():
        for first, ref in ((0, passed0_ref), (9, passed1_ref)):
            for n in range(ref.shape[0]):
                envs[first + n] = stacked(ref[n])

    def left_half(t2):
        kets_copy(t2).wait()

        def form(w):
            result = folded(dot(kets[t2, class_ref[w]], envs[w]))
            product[pl.ds(4 * w, 4)] = result.reshape(4, TILE, TILE)

        loop(0, NW, form, 1)

        def left(s):
            for i in range(NW):
                place = s * NW + i
                terms = LONG if i < LONG else SHORT
                total = mix(product, 0, block_ref, place_ref, rule_ref, 0, place * LONG, terms)
                middle[s * 4 * NW + 4 * out_ref[place] + t2] = total

        loop(0, 4, left, 1)

    loop(0, 4, left_half, 1)
    for copy in rights_copies:
        copy.wait()

    rows = lax.broadcasted_iota(jnp.int32, (TILE, TILE), 0)
    columns = lax.broadcasted_iota(jnp.int32, (TILE, TILE), 1)
    own = live_ref[MAXLEN * NSEC + sector]

    def right_half(n):
        p = p_ref[n]
        s1 = p // 4
        s2 = p % 4
        ups = s1 % 2 + s2 % 2
        downs = s1 // 2 + s2 // 2
        far = sector + ND * ups + downs
        for i in range(NW):
            place = s2 * NW + i
            x = out_ref[place]
            keep = inside(far + class_shift(class_ref[x]))
            high, low = split(rights[3 * ups + downs, x] * keep)
            lhs[:TILE, i * TILE : (i + 1) * TILE] = high
            lhs[TILE:, i * TILE : (i + 1) * TILE] = low
            terms = LONG if i < LONG else SHORT
            total = mix(middle, s1 * 4 * NW, block_ref, place_ref, rule_ref, 1, place * LONG, terms)
            high, low = split(total)
            outer[i * TILE : (i + 1) * TILE, :TILE] = high
            outer[i * TILE : (i + 1) * TILE, TILE:] = low
        total = dot(lhs[...], outer[...])
        total = folded(total[:TILE] + total[TILE:]).T
        count = jnp.where(far < NSEC, live_ref[MAXLEN * NSEC + jnp.minimum(far, NSEC - 1)], 0)
        image_ref[p] = jnp.where((rows < own) & (columns < count), total, 0.0)

    loop(0, 16, right_half, 1)


def pair(scalars, start, passed, kets, rights):
    order = jnp.arange(16, dtype=jnp.int32)
    return pl.pallas_call(
        pair_kernel,
        out_shape=jax.ShapeDtypeStruct((16, TILE, TILE), F32),
        in_specs=[SMEM_SPEC] * 9 + [VMEM_SPEC] * 3 + [HBM_SPEC] * 10,
        out_specs=VMEM_SPEC,
        scratch_shapes=[
            pltpu.VMEM((4, 5, 4 * TILE, 2 * TILE), BF16),
            pltpu.VMEM((9, NW, TILE, TILE), F32),
            pltpu.VMEM((NW, 2 * TILE, 2 * TILE), BF16),
            pltpu.VMEM((4 * NW, TILE, TILE), F32),
            pltpu.VMEM((16 * NW, TILE, TILE), F32),
            pltpu.VMEM((2 * TILE, NW * TILE), BF16),
            pltpu.VMEM((NW * TILE, 2 * TILE), BF16),
            pltpu.SemaphoreType.DMA((13,)),
        ],
        compiler_params=pltpu.CompilerParams(vmem_limit_bytes=60 * 2**20),
        cost_estimate=pl.CostEstimate(flops=20 * 10**9, bytes_accessed=18 * 10**6, transcendentals=0),
        name="pair",
    )(*scalars, order, start, *passed, kets, *rights)


def turn_kernel(e0, e1, out_ref):
    for first, ref in ((0, e0), (9, e1)):
        for n in range(ref.shape[0]):
            out_ref[first + n] = ref[n].T


def turned(parts):
    return pl.pallas_call(
        turn_kernel,
        out_shape=jax.ShapeDtypeStruct((NW, TILE, TILE), F32),
        in_specs=[VMEM_SPEC] * 2,
        out_specs=VMEM_SPEC,
        cost_estimate=pl.CostEstimate(flops=10**6, bytes_accessed=2228224, transcendentals=0),
        name="turn",
    )(*parts)


def fetch(blocks, offset, axis="block"):
    length = lax.axis_size(axis)
    pairs = [(i, i - offset) for i in range(length) if 0 <= i - offset < length]
    return lax.ppermute(blocks, axis, pairs)


def flat_rules(rules):
    return jnp.pad(rules.reshape(2, RULE), ((0, 0), (0, PADDED - RULE))).reshape(-1)


def shards(
    env_left,
    env_right,
    site_tensors,
    pair_state,
    mpo_sites,
    mpo_pair,
    channel_class,
    live_rows,
    region_sites,
):
    start = env_left[0, :, 0]
    right = env_right[0, :, 0]
    tensors = site_tensors[0, :, :, 0]
    pairs = pair_state[0, :, 0]
    sector = lax.axis_index("block").astype(jnp.int32).reshape(1)
    region = lax.axis_index("region").astype(jnp.int32).reshape(1)
    live = live_rows.reshape(-1)

    near3 = fetch(tensors, ND)
    near4 = fetch(tensors, -ND)
    near1 = fetch(tensors, 1)
    near2 = fetch(tensors, -1)
    near = [tensors, near1, near2, near3, near4]
    rights = {(0, 0): right}
    rights[1, 0] = fetch(right, ND)
    rights[0, 1] = fetch(right, 1)
    rights[0, 2] = fetch(rights[0, 1], 1)
    rights[2, 0] = fetch(rights[1, 0], ND)
    for up in (1, 2):
        for down in (1, 2):
            rights[up, down] = fetch(rights[up, down - 1], 1)
    kets = [pairs] + [fetch(pairs, CLASS_STEPS[n]) for n in range(1, 5)]

    tables = mix_tables(channel_class)
    scalars = (sector, channel_class, live, *tables)
    site_rules = flat_rules(mpo_sites)
    h0, h1, h2, h3 = site(0, (*scalars, site_rules), [start], near)
    below3 = fetch(h3, -1)
    below2 = fetch(h2, -1)
    partial = fetch(h1 + below3, -ND)

    h0, h1, h2, h3, first = site(1, (*scalars, site_rules), [h0, below2, partial], near)
    below3 = fetch(h3, -1)
    below2 = fetch(h2, -1)
    upper = h1 + below3
    ket = sector + class_shift(channel_class)
    sectors = jnp.arange(NSEC, dtype=jnp.int32)
    width = jnp.arange(TILE, dtype=jnp.int32)
    count = jnp.where(ket[:, None] == sectors, live_rows[0, 1], 0).sum(-1)
    own = jnp.where(sector == sectors, live_rows[0, 1], 0).sum()
    keep = (width[:, None] < count[:, None, None]) & (width < own)
    parts = []
    passed = []
    for lo, hi in ((0, 9), (9, NW)):
        partial = fetch(upper[lo:hi], -ND)
        second = jnp.where(keep[lo:hi], h0[lo:hi] + below2[lo:hi] + partial, 0.0)
        second = jnp.where(region_sites[0] > 1, second, first[lo:hi])
        parts.append(second)
        passed.append(fetch(second, -1, "region"))

    environment = turned(parts)
    split = split_kets(sector, kets)
    scalars = (sector, region, channel_class, live, *tables, flat_rules(mpo_pair))
    images = pair(scalars, start, passed, split, [rights[u, d] for u in range(3) for d in range(3)])
    return environment[None, :, None], images[None, :, None]


def solution(mesh):
    in_specs = (
        P("region", None, "block", None, None),
        P("region", None, "block", None, None),
        P("region", None, None, "block", None, None),
        P("region", None, "block", None, None),
        P("region", None, None, None, None, None),
        P("region", None, None, None, None, None),
        P(),
        P("region", None, None),
        P("region"),
    )
    out_specs = (P("region", None, "block", None, None), P("region", None, "block", None, None))
    return jax.shard_map(shards, mesh=mesh, in_specs=in_specs, out_specs=out_specs, check_vma=False)
```

profile of v0, /device:TPU:32, one launch (start us, length us, event | category | flops | bytes accessed | tf_op | source)
XLA Modules:
  0.0 284.8 jit_solution(10939738198561220307)
XLA Ops:
  0.6 4.0 %collective-permute-start = (f32[2,4,128,128]{3,2,1,0:T(8,128)}, f32[2,4,128,128]{3,2,1,0:T(8,128)S(1)}, u32[]{:S(2)}, u32[]{:S(2)}) collective-permute-start(f32[2,4,128,128]{3,2,1,0:T(8,128)} %bitcast.27), channel_id=1, source_target_pairs={{1,0},{2,1},{3,2},{4,3},{5,4},{6,5},{7,6},{8,7},{9,8},{10,9},{11,1... | collective-permute-start | bytes 1572872 | tf_op jit(solution)/shard_map/ppermute | solution.py:331
  4.7 1.9 collective-permute-start.1
  6.6 1.9 collective-permute-start.2
  8.5 3.9 %collective-permute-start.3 = (f32[2,4,128,128]{3,2,1,0:T(8,128)}, f32[2,4,128,128]{3,2,1,0:T(8,128)}, u32[]{:S(2)}, u32[]{:S(2)}) collective-permute-start(f32[2,4,128,128]{3,2,1,0:T(8,128)} %bitcast.30), channel_id=1, source_target_pairs={{0,8},{1,9},{2,10},{3,11},{4,12},{5,13},{6,14},{7,15},{8,16},{9,17... | collective-permute-start | bytes 1572872 | tf_op jit(solution)/shard_map/ppermute | solution.py:331
  15.2 0.7 broadcast_add_fusion
  16.1 0.7 broadcast_add_fusion.1
  18.2 3.2 %select_reduce_fusion = s32[4,17,11]{0,2,1:T(8,128)S(1)} fusion(s32[4,17,68]{2,0,1:T(4,128)S(1)} %copy.35, pred[4,17,68]{2,0,1:T(4,128)(4,1)S(1)} %copy.34), kind=kLoop, calls=%fused_computation.10 | loop fusion | flops 202708 | bytes 26112 | tf_op jit(solution)/shard_map/reduce_sum | solution.py:51
  22.6 1.9 copy.38
  24.6 2.1 reshape.416
  26.8 2.0 collective-permute-done.3.refs_5_.refs_7_
  28.9 10.8 %shard_map.113 = (f32[17,128,128]{2,1,0:T(8,128)S(1)}, f32[17,128,128]{2,1,0:T(8,128)S(1)}, f32[17,128,128]{2,1,0:T(8,128)S(1)}, f32[17,128,128]{2,1,0:T(8,128)S(1)}) custom-call(s32[1]{0:T(128)} %bitcast.2.sector_ref, s32[17]{0:T(128)S(1)} %copy-done.2, s32[96]{0:T(128)S(1)} %reshape.413.live_ref, s32[68]{0:T(128)S(1)} %reshape.414.out_ref, ...), custom_call_target="tpu_custom_call" | custom-call | flops 4000000000 | bytes 10000000 | tf_op jit(solution)/shard_map/pallas_call | solution.py:163
  39.7 1.9 collective-permute-start.5
  41.6 1.9 collective-permute-start.19
  43.6 1.9 collective-permute-start.4
  45.5 13.1 %collective-permute-done.5 = f32[17,128,128]{2,1,0:T(8,128)S(1)} collective-permute-done((f32[17,128,128]{2,1,0:T(8,128)S(1)}, f32[17,128,128]{2,1,0:T(8,128)S(1)}, u32[]{:S(2)}, u32[]{:S(2)}) %collective-permute-start.5) | collective-permute-done | bytes 1114144 | tf_op jit(solution)/shard_map/ppermute | solution.py:331
  58.8 4.0 %collective-permute-start.6 = (f32[17,128,128]{2,1,0:T(8,128)S(1)}, f32[17,128,128]{2,1,0:T(8,128)S(1)}, u32[]{:S(2)}, u32[]{:S(2)}) collective-permute-start(f32[17,128,128]{2,1,0:T(8,128)S(1)} %add.155), channel_id=1, source_target_pairs={{0,8},{1,9},{2,10},{3,11},{4,12},{5,13},{6,14},{7,15},{8,16},{9,17... | collective-permute-start | bytes 3342344 | tf_op jit(solution)/shard_map/ppermute | solution.py:331
  62.7 1.9 collective-permute-start.13
  64.7 2.4 collective-permute-start.14
  67.1 3.1 %collective-permute-done.19.refs_3_ = f32[17,128,128]{2,1,0:T(8,128)S(1)} collective-permute-done((f32[17,128,128]{2,1,0:T(8,128)S(1)}, f32[17,128,128]{2,1,0:T(8,128)S(1)}, u32[]{:S(2)}, u32[]{:S(2)}) %collective-permute-start.19) | collective-permute-done | bytes 1114144 | tf_op jit(solution)/shard_map/ppermute | solution.py:331
  70.2 2.2 collective-permute-start.22
  72.4 33.3 %collective-permute-done.6.refs_2_ = f32[17,128,128]{2,1,0:T(8,128)S(1)} collective-permute-done((f32[17,128,128]{2,1,0:T(8,128)S(1)}, f32[17,128,128]{2,1,0:T(8,128)S(1)}, u32[]{:S(2)}, u32[]{:S(2)}) %collective-permute-start.6) | collective-permute-done | bytes 1114144 | tf_op jit(solution)/shard_map/ppermute | solution.py:331
  105.7 9.5 %shard_map.114 = (f32[17,128,128]{2,1,0:T(8,128)S(1)}, f32[17,128,128]{2,1,0:T(8,128)S(1)}, f32[17,128,128]{2,1,0:T(8,128)S(1)}, f32[17,128,128]{2,1,0:T(8,128)S(1)}, f32[17,128,128]{2,1,0:T(8,128)S(1)}) custom-call(s32[1]{0:T(128)} %bitcast.2.sector_ref, s32[17]{0:T(128)S(1)} %copy-done.2, s32[96]{0:T(128)S(1)} %reshape.413.live_ref, ...), custom_call_target="tpu_custom_call" | custom-call | flops 4000000000 | bytes 10000000 | tf_op jit(solution)/shard_map/pallas_call | solution.py:163
  115.2 2.0 collective-permute-start.8
  117.2 1.9 collective-permute-start.15
  119.1 5.1 %collective-permute-start.17 = (f32[17,128,128]{2,1,0:T(8,128)S(1)}, f32[17,128,128]{2,1,0:T(8,128)}, u32[]{:S(2)}, u32[]{:S(2)}) collective-permute-start(f32[17,128,128]{2,1,0:T(8,128)S(1)} %bitcast.45), channel_id=1, source_target_pairs={{1,0},{2,1},{3,2},{4,3},{5,4},{6,5},{7,6},{8,7},{9,8},{10,9},{11,1... | collective-permute-start | bytes 3342344 | tf_op jit(solution)/shard_map/ppermute | solution.py:331
  124.2 1.9 collective-permute-start.20
  126.2 1.9 collective-permute-start.23
  128.1 6.0 %collective-permute-done.8 = f32[17,128,128]{2,1,0:T(8,128)S(1)} collective-permute-done((f32[17,128,128]{2,1,0:T(8,128)S(1)}, f32[17,128,128]{2,1,0:T(8,128)S(1)}, u32[]{:S(2)}, u32[]{:S(2)}) %collective-permute-start.8) | collective-permute-done | bytes 1114144 | tf_op jit(solution)/shard_map/ppermute | solution.py:331
  134.1 1.9 collective-permute-start.7
  136.9 7.4 %collective-permute-done.15 = f32[16,128,128]{2,1,0:T(8,128)S(1)} collective-permute-done((f32[16,128,128]{2,1,0:T(8,128)S(1)}, f32[16,128,128]{2,1,0:T(8,128)S(1)}, u32[]{:S(2)}, u32[]{:S(2)}) %collective-permute-start.15) | collective-permute-done | bytes 1048608 | tf_op jit(solution)/shard_map/ppermute | solution.py:331
  144.3 3.6 %collective-permute-start.9 = (f32[9,128,128]{2,1,0:T(8,128)S(1)}, f32[9,128,128]{2,1,0:T(8,128)S(1)}, u32[]{:S(2)}, u32[]{:S(2)}) collective-permute-start(f32[9,128,128]{2,1,0:T(8,128)S(1)} %slice.47), channel_id=1, source_target_pairs={{0,8},{1,9},{2,10},{3,11},{4,12},{5,13},{6,14},{7,15},{8,16},{9,17... | collective-permute-start | bytes 1769480 | tf_op jit(solution)/shard_map/ppermute | solution.py:331
  149.5 1.9 collective-permute-start.16
  151.5 2.1 collective-permute-start.10
  154.1 7.0 %collective-permute-done.23.refs_7_ = f32[17,128,128]{2,1,0:T(8,128)} collective-permute-done((f32[17,128,128]{2,1,0:T(8,128)S(1)}, f32[17,128,128]{2,1,0:T(8,128)}, u32[]{:S(2)}, u32[]{:S(2)}) %collective-permute-start.23) | collective-permute-done | bytes 1114144 | tf_op jit(solution)/shard_map/ppermute | solution.py:331
  161.1 24.3 %collective-permute-start.18 = (f32[17,128,128]{2,1,0:T(8,128)}, f32[17,128,128]{2,1,0:T(8,128)}, u32[]{:S(2)}, u32[]{:S(2)}) collective-permute-start(f32[17,128,128]{2,1,0:T(8,128)} %collective-permute-done.17.refs_1_), channel_id=1, source_target_pairs={{1,0},{2,1},{3,2},{4,3},{5,4},{6,5},{7,6},{8,7},{9,8},{10,9},{11,1... | collective-permute-start | bytes 3342344 | tf_op jit(solution)/shard_map/ppermute | solution.py:331
  185.4 1.9 collective-permute-start.21
  187.4 1.9 collective-permute-start.24
  189.5 9.9 %collective-permute-done.10 = f32[8,128,128]{2,1,0:T(8,128)S(1)} collective-permute-done((f32[8,128,128]{2,1,0:T(8,128)S(1)}, f32[8,128,128]{2,1,0:T(8,128)S(1)}, u32[]{:S(2)}, u32[]{:S(2)}) %collective-permute-start.10) | collective-permute-done | bytes 524320 | tf_op jit(solution)/shard_map/ppermute | solution.py:331
  199.4 3.4 %collective-permute-start.11 = (f32[9,128,128]{2,1,0:T(8,128)S(1)}, f32[9,128,128]{2,1,0:T(8,128)S(1)}, u32[]{:S(2)}, u32[]{:S(2)}) collective-permute-start(f32[9,128,128]{2,1,0:T(8,128)S(1)} %fusion.2.e0), channel_id=1, source_target_pairs={{0,32},{32,64},{64,96},{1,33},{33,65},{65,97},{2,34},{34,66},{66,9... | collective-permute-start | bytes 1769480 | tf_op jit(solution)/shard_map/ppermute | solution.py:331
  203.0 1.0 copy-done.13
  204.1 4.1 %collective-permute-start.12 = (f32[8,128,128]{2,1,0:T(8,128)S(1)}, f32[8,128,128]{2,1,0:T(8,128)}, u32[]{:S(2)}, u32[]{:S(2)}) collective-permute-start(f32[8,128,128]{2,1,0:T(8,128)S(1)} %fusion.5.e1), channel_id=1, source_target_pairs={{0,32},{32,64},{64,96},{1,33},{33,65},{65,97},{2,34},{34,66},{66,9... | collective-permute-start | bytes 1572872 | tf_op jit(solution)/shard_map/ppermute | solution.py:331
  208.2 0.9 copy.39
  209.1 0.8 reshape.419
  210.7 5.9 %split_kets.1.kets_hbm = bf16[4,5,512,256]{3,2,1,0:T(8,128)(2,1)} custom-call(s32[1]{0:T(128)} %bitcast.2.sector_ref, f32[4,4,128,128]{3,2,1,0:T(8,128)} %bitcast.34, f32[4,4,128,128]{3,2,1,0:T(8,128)} %bitcast.39, f32[4,4,128,128]{3,2,1,0:T(8,128)} %bitcast.40, f32[4,4,128,128]{3,2,1,0:T(8,128)} %bitcast.41, f32[4,4,128,128]{3,2,1,0:T(8,128)} %bitcast.42), custom_call_target="tpu_custom_call" | custom-call | flops 5000000 | bytes 10000000 | tf_op jit(solution)/shard_map/split_kets/pallas_call | solution.py:192
  216.6 2.6 turn.1
  219.2 3.4 %collective-permute-done.24.refs_8_ = f32[17,128,128]{2,1,0:T(8,128)} collective-permute-done((f32[17,128,128]{2,1,0:T(8,128)}, f32[17,128,128]{2,1,0:T(8,128)}, u32[]{:S(2)}, u32[]{:S(2)}) %collective-permute-start.24) | collective-permute-done | bytes 1114144 | tf_op jit(solution)/shard_map/ppermute | solution.py:331
  222.6 4.2 %collective-permute-done.12.passed1_ref = f32[8,128,128]{2,1,0:T(8,128)} collective-permute-done((f32[8,128,128]{2,1,0:T(8,128)S(1)}, f32[8,128,128]{2,1,0:T(8,128)}, u32[]{:S(2)}, u32[]{:S(2)}) %collective-permute-start.12) | collective-permute-done | bytes 524320 | tf_op jit(solution)/shard_map/ppermute | solution.py:331
  227.6 57.1 %pair.1 = f32[16,128,128]{2,1,0:T(8,128)} custom-call(s32[1]{0:T(128)} %bitcast.2.sector_ref, s32[1]{0:T(128)} %bitcast.8.region_ref, s32[17]{0:T(128)} %class_ref.5, s32[96]{0:T(128)} %copy-done.3, s32[68]{0:T(128)} %copy-done.4, s32[748]{0:T(1024)} %copy-done, s32[748]{0:T(1024)} %copy-done.1, f32[9792]{0:T(1024)} %reshape.420.rule_ref, s32[16]{0:T(128)} %iota.79.p_ref, ...), custom_call_target="tpu_custom_call" | custom-call | flops 20000000000 | bytes 18000000 | tf_op jit(solution)/shard_map/pair/pallas_call | solution.py:290
  (102 shorter events, 9.9 us)
Async XLA Ops:
  0.6 22.0 %copy-start.14 = (f32[1,2,17,17,4,4]{3,5,4,2,1,0:T(4,128)S(1)}, f32[1,2,17,17,4,4]{3,5,4,2,1,0:T(4,128)}, u32[]{:S(2)}) copy-start(f32[1,2,17,17,4,4]{3,5,4,2,1,0:T(4,128)} %param.14) | copy-start | bytes 110980
  0.6 26.2 %collective-permute-start = (f32[2,4,128,128]{3,2,1,0:T(8,128)}, f32[2,4,128,128]{3,2,1,0:T(8,128)S(1)}, u32[]{:S(2)}, u32[]{:S(2)}) collective-permute-start(f32[2,4,128,128]{3,2,1,0:T(8,128)} %bitcast.27), channel_id=1, source_target_pairs={{1,0},{2,1},{3,2},{4,3},{5,4},{6,5},{7,6},{8,7},{9,8},{10,9},{11,1... | collective-permute-start | bytes 1572872 | tf_op jit(solution)/shard_map/ppermute | solution.py:331
  4.7 22.1 %collective-permute-start.1 = (f32[2,4,128,128]{3,2,1,0:T(8,128)}, f32[2,4,128,128]{3,2,1,0:T(8,128)S(1)}, u32[]{:S(2)}, u32[]{:S(2)}) collective-permute-start(f32[2,4,128,128]{3,2,1,0:T(8,128)} %bitcast.28), channel_id=1, source_target_pairs={{0,1},{1,2},{2,3},{3,4},{4,5},{5,6},{6,7},{7,8},{8,9},{9,10},{10,1... | collective-permute-start | bytes 1572872 | tf_op jit(solution)/shard_map/ppermute | solution.py:331
  6.6 20.2 %collective-permute-start.2 = (f32[2,4,128,128]{3,2,1,0:T(8,128)}, f32[2,4,128,128]{3,2,1,0:T(8,128)S(1)}, u32[]{:S(2)}, u32[]{:S(2)}) collective-permute-start(f32[2,4,128,128]{3,2,1,0:T(8,128)} %bitcast.29), channel_id=1, source_target_pairs={{8,0},{9,1},{10,2},{11,3},{12,4},{13,5},{14,6},{15,7},{16,8},{17,9... | collective-permute-start | bytes 1572872 | tf_op jit(solution)/shard_map/ppermute | solution.py:331
  8.5 20.3 %collective-permute-start.3 = (f32[2,4,128,128]{3,2,1,0:T(8,128)}, f32[2,4,128,128]{3,2,1,0:T(8,128)}, u32[]{:S(2)}, u32[]{:S(2)}) collective-permute-start(f32[2,4,128,128]{3,2,1,0:T(8,128)} %bitcast.30), channel_id=1, source_target_pairs={{0,8},{1,9},{2,10},{3,11},{4,12},{5,13},{6,14},{7,15},{8,16},{9,17... | collective-permute-start | bytes 1572872 | tf_op jit(solution)/shard_map/ppermute | solution.py:331
  17.9 87.7 %copy-start.3 = (s32[96]{0:T(128)}, s32[96]{0:T(128)S(1)}, u32[]{:S(2)}) copy-start(s32[96]{0:T(128)S(1)} %reshape.413.live_ref) | copy-start | bytes 1156
  18.1 87.5 %copy-start.4 = (s32[68]{0:T(128)}, s32[68]{0:T(128)S(1)}, u32[]{:S(2)}) copy-start(s32[68]{0:T(128)S(1)} %reshape.414.out_ref) | copy-start | bytes 820
  21.8 83.9 %copy-start = (s32[748]{0:T(1024)}, s32[748]{0:T(1024)S(1)}, u32[]{:S(2)}) copy-start(s32[748]{0:T(1024)S(1)} %reshape.415.block_ref) | copy-start | bytes 8980
  22.6 6.3 %copy-start.2 = (s32[17]{0:T(128)S(1)}, s32[17]{0:T(128)}, u32[]{:S(2)}) copy-start(s32[17]{0:T(128)} %class_ref.5) | copy-start | bytes 208
  22.6 6.3 %copy-start.5 = (f32[1,17,1,128,128]{4,3,2,1,0:T(8,128)S(1)}, f32[1,17,1,128,128]{4,3,2,1,0:T(8,128)}, u32[]{:S(2)}) copy-start(f32[1,17,1,128,128]{4,3,2,1,0:T(8,128)} %param.10) | copy-start | bytes 3342340
  22.6 6.2 %copy-start.6 = (f32[1,2,4,1,128,128]{5,4,3,2,1,0:T(8,128)S(1)}, f32[1,2,4,1,128,128]{5,4,3,2,1,0:T(8,128)}, u32[]{:S(2)}) copy-start(f32[1,2,4,1,128,128]{5,4,3,2,1,0:T(8,128)} %param.12) | copy-start | bytes 1572868
  26.8 78.9 %copy-start.1 = (s32[748]{0:T(1024)}, s32[748]{0:T(1024)S(1)}, u32[]{:S(2)}) copy-start(s32[748]{0:T(1024)S(1)} %fusion.15.place_ref) | copy-start | bytes 8980
  28.9 12.8 %copy-start.17 = (f32[1,17,1,128,128]{4,3,2,1,0:T(8,128)S(1)}, f32[1,17,1,128,128]{4,3,2,1,0:T(8,128)}, u32[]{:S(2)}) copy-start(f32[1,17,1,128,128]{4,3,2,1,0:T(8,128)} %param.11) | copy-start | bytes 3342340
  39.7 18.9 %collective-permute-start.5 = (f32[17,128,128]{2,1,0:T(8,128)S(1)}, f32[17,128,128]{2,1,0:T(8,128)S(1)}, u32[]{:S(2)}, u32[]{:S(2)}) collective-permute-start(f32[17,128,128]{2,1,0:T(8,128)S(1)} %get-tuple-element.14), channel_id=1, source_target_pairs={{0,1},{1,2},{2,3},{3,4},{4,5},{5,6},{6,7},{7,8},{8,9},{9,10},{10,1... | collective-permute-start | bytes 3342344 | tf_op jit(solution)/shard_map/ppermute | solution.py:331
  41.6 28.5 %collective-permute-start.19 = (f32[17,128,128]{2,1,0:T(8,128)S(1)}, f32[17,128,128]{2,1,0:T(8,128)S(1)}, u32[]{:S(2)}, u32[]{:S(2)}) collective-permute-start(f32[17,128,128]{2,1,0:T(8,128)S(1)} %bitcast.44), channel_id=1, source_target_pairs={{8,0},{9,1},{10,2},{11,3},{12,4},{13,5},{14,6},{15,7},{16,8},{17,9... | collective-permute-start | bytes 3342344 | tf_op jit(solution)/shard_map/ppermute | solution.py:331
  43.6 28.8 %collective-permute-start.4 = (f32[17,128,128]{2,1,0:T(8,128)S(1)}, f32[17,128,128]{2,1,0:T(8,128)S(1)}, u32[]{:S(2)}, u32[]{:S(2)}) collective-permute-start(f32[17,128,128]{2,1,0:T(8,128)S(1)} %get-tuple-element.12), channel_id=1, source_target_pairs={{0,1},{1,2},{2,3},{3,4},{4,5},{5,6},{6,7},{7,8},{8,9},{9,10},{10,1... | collective-permute-start | bytes 3342344 | tf_op jit(solution)/shard_map/ppermute | solution.py:331
  58.6 4.1 %copy-start.9 = (f32[1,16,1,128,128]{4,3,2,1,0:T(8,128)S(1)}, f32[1,16,1,128,128]{4,3,2,1,0:T(8,128)}, u32[]{:S(2)}) copy-start(f32[1,16,1,128,128]{4,3,2,1,0:T(8,128)} %param.13) | copy-start | bytes 3145732
  58.8 46.9 %collective-permute-start.6 = (f32[17,128,128]{2,1,0:T(8,128)S(1)}, f32[17,128,128]{2,1,0:T(8,128)S(1)}, u32[]{:S(2)}, u32[]{:S(2)}) collective-permute-start(f32[17,128,128]{2,1,0:T(8,128)S(1)} %add.155), channel_id=1, source_target_pairs={{0,8},{1,9},{2,10},{3,11},{4,12},{5,13},{6,14},{7,15},{8,16},{9,17... | collective-permute-start | bytes 3342344 | tf_op jit(solution)/shard_map/ppermute | solution.py:331
  62.7 56.3 %collective-permute-start.13 = (f32[16,128,128]{2,1,0:T(8,128)S(1)}, f32[16,128,128]{2,1,0:T(8,128)S(1)}, u32[]{:S(2)}, u32[]{:S(2)}) collective-permute-start(f32[16,128,128]{2,1,0:T(8,128)S(1)} %bitcast.35), channel_id=1, source_target_pairs={{1,0},{2,1},{3,2},{4,3},{5,4},{6,5},{7,6},{8,7},{9,8},{10,9},{11,1... | collective-permute-start | bytes 3145736 | tf_op jit(solution)/shard_map/ppermute | solution.py:331
  64.7 59.5 %collective-permute-start.14 = (f32[16,128,128]{2,1,0:T(8,128)S(1)}, f32[16,128,128]{2,1,0:T(8,128)S(1)}, u32[]{:S(2)}, u32[]{:S(2)}) collective-permute-start(f32[16,128,128]{2,1,0:T(8,128)S(1)} %bitcast.36), channel_id=1, source_target_pairs={{0,1},{1,2},{2,3},{3,4},{4,5},{5,6},{6,7},{7,8},{8,9},{9,10},{10,1... | collective-permute-start | bytes 3145736 | tf_op jit(solution)/shard_map/ppermute | solution.py:331
  70.2 54.0 %copy-start.18 = (f32[17,128,128]{2,1,0:T(8,128)}, f32[17,128,128]{2,1,0:T(8,128)S(1)}, u32[]{:S(2)}) copy-start(f32[17,128,128]{2,1,0:T(8,128)S(1)} %collective-permute-done.19.refs_3_) | copy-start | bytes 3342340
  70.2 56.0 %collective-permute-start.22 = (f32[17,128,128]{2,1,0:T(8,128)S(1)}, f32[17,128,128]{2,1,0:T(8,128)S(1)}, u32[]{:S(2)}, u32[]{:S(2)}) collective-permute-start(f32[17,128,128]{2,1,0:T(8,128)S(1)} %collective-permute-done.19.refs_3_), channel_id=1, source_target_pairs={{8,0},{9,1},{10,2},{11,3},{12,4},{13,5},{14,6},{15,7},{16,8},{17,9... | collective-permute-start | bytes 3342344 | tf_op jit(solution)/shard_map/ppermute | solution.py:331
  105.7 30.3 %copy-start.16 = (s32[1,3,32]{2,0,1:T(1,128)S(1)}, s32[1,3,32]{2,0,1:T(1,128)}, u32[]{:S(2)}) copy-start(s32[1,3,32]{2,0,1:T(1,128)} %param.17) | copy-start | bytes 1156
  115.2 18.9 %collective-permute-start.8 = (f32[17,128,128]{2,1,0:T(8,128)S(1)}, f32[17,128,128]{2,1,0:T(8,128)S(1)}, u32[]{:S(2)}, u32[]{:S(2)}) collective-permute-start(f32[17,128,128]{2,1,0:T(8,128)S(1)} %get-tuple-element.18), channel_id=1, source_target_pairs={{0,1},{1,2},{2,3},{3,4},{4,5},{5,6},{6,7},{7,8},{8,9},{9,10},{10,1... | collective-permute-start | bytes 3342344 | tf_op jit(solution)/shard_map/ppermute | solution.py:331
  117.2 27.2 %collective-permute-start.15 = (f32[16,128,128]{2,1,0:T(8,128)S(1)}, f32[16,128,128]{2,1,0:T(8,128)S(1)}, u32[]{:S(2)}, u32[]{:S(2)}) collective-permute-start(f32[16,128,128]{2,1,0:T(8,128)S(1)} %bitcast.37), channel_id=1, source_target_pairs={{8,0},{9,1},{10,2},{11,3},{12,4},{13,5},{14,6},{15,7},{16,8},{17,9... | collective-permute-start | bytes 3145736 | tf_op jit(solution)/shard_map/ppermute | solution.py:331
  119.1 17.8 %copy-start.10 = (f32[16,128,128]{2,1,0:T(8,128)}, f32[16,128,128]{2,1,0:T(8,128)S(1)}, u32[]{:S(2)}) copy-start(f32[16,128,128]{2,1,0:T(8,128)S(1)} %collective-permute-done.13) | copy-start | bytes 3145732
  119.1 30.4 %collective-permute-start.17 = (f32[17,128,128]{2,1,0:T(8,128)S(1)}, f32[17,128,128]{2,1,0:T(8,128)}, u32[]{:S(2)}, u32[]{:S(2)}) collective-permute-start(f32[17,128,128]{2,1,0:T(8,128)S(1)} %bitcast.45), channel_id=1, source_target_pairs={{1,0},{2,1},{3,2},{4,3},{5,4},{6,5},{7,6},{8,7},{9,8},{10,9},{11,1... | collective-permute-start | bytes 3342344 | tf_op jit(solution)/shard_map/ppermute | solution.py:331
  124.2 12.7 %copy-start.11 = (f32[16,128,128]{2,1,0:T(8,128)}, f32[16,128,128]{2,1,0:T(8,128)S(1)}, u32[]{:S(2)}) copy-start(f32[16,128,128]{2,1,0:T(8,128)S(1)} %collective-permute-done.14) | copy-start | bytes 3145732
  124.2 27.3 %collective-permute-start.20 = (f32[17,128,128]{2,1,0:T(8,128)S(1)}, f32[17,128,128]{2,1,0:T(8,128)}, u32[]{:S(2)}, u32[]{:S(2)}) collective-permute-start(f32[17,128,128]{2,1,0:T(8,128)S(1)} %collective-permute-done.19.refs_3_), channel_id=1, source_target_pairs={{1,0},{2,1},{3,2},{4,3},{5,4},{6,5},{7,6},{8,7},{9,8},{10,9},{11,1... | collective-permute-start | bytes 3342344 | tf_op jit(solution)/shard_map/ppermute | solution.py:331
  126.2 10.7 %copy-start.19 = (f32[17,128,128]{2,1,0:T(8,128)}, f32[17,128,128]{2,1,0:T(8,128)S(1)}, u32[]{:S(2)}) copy-start(f32[17,128,128]{2,1,0:T(8,128)S(1)} %collective-permute-done.22.refs_6_) | copy-start | bytes 3342340
  126.2 34.9 %collective-permute-start.23 = (f32[17,128,128]{2,1,0:T(8,128)S(1)}, f32[17,128,128]{2,1,0:T(8,128)}, u32[]{:S(2)}, u32[]{:S(2)}) collective-permute-start(f32[17,128,128]{2,1,0:T(8,128)S(1)} %collective-permute-done.22.refs_6_), channel_id=1, source_target_pairs={{1,0},{2,1},{3,2},{4,3},{5,4},{6,5},{7,6},{8,7},{9,8},{10,9},{11,1... | collective-permute-start | bytes 3342344 | tf_op jit(solution)/shard_map/ppermute | solution.py:331
  134.1 51.3 %collective-permute-start.7 = (f32[17,128,128]{2,1,0:T(8,128)S(1)}, f32[17,128,128]{2,1,0:T(8,128)S(1)}, u32[]{:S(2)}, u32[]{:S(2)}) collective-permute-start(f32[17,128,128]{2,1,0:T(8,128)S(1)} %get-tuple-element.16), channel_id=1, source_target_pairs={{0,1},{1,2},{2,3},{3,4},{4,5},{5,6},{6,7},{7,8},{8,9},{9,10},{10,1... | collective-permute-start | bytes 3342344 | tf_op jit(solution)/shard_map/ppermute | solution.py:331
  144.3 45.2 %copy-start.12 = (f32[16,128,128]{2,1,0:T(8,128)}, f32[16,128,128]{2,1,0:T(8,128)S(1)}, u32[]{:S(2)}) copy-start(f32[16,128,128]{2,1,0:T(8,128)S(1)} %collective-permute-done.15) | copy-start | bytes 3145732
  144.3 43.0 %collective-permute-start.9 = (f32[9,128,128]{2,1,0:T(8,128)S(1)}, f32[9,128,128]{2,1,0:T(8,128)S(1)}, u32[]{:S(2)}, u32[]{:S(2)}) collective-permute-start(f32[9,128,128]{2,1,0:T(8,128)S(1)} %slice.47), channel_id=1, source_target_pairs={{0,8},{1,9},{2,10},{3,11},{4,12},{5,13},{6,14},{7,15},{8,16},{9,17... | collective-permute-start | bytes 1769480 | tf_op jit(solution)/shard_map/ppermute | solution.py:331
  149.5 53.5 %collective-permute-start.16 = (f32[16,128,128]{2,1,0:T(8,128)S(1)}, f32[16,128,128]{2,1,0:T(8,128)S(1)}, u32[]{:S(2)}, u32[]{:S(2)}) collective-permute-start(f32[16,128,128]{2,1,0:T(8,128)S(1)} %bitcast.38), channel_id=1, source_target_pairs={{0,8},{1,9},{2,10},{3,11},{4,12},{5,13},{6,14},{7,15},{8,16},{9,17... | collective-permute-start | bytes 3145736 | tf_op jit(solution)/shard_map/ppermute | solution.py:331
  151.5 47.9 %collective-permute-start.10 = (f32[8,128,128]{2,1,0:T(8,128)S(1)}, f32[8,128,128]{2,1,0:T(8,128)S(1)}, u32[]{:S(2)}, u32[]{:S(2)}) collective-permute-start(f32[8,128,128]{2,1,0:T(8,128)S(1)} %slice.50), channel_id=1, source_target_pairs={{0,8},{1,9},{2,10},{3,11},{4,12},{5,13},{6,14},{7,15},{8,16},{9,17... | collective-permute-start | bytes 1572872 | tf_op jit(solution)/shard_map/ppermute | solution.py:331
  161.1 58.0 %collective-permute-start.18 = (f32[17,128,128]{2,1,0:T(8,128)}, f32[17,128,128]{2,1,0:T(8,128)}, u32[]{:S(2)}, u32[]{:S(2)}) collective-permute-start(f32[17,128,128]{2,1,0:T(8,128)} %collective-permute-done.17.refs_1_), channel_id=1, source_target_pairs={{1,0},{2,1},{3,2},{4,3},{5,4},{6,5},{7,6},{8,7},{9,8},{10,9},{11,1... | collective-permute-start | bytes 3342344 | tf_op jit(solution)/shard_map/ppermute | solution.py:331
  185.4 33.7 %collective-permute-start.21 = (f32[17,128,128]{2,1,0:T(8,128)}, f32[17,128,128]{2,1,0:T(8,128)}, u32[]{:S(2)}, u32[]{:S(2)}) collective-permute-start(f32[17,128,128]{2,1,0:T(8,128)} %collective-permute-done.20.refs_4_), channel_id=1, source_target_pairs={{1,0},{2,1},{3,2},{4,3},{5,4},{6,5},{7,6},{8,7},{9,8},{10,9},{11,1... | collective-permute-start | bytes 3342344 | tf_op jit(solution)/shard_map/ppermute | solution.py:331
  187.4 35.2 %collective-permute-start.24 = (f32[17,128,128]{2,1,0:T(8,128)}, f32[17,128,128]{2,1,0:T(8,128)}, u32[]{:S(2)}, u32[]{:S(2)}) collective-permute-start(f32[17,128,128]{2,1,0:T(8,128)} %collective-permute-done.23.refs_7_), channel_id=1, source_target_pairs={{1,0},{2,1},{3,2},{4,3},{5,4},{6,5},{7,6},{8,7},{9,8},{10,9},{11,1... | collective-permute-start | bytes 3342344 | tf_op jit(solution)/shard_map/ppermute | solution.py:331
  189.5 13.5 %copy-start.7 = (f32[9,128,128]{2,1,0:T(8,128)}, f32[9,128,128]{2,1,0:T(8,128)S(1)}, u32[]{:S(2)}) copy-start(f32[9,128,128]{2,1,0:T(8,128)S(1)} %fusion.2.e0) | copy-start | bytes 1769476
  189.5 18.7 %copy-start.15 = (f32[1,2,17,17,4,4]{3,5,4,2,1,0:T(4,128)S(1)}, f32[1,2,17,17,4,4]{3,5,4,2,1,0:T(4,128)}, u32[]{:S(2)}) copy-start(f32[1,2,17,17,4,4]{3,5,4,2,1,0:T(4,128)} %param.15) | copy-start | bytes 110980
  199.4 27.4 %collective-permute-start.11 = (f32[9,128,128]{2,1,0:T(8,128)S(1)}, f32[9,128,128]{2,1,0:T(8,128)S(1)}, u32[]{:S(2)}, u32[]{:S(2)}) collective-permute-start(f32[9,128,128]{2,1,0:T(8,128)S(1)} %fusion.2.e0), channel_id=1, source_target_pairs={{0,32},{32,64},{64,96},{1,33},{33,65},{65,97},{2,34},{34,66},{66,9... | collective-permute-start | bytes 1769480 | tf_op jit(solution)/shard_map/ppermute | solution.py:331
  203.0 7.0 %copy-start.8 = (f32[8,128,128]{2,1,0:T(8,128)}, f32[8,128,128]{2,1,0:T(8,128)S(1)}, u32[]{:S(2)}) copy-start(f32[8,128,128]{2,1,0:T(8,128)S(1)} %fusion.5.e1) | copy-start | bytes 1572868
  203.0 1.0 copy-start.13
  204.1 22.7 %collective-permute-start.12 = (f32[8,128,128]{2,1,0:T(8,128)S(1)}, f32[8,128,128]{2,1,0:T(8,128)}, u32[]{:S(2)}, u32[]{:S(2)}) collective-permute-start(f32[8,128,128]{2,1,0:T(8,128)S(1)} %fusion.5.e1), channel_id=1, source_target_pairs={{0,32},{32,64},{64,96},{1,33},{33,65},{65,97},{2,34},{34,66},{66,9... | collective-permute-start | bytes 1572872 | tf_op jit(solution)/shard_map/ppermute | solution.py:331
  226.8 0.8 copy-start.20
where the time goes:
time: 287 us; the launch traced here: 285 us
  waiting for transfers between devices  89.4 us (31%)
  starting transfers between devices  86.1 us (30%)
  Pallas kernels  85.8 us (30%)
  other arithmetic  11.1 us (4%)
  local copies, waits for them, and re-layouts  10.1 us (4%)
    ppermute x25, waiting for transfers between devices, fetch(): return lax.ppermute(blocks, axis, pairs)  89.4 us
    ppermute x25, starting transfers between devices, fetch(): return lax.ppermute(blocks, axis, pairs)  86.1 us
    pallas_call x1, Pallas kernels, pair(): pl.pallas_call(pair_kernel, out_shape=jax.ShapeDtypeStruct((16, TILE, TIL...  57.1 us
    pallas_call x2, Pallas kernels, site(): pl.pallas_call(functools.partial(site_kernel, number), grid=(1,), out_sha...  20.3 us
    pallas_call x1, Pallas kernels, split_kets(): pl.pallas_call(kets_kernel, grid=(4,), out_shape=jax.ShapeDtypeStruct((4,...  5.87 us
  transfers between devices with their start and end apart: 25, of which 10 were waited for; matrix products, arithmetic and copies ran while one was open for 7% of the time, Pallas kernels for 6%

commit v1 on v0

--- a/solution.py
+++ b/solution.py
@@ -24,6 +24,16 @@
 def mix_tables(channel_class):
     steps = jnp.array(STATE_STEPS, dtype=jnp.int32)
     shifts = class_shift(channel_class)
+    source = (shifts[:, None] + steps[None, :]).reshape(-1)
+    goal = (jnp.array(CLASS_STEPS, dtype=jnp.int32)[:, None] + steps[None, :]).reshape(-1)
+    order = jnp.arange(4 * NW, dtype=jnp.int32)
+    allowed = goal[:, None] == source[None, :]
+    earlier = allowed[:, None, :] & (order[None, :] < order[:, None])
+    rank = earlier.astype(jnp.int32).sum(-1)
+    term = allowed[:, None, :] & (rank[:, None, :] == jnp.arange(LONG, dtype=jnp.int32)[:, None])
+    block = jnp.where(term, order, 0).sum(-1)
+    place = jnp.where(term, (order // 4) * (NW * 16) + order % 4 - RULE, 0).sum(-1) + RULE
+
     down = (jnp.arange(4) // 2)[:, None]
     up = (jnp.arange(4) % 2)[:, None]
     kind = channel_class[None, :]
@@ -36,22 +46,8 @@
     )
     channels = jnp.arange(NW, dtype=jnp.int32)
     key = jnp.where(three, 0, NW) + channels[None, :]
-    place = (key[:, None, :] < key[:, :, None]).astype(jnp.int32).sum(-1)
-    hot = place[:, None, :] == channels[None, :, None]
-    out = jnp.where(hot, channels, 0).sum(-1)
-    goal = jnp.where(hot, shifts, 0).sum(-1)
-    source = shifts[:, None] + steps[None, :]
-    allowed = (goal + steps[:, None])[:, :, None] == source.reshape(-1)[None, None, :]
-    size = 4 * NW
-    order = jnp.arange(size, dtype=jnp.int32)
-    earlier = (order[:, None] < order[None, :]).astype(F32)
-    rank = jnp.einsum("sim,mn->sin", allowed.astype(F32), earlier).astype(jnp.int32)
-    term = allowed[:, :, None, :] & (rank[:, :, None, :] == jnp.arange(LONG)[:, None])
-    count = allowed.astype(jnp.int32).sum(-1)
-    block = jnp.where(term, order, 0).sum(-1)
-    used = jnp.arange(LONG) < count[:, :, None]
-    place = (block // 4) * (NW * 16) + block % 4
-    place = jnp.where(used, place, RULE) + (out * 16 + 4 * jnp.arange(4)[:, None])[:, :, None]
+    position = (key[:, None, :] < key[:, :, None]).astype(jnp.int32).sum(-1)
+    out = jnp.where(position[:, None, :] == channels[:, None], channels, 0).sum(-1)
     return out.reshape(-1), block.reshape(-1), place.reshape(-1)
 
 
@@ -68,10 +64,12 @@
     return high, (x - high.astype(F32)).astype(BF16)
 
 
-def mix(blocks, base, block_ref, place_ref, rule_ref, rule, first, terms):
+def mix(blocks, base, block_ref, place_ref, rule_ref, v, kind, s, terms):
+    first = (4 * kind + s) * LONG
+    shift = 16 * v + 4 * s
     total = None
     for k in range(terms):
-        term = blocks[base + block_ref[first + k]] * rule_ref[rule * PADDED + place_ref[first + k]]
+        term = blocks[base + block_ref[first + k]] * rule_ref[place_ref[first + k] + shift]
         total = term if total is None else total + term
     return total
 
@@ -140,10 +138,10 @@
     for s in (3, 2, 1, 0):
 
         def close(terms, i):
-            place = s * NW + i
-            total = mix(product, 0, block_ref, place_ref, rule_ref, number, place * LONG, terms)
+            v = out_ref[s * NW + i]
+            total = mix(product, 0, block_ref, place_ref, rule_ref, v, class_ref[v], s, terms)
             result = folded(dot(jnp.concatenate(split(total), axis=1), bras[s]))
-            closed_refs[s][out_ref[place]] = result
+            closed_refs[s][v] = result
 
         loop(0, LONG, functools.partial(close, LONG), UNROLL_LONG)
         loop(LONG, NW, functools.partial(close, SHORT), UNROLL_SHORT)
@@ -201,22 +199,23 @@
 
 
 def pair_kernel(
-    sector_ref, region_ref, class_ref, live_ref, out_ref, block_ref, place_ref, rule_ref, p_ref,
+    sector_ref, region_ref, class_ref, live_ref, out_ref, block_ref, place_ref, left_ref, right_ref,
     start_ref, passed0_ref, passed1_ref, kets_hbm, *refs,
 ):
-    rights_hbm, (image_ref, kets, rights, envs, product, middle, lhs, outer, sems) = refs[:9], refs[9:]
+    rights_hbm = refs[:9]
+    image_ref, kets, arrived, rights, envs, even, odd, middle, outer, sems = refs[9:]
     sector = sector_ref[0]
 
     def kets_copy(t):
         return pltpu.make_async_copy(kets_hbm.at[t], kets.at[t], sems.at[t])
 
-    rights_copies = [
-        pltpu.make_async_copy(ref, rights.at[n], sems.at[4 + n]) for n, ref in enumerate(rights_hbm)
-    ]
+    def rights_copy(n):
+        return pltpu.make_async_copy(rights_hbm[n], arrived.at[n % 2], sems.at[4 + n % 2])
+
     for t in range(4):
         kets_copy(t).start()
-    for copy in rights_copies:
-        copy.start()
+    for n in range(2):
+        rights_copy(n).start()
 
     @pl.when(region_ref[0] == 0)
     def _():
@@ -232,52 +231,69 @@
             for n in range(ref.shape[0]):
                 envs[first + n] = stacked(ref[n])
 
-    def left_half(t2):
-        kets_copy(t2).wait()
-
-        def form(w):
-            result = folded(dot(kets[t2, class_ref[w]], envs[w]))
-            product[pl.ds(4 * w, 4)] = result.reshape(4, TILE, TILE)
-
-        loop(0, NW, form, 1)
-
-        def left(s):
+    def form(product, t2, w):
+        result = folded(dot(kets[t2, class_ref[w]], envs[w]))
+        product[pl.ds(4 * w, 4)] = result.reshape(4, TILE, TILE)
+
+    def left(product, t2, s, i):
+        v = out_ref[s * NW + i]
+        terms = LONG if i < LONG else SHORT
+        total = mix(product, 0, block_ref, place_ref, left_ref, v, class_ref[v], s, terms)
+        middle[s * 4 * NW + 4 * v + t2] = total
+
+    kets_copy(0).wait()
+    loop(0, NW, functools.partial(form, even, 0), 1)
+    for n in range(9):
+        rights_copy(n).wait()
+
+        def cut(x):
+            ups, downs = n // 3, n % 3
+            keep = inside(sector + ND * ups + downs + class_shift(class_ref[x]))
+            rights[n, x] = jnp.concatenate(split(arrived[n % 2, x] * keep), axis=0)
+
+        loop(0, NW, cut, 1)
+        if n + 2 < 9:
+            rights_copy(n + 2).start()
+    for t in range(1, 4):
+        kets_copy(t).wait()
+
+    def stage(here, there, t2):
+        later = jnp.minimum(t2 + 1, 3)
+
+        def step(s):
             for i in range(NW):
-                place = s * NW + i
-                terms = LONG if i < LONG else SHORT
-                total = mix(product, 0, block_ref, place_ref, rule_ref, 0, place * LONG, terms)
-                middle[s * 4 * NW + 4 * out_ref[place] + t2] = total
-
-        loop(0, 4, left, 1)
-
-    loop(0, 4, left_half, 1)
-    for copy in rights_copies:
-        copy.wait()
+                left(here, t2, s, i)
+                if i % 4 == 0:
+                    form(there, later, jnp.minimum(5 * s + i // 4, NW - 1))
+
+        loop(0, 4, step, 1)
+
+    def stages(half):
+        stage(even, odd, 2 * half)
+        stage(odd, even, 2 * half + 1)
+
+    loop(0, 2, stages, 1)
 
     rows = lax.broadcasted_iota(jnp.int32, (TILE, TILE), 0)
     columns = lax.broadcasted_iota(jnp.int32, (TILE, TILE), 1)
     own = live_ref[MAXLEN * NSEC + sector]
 
-    def right_half(n):
-        p = p_ref[n]
+    def right_half(p):
         s1 = p // 4
         s2 = p % 4
         ups = s1 % 2 + s2 % 2
         downs = s1 // 2 + s2 // 2
         far = sector + ND * ups + downs
+        lhs = []
         for i in range(NW):
-            place = s2 * NW + i
-            x = out_ref[place]
-            keep = inside(far + class_shift(class_ref[x]))
-            high, low = split(rights[3 * ups + downs, x] * keep)
-            lhs[:TILE, i * TILE : (i + 1) * TILE] = high
-            lhs[TILE:, i * TILE : (i + 1) * TILE] = low
+            x = out_ref[s2 * NW + i]
+            lhs.append(rights[3 * ups + downs, x])
             terms = LONG if i < LONG else SHORT
-            total = mix(middle, s1 * 4 * NW, block_ref, place_ref, rule_ref, 1, place * LONG, terms)
+            total = mix(middle, s1 * 4 * NW, block_ref, place_ref, right_ref, x, class_ref[x], s2, terms)
             high, low = split(total)
             outer[i * TILE : (i + 1) * TILE, :TILE] = high
             outer[i * TILE : (i + 1) * TILE, TILE:] = low
-        total = dot(lhs[...], outer[...])
+        total = dot(jnp.concatenate(lhs, axis=1), outer[...])
         total = folded(total[:TILE] + total[TILE:]).T
         count = jnp.where(far < NSEC, live_ref[MAXLEN * NSEC + jnp.minimum(far, NSEC - 1)], 0)
         image_ref[p] = jnp.where((rows < own) & (columns < count), total, 0.0)
@@ -286,7 +302,6 @@
 
 
 def pair(scalars, start, passed, kets, rights):
-    order = jnp.arange(16, dtype=jnp.int32)
     return pl.pallas_call(
         pair_kernel,
         out_shape=jax.ShapeDtypeStruct((16, TILE, TILE), F32),
@@ -294,18 +309,19 @@
         out_specs=VMEM_SPEC,
         scratch_shapes=[
             pltpu.VMEM((4, 5, 4 * TILE, 2 * TILE), BF16),
-            pltpu.VMEM((9, NW, TILE, TILE), F32),
+            pltpu.VMEM((2, NW, TILE, TILE), F32),
+            pltpu.VMEM((9, NW, 2 * TILE, TILE), BF16),
             pltpu.VMEM((NW, 2 * TILE, 2 * TILE), BF16),
             pltpu.VMEM((4 * NW, TILE, TILE), F32),
+            pltpu.VMEM((4 * NW, TILE, TILE), F32),
             pltpu.VMEM((16 * NW, TILE, TILE), F32),
-            pltpu.VMEM((2 * TILE, NW * TILE), BF16),
             pltpu.VMEM((NW * TILE, 2 * TILE), BF16),
-            pltpu.SemaphoreType.DMA((13,)),
+            pltpu.SemaphoreType.DMA((6,)),
         ],
         compiler_params=pltpu.CompilerParams(vmem_limit_bytes=60 * 2**20),
         cost_estimate=pl.CostEstimate(flops=20 * 10**9, bytes_accessed=18 * 10**6, transcendentals=0),
         name="pair",
-    )(*scalars, order, start, *passed, kets, *rights)
+    )(*scalars, start, *passed, kets, *rights)
 
 
 def turn_kernel(e0, e1, out_ref):
@@ -331,8 +347,8 @@
     return lax.ppermute(blocks, axis, pairs)
 
 
-def flat_rules(rules):
-    return jnp.pad(rules.reshape(2, RULE), ((0, 0), (0, PADDED - RULE))).reshape(-1)
+def flat_rule(rule):
+    return jnp.pad(rule.reshape(RULE), (0, PADDED - RULE))
 
 
 def shards(
@@ -371,13 +387,12 @@
 
     tables = mix_tables(channel_class)
     scalars = (sector, channel_class, live, *tables)
-    site_rules = flat_rules(mpo_sites)
-    h0, h1, h2, h3 = site(0, (*scalars, site_rules), [start], near)
+    h0, h1, h2, h3 = site(0, (*scalars, flat_rule(mpo_sites[0, 0])), [start], near)
     below3 = fetch(h3, -1)
     below2 = fetch(h2, -1)
     partial = fetch(h1 + below3, -ND)
 
-    h0, h1, h2, h3, first = site(1, (*scalars, site_rules), [h0, below2, partial], near)
+    h0, h1, h2, h3, first = site(1, (*scalars, flat_rule(mpo_sites[0, 1])), [h0, below2, partial], near)
     below3 = fetch(h3, -1)
     below2 = fetch(h2, -1)
     upper = h1 + below3
@@ -398,7 +413,7 @@
 
     environment = turned(parts)
     split = split_kets(sector, kets)
-    scalars = (sector, region, channel_class, live, *tables, flat_rules(mpo_pair))
+    scalars = (sector, region, channel_class, live, *tables, flat_rule(mpo_pair[0, 0]), flat_rule(mpo_pair[0, 1]))
     images = pair(scalars, start, passed, split, [rights[u, d] for u in range(3) for d in range(3)])
     return environment[None, :, None], images[None, :, None]
 

time: 287 us -> 291 us (1.014)
  local copies, waits for them, and re-layouts: 10.1 us -> 23 us
  waiting for transfers between devices: 89.4 us -> 85.9 us
  Pallas kernels: 85.8 us -> 82.7 us
    slice x0 -> x6, local copies, waits for them, and re-layouts: none -> 6.27 us  [the longest x2 3.88 us: shards(): mpo_sites[0, 0]]
    unnamed x44 -> x54, local copies, waits for them, and re-layouts: 4.23 us -> 10.2 us
    another operation x0 -> x4, local copies, waits for them, and re-layouts: none -> 4.25 us  [flat_rule(): return jnp.pad(rule.reshape(RULE), (0, PADDED - RULE))]
    reshape x4 -> x0, local copies, waits for them, and re-layouts: 3.73 us -> none  [the longest x2 2.91 us: flat_rules(): rules.reshape(2, RULE)]
    ppermute x25, waiting for transfers between devices: 89.4 us -> 85.9 us  [fetch(): return lax.ppermute(blocks, axis, pairs)]
    pallas_call x1, Pallas kernels: 57.1 us -> 54 us  [pair(): pl.pallas_call(pair_kernel, out_shape=jax.ShapeDtypeStruct((16, TILE, TIL...]
  transfers between devices with their start and end apart: 25 -> 25, of which waited for: 10 -> 9; matrix products, arithmetic and copies ran while one was open for 7% -> 8% of each run, Pallas kernels for 6% -> 6%
where the time goes in v1:
time: 291 us; the launch traced here: 289 us
  starting transfers between devices  86.6 us (30%)
  waiting for transfers between devices  85.9 us (30%)
  Pallas kernels  82.7 us (28%)
  local copies, waits for them, and re-layouts  23 us (8%)
  other arithmetic  8.93 us (3%)
    ppermute x25, starting transfers between devices, fetch(): return lax.ppermute(blocks, axis, pairs)  86.6 us
    ppermute x25, waiting for transfers between devices, fetch(): return lax.ppermute(blocks, axis, pairs)  85.9 us
    pallas_call x1, Pallas kernels, pair(): pl.pallas_call(pair_kernel, out_shape=jax.ShapeDtypeStruct((16, TILE, TIL...  54 us
    pallas_call x2, Pallas kernels, site(): pl.pallas_call(functools.partial(site_kernel, number), grid=(1,), out_sha...  20.2 us
    unnamed x54, local copies, waits for them, and re-layouts  10.2 us
    pallas_call x1, Pallas kernels, split_kets(): pl.pallas_call(kets_kernel, grid=(4,), out_shape=jax.ShapeDtypeStruct((4,...  5.88 us
  transfers between devices with their start and end apart: 25, of which 9 were waited for; matrix products, arithmetic and copies ran while one was open for 8% of the time, Pallas kernels for 6%

profile of v1, /device:TPU:32, one launch (start us, length us, event | category | flops | bytes accessed | tf_op | source)
XLA Modules:
  0.0 289.3 jit_solution(5400979856522883427)
XLA Ops:
  0.6 3.9 %collective-permute-start = (f32[2,4,128,128]{3,2,1,0:T(8,128)}, f32[2,4,128,128]{3,2,1,0:T(8,128)S(1)}, u32[]{:S(2)}, u32[]{:S(2)}) collective-permute-start(f32[2,4,128,128]{3,2,1,0:T(8,128)} %bitcast.24), channel_id=1, source_target_pairs={{1,0},{2,1},{3,2},{4,3},{5,4},{6,5},{7,6},{8,7},{9,8},{10,9},{11,1... | collective-permute-start | bytes 1572872 | tf_op jit(solution)/shard_map/ppermute | solution.py:347
  4.5 1.9 collective-permute-start.1
  6.5 1.9 collective-permute-start.2
  8.4 3.9 %collective-permute-start.3 = (f32[2,4,128,128]{3,2,1,0:T(8,128)}, f32[2,4,128,128]{3,2,1,0:T(8,128)}, u32[]{:S(2)}, u32[]{:S(2)}) collective-permute-start(f32[2,4,128,128]{3,2,1,0:T(8,128)} %bitcast.27), channel_id=1, source_target_pairs={{0,8},{1,9},{2,10},{3,11},{4,12},{5,13},{6,14},{7,15},{8,16},{9,17... | collective-permute-start | bytes 1572872 | tf_op jit(solution)/shard_map/ppermute | solution.py:347
  18.8 1.7 fusion.12
  20.5 2.2 copy.38
  22.7 1.6 reshape_squeeze.16
  26.0 2.7 collective-permute-done.3.refs_5_.refs_7_
  29.8 1.0 copy-done.14
  30.8 10.7 %shard_map.122 = (f32[17,128,128]{2,1,0:T(8,128)S(1)}, f32[17,128,128]{2,1,0:T(8,128)S(1)}, f32[17,128,128]{2,1,0:T(8,128)S(1)}, f32[17,128,128]{2,1,0:T(8,128)S(1)}) custom-call(s32[1]{0:T(128)} %bitcast.2.sector_ref, s32[17]{0:T(128)S(1)} %copy-done, s32[96]{0:T(128)S(1)} %reshape.406.live_ref, s32[68]{0:T(128)S(1)} %reshape.407.out_ref, ...), custom_call_target="tpu_custom_call" | custom-call | flops 4000000000 | bytes 10000000 | tf_op jit(solution)/shard_map/pallas_call | solution.py:161
  41.5 2.0 collective-permute-start.5
  43.6 1.9 collective-permute-start.19
  45.5 1.9 collective-permute-start.4
  47.4 13.0 %collective-permute-done.5 = f32[17,128,128]{2,1,0:T(8,128)S(1)} collective-permute-done((f32[17,128,128]{2,1,0:T(8,128)S(1)}, f32[17,128,128]{2,1,0:T(8,128)S(1)}, u32[]{:S(2)}, u32[]{:S(2)}) %collective-permute-start.5) | collective-permute-done | bytes 1114144 | tf_op jit(solution)/shard_map/ppermute | solution.py:347
  60.5 1.1 add.152
  61.6 3.8 %collective-permute-start.6 = (f32[17,128,128]{2,1,0:T(8,128)}, f32[17,128,128]{2,1,0:T(8,128)S(1)}, u32[]{:S(2)}, u32[]{:S(2)}) collective-permute-start(f32[17,128,128]{2,1,0:T(8,128)} %add.152), channel_id=1, source_target_pairs={{0,8},{1,9},{2,10},{3,11},{4,12},{5,13},{6,14},{7,15},{8,16},{9,17... | collective-permute-start | bytes 3342344 | tf_op jit(solution)/shard_map/ppermute | solution.py:347
  65.4 1.9 collective-permute-start.13
  67.4 2.4 collective-permute-start.14
  69.8 1.3 copy.37
  71.1 1.6 reshape_squeeze.15
  72.7 3.2 %collective-permute-start.22 = (f32[17,128,128]{2,1,0:T(8,128)}, f32[17,128,128]{2,1,0:T(8,128)S(1)}, u32[]{:S(2)}, u32[]{:S(2)}) collective-permute-start(f32[17,128,128]{2,1,0:T(8,128)} %collective-permute-done.19.refs_3_), channel_id=1, source_target_pairs={{8,0},{9,1},{10,2},{11,3},{12,4},{13,5},{14,6},{15,7},{16,8},{17,9... | collective-permute-start | bytes 3342344 | tf_op jit(solution)/shard_map/ppermute | solution.py:347
  76.0 31.5 %collective-permute-done.6.refs_2_ = f32[17,128,128]{2,1,0:T(8,128)S(1)} collective-permute-done((f32[17,128,128]{2,1,0:T(8,128)}, f32[17,128,128]{2,1,0:T(8,128)S(1)}, u32[]{:S(2)}, u32[]{:S(2)}) %collective-permute-start.6) | collective-permute-done | bytes 1114144 | tf_op jit(solution)/shard_map/ppermute | solution.py:347
  110.7 1.0 copy-done.15
  111.7 1.2 copy-done.17
  113.0 9.5 %shard_map.123 = (f32[17,128,128]{2,1,0:T(8,128)S(1)}, f32[17,128,128]{2,1,0:T(8,128)S(1)}, f32[17,128,128]{2,1,0:T(8,128)S(1)}, f32[17,128,128]{2,1,0:T(8,128)S(1)}, f32[17,128,128]{2,1,0:T(8,128)S(1)}) custom-call(s32[1]{0:T(128)} %bitcast.2.sector_ref, s32[17]{0:T(128)S(1)} %copy-done, s32[96]{0:T(128)S(1)} %reshape.406.live_ref, ...), custom_call_target="tpu_custom_call" | custom-call | flops 4000000000 | bytes 10000000 | tf_op jit(solution)/shard_map/pallas_call | solution.py:161
  122.5 1.9 collective-permute-start.8
  124.4 1.9 collective-permute-start.15
  126.3 5.1 %collective-permute-start.17 = (f32[17,128,128]{2,1,0:T(8,128)}, f32[17,128,128]{2,1,0:T(8,128)}, u32[]{:S(2)}, u32[]{:S(2)}) collective-permute-start(f32[17,128,128]{2,1,0:T(8,128)} %bitcast.14.refs_0_), channel_id=1, source_target_pairs={{1,0},{2,1},{3,2},{4,3},{5,4},{6,5},{7,6},{8,7},{9,8},{10,9},{11,1... | collective-permute-start | bytes 3342344 | tf_op jit(solution)/shard_map/ppermute | solution.py:347
  131.5 1.9 collective-permute-start.20
  133.4 1.9 collective-permute-start.23
  135.4 6.0 %collective-permute-done.8 = f32[17,128,128]{2,1,0:T(8,128)S(1)} collective-permute-done((f32[17,128,128]{2,1,0:T(8,128)S(1)}, f32[17,128,128]{2,1,0:T(8,128)S(1)}, u32[]{:S(2)}, u32[]{:S(2)}) %collective-permute-start.8) | collective-permute-done | bytes 1114144 | tf_op jit(solution)/shard_map/ppermute | solution.py:347
  141.4 1.9 collective-permute-start.7
  144.1 7.6 %collective-permute-done.15 = f32[16,128,128]{2,1,0:T(8,128)S(1)} collective-permute-done((f32[16,128,128]{2,1,0:T(8,128)}, f32[16,128,128]{2,1,0:T(8,128)S(1)}, u32[]{:S(2)}, u32[]{:S(2)}) %collective-permute-start.15) | collective-permute-done | bytes 1048608 | tf_op jit(solution)/shard_map/ppermute | solution.py:347
  151.8 3.6 %collective-permute-start.9 = (f32[9,128,128]{2,1,0:T(8,128)S(1)}, f32[9,128,128]{2,1,0:T(8,128)S(1)}, u32[]{:S(2)}, u32[]{:S(2)}) collective-permute-start(f32[9,128,128]{2,1,0:T(8,128)S(1)} %slice.63), channel_id=1, source_target_pairs={{0,8},{1,9},{2,10},{3,11},{4,12},{5,13},{6,14},{7,15},{8,16},{9,17... | collective-permute-start | bytes 1769480 | tf_op jit(solution)/shard_map/ppermute | solution.py:347
  156.9 1.9 collective-permute-start.16
  159.0 2.3 collective-permute-start.10
  161.7 6.9 %collective-permute-done.23.refs_7_ = f32[17,128,128]{2,1,0:T(8,128)} collective-permute-done((f32[17,128,128]{2,1,0:T(8,128)S(1)}, f32[17,128,128]{2,1,0:T(8,128)}, u32[]{:S(2)}, u32[]{:S(2)}) %collective-permute-start.23) | collective-permute-done | bytes 1114144 | tf_op jit(solution)/shard_map/ppermute | solution.py:347
  168.6 24.4 %collective-permute-start.18 = (f32[17,128,128]{2,1,0:T(8,128)}, f32[17,128,128]{2,1,0:T(8,128)}, u32[]{:S(2)}, u32[]{:S(2)}) collective-permute-start(f32[17,128,128]{2,1,0:T(8,128)} %collective-permute-done.17.refs_1_), channel_id=1, source_target_pairs={{1,0},{2,1},{3,2},{4,3},{5,4},{6,5},{7,6},{8,7},{9,8},{10,9},{11,1... | collective-permute-start | bytes 3342344 | tf_op jit(solution)/shard_map/ppermute | solution.py:347
  193.0 1.9 collective-permute-start.21
  194.9 1.9 collective-permute-start.24
  197.0 9.6 %collective-permute-done.10 = f32[8,128,128]{2,1,0:T(8,128)S(1)} collective-permute-done((f32[8,128,128]{2,1,0:T(8,128)S(1)}, f32[8,128,128]{2,1,0:T(8,128)S(1)}, u32[]{:S(2)}, u32[]{:S(2)}) %collective-permute-start.10) | collective-permute-done | bytes 524320 | tf_op jit(solution)/shard_map/ppermute | solution.py:347
  206.7 3.4 %collective-permute-start.11 = (f32[9,128,128]{2,1,0:T(8,128)S(1)}, f32[9,128,128]{2,1,0:T(8,128)S(1)}, u32[]{:S(2)}, u32[]{:S(2)}) collective-permute-start(f32[9,128,128]{2,1,0:T(8,128)S(1)} %fusion.2.e0), channel_id=1, source_target_pairs={{0,32},{32,64},{64,96},{1,33},{33,65},{65,97},{2,34},{34,66},{66,9... | collective-permute-start | bytes 1769480 | tf_op jit(solution)/shard_map/ppermute | solution.py:347
  210.3 3.5 %collective-permute-start.12 = (f32[8,128,128]{2,1,0:T(8,128)S(1)}, f32[8,128,128]{2,1,0:T(8,128)S(1)}, u32[]{:S(2)}, u32[]{:S(2)}) collective-permute-start(f32[8,128,128]{2,1,0:T(8,128)S(1)} %fusion.5.e1), channel_id=1, source_target_pairs={{0,32},{32,64},{64,96},{1,33},{33,65},{65,97},{2,34},{34,66},{66,9... | collective-permute-start | bytes 1572872 | tf_op jit(solution)/shard_map/ppermute | solution.py:347
  217.1 5.9 %split_kets.1.kets_hbm = bf16[4,5,512,256]{3,2,1,0:T(8,128)(2,1)} custom-call(s32[1]{0:T(128)} %bitcast.2.sector_ref, f32[4,4,128,128]{3,2,1,0:T(8,128)} %bitcast.8.k0, f32[4,4,128,128]{3,2,1,0:T(8,128)} %bitcast.10.k1, f32[4,4,128,128]{3,2,1,0:T(8,128)} %bitcast.11.k2, f32[4,4,128,128]{3,2,1,0:T(8,128)} %bitcast.31, f32[4,4,128,128]{3,2,1,0:T(8,128)} %bitcast.32), custom_call_target="tpu_custom_call" | custom-call | flops 5000000 | bytes 10000000 | tf_op jit(solution)/shard_map/split_kets/pallas_call | solution.py:190
  223.0 2.6 turn.1
  225.6 4.6 %collective-permute-done.24.refs_8_ = f32[17,128,128]{2,1,0:T(8,128)} collective-permute-done((f32[17,128,128]{2,1,0:T(8,128)}, f32[17,128,128]{2,1,0:T(8,128)}, u32[]{:S(2)}, u32[]{:S(2)}) %collective-permute-start.24) | collective-permute-done | bytes 1114144 | tf_op jit(solution)/shard_map/ppermute | solution.py:347
  230.2 3.9 %collective-permute-done.12.passed1_ref = f32[8,128,128]{2,1,0:T(8,128)S(1)} collective-permute-done((f32[8,128,128]{2,1,0:T(8,128)S(1)}, f32[8,128,128]{2,1,0:T(8,128)S(1)}, u32[]{:S(2)}, u32[]{:S(2)}) %collective-permute-start.12) | collective-permute-done | bytes 524320 | tf_op jit(solution)/shard_map/ppermute | solution.py:347
  235.0 54.0 %pair.1 = f32[16,128,128]{2,1,0:T(8,128)} custom-call(s32[1]{0:T(128)} %bitcast.2.sector_ref, s32[1]{0:T(128)} %bitcast.7.region_ref, s32[17]{0:T(128)} %class_ref.5, s32[96]{0:T(128)} %copy-done.4, s32[68]{0:T(128)} %copy-done.3, s32[220]{0:T(256)} %copy-done.2, s32[220]{0:T(256)} %copy-done.1, f32[4896]{0:T(1024)} %pad.15.left_ref, f32[4896]{0:T(1024)} %pad.16.right_ref, ...), custom_call_target="tpu_custom_call" | custom-call | flops 20000000000 | bytes 18000000 | tf_op jit(solution)/shard_map/pair/pallas_call | solution.py:305
  (114 shorter events, 19.1 us)
Async XLA Ops:
  0.6 23.7 %collective-permute-start = (f32[2,4,128,128]{3,2,1,0:T(8,128)}, f32[2,4,128,128]{3,2,1,0:T(8,128)S(1)}, u32[]{:S(2)}, u32[]{:S(2)}) collective-permute-start(f32[2,4,128,128]{3,2,1,0:T(8,128)} %bitcast.24), channel_id=1, source_target_pairs={{1,0},{2,1},{3,2},{4,3},{5,4},{6,5},{7,6},{8,7},{9,8},{10,9},{11,1... | collective-permute-start | bytes 1572872 | tf_op jit(solution)/shard_map/ppermute | solution.py:347
  4.5 19.8 %collective-permute-start.1 = (f32[2,4,128,128]{3,2,1,0:T(8,128)}, f32[2,4,128,128]{3,2,1,0:T(8,128)S(1)}, u32[]{:S(2)}, u32[]{:S(2)}) collective-permute-start(f32[2,4,128,128]{3,2,1,0:T(8,128)} %bitcast.25), channel_id=1, source_target_pairs={{0,1},{1,2},{2,3},{3,4},{4,5},{5,6},{6,7},{7,8},{8,9},{9,10},{10,1... | collective-permute-start | bytes 1572872 | tf_op jit(solution)/shard_map/ppermute | solution.py:347
  6.5 18.7 %collective-permute-start.2 = (f32[2,4,128,128]{3,2,1,0:T(8,128)}, f32[2,4,128,128]{3,2,1,0:T(8,128)S(1)}, u32[]{:S(2)}, u32[]{:S(2)}) collective-permute-start(f32[2,4,128,128]{3,2,1,0:T(8,128)} %bitcast.26), channel_id=1, source_target_pairs={{8,0},{9,1},{10,2},{11,3},{12,4},{13,5},{14,6},{15,7},{16,8},{17,9... | collective-permute-start | bytes 1572872 | tf_op jit(solution)/shard_map/ppermute | solution.py:347
  8.4 20.3 %collective-permute-start.3 = (f32[2,4,128,128]{3,2,1,0:T(8,128)}, f32[2,4,128,128]{3,2,1,0:T(8,128)}, u32[]{:S(2)}, u32[]{:S(2)}) collective-permute-start(f32[2,4,128,128]{3,2,1,0:T(8,128)} %bitcast.27), channel_id=1, source_target_pairs={{0,8},{1,9},{2,10},{3,11},{4,12},{5,13},{6,14},{7,15},{8,16},{9,17... | collective-permute-start | bytes 1572872 | tf_op jit(solution)/shard_map/ppermute | solution.py:347
  13.1 15.6 %copy-start = (s32[17]{0:T(128)S(1)}, s32[17]{0:T(128)}, u32[]{:S(2)}) copy-start(s32[17]{0:T(128)} %class_ref.5) | copy-start | bytes 208
  13.1 15.6 %copy-start.5 = (f32[1,17,1,128,128]{4,3,2,1,0:T(8,128)S(1)}, f32[1,17,1,128,128]{4,3,2,1,0:T(8,128)}, u32[]{:S(2)}) copy-start(f32[1,17,1,128,128]{4,3,2,1,0:T(8,128)} %param.11) | copy-start | bytes 3342340
  13.2 15.6 %copy-start.6 = (f32[1,2,4,1,128,128]{5,4,3,2,1,0:T(8,128)S(1)}, f32[1,2,4,1,128,128]{5,4,3,2,1,0:T(8,128)}, u32[]{:S(2)}) copy-start(f32[1,2,4,1,128,128]{5,4,3,2,1,0:T(8,128)} %param.13) | copy-start | bytes 1572868
  14.4 93.1 %copy-start.3 = (s32[68]{0:T(128)}, s32[68]{0:T(128)S(1)}, u32[]{:S(2)}) copy-start(s32[68]{0:T(128)S(1)} %reshape.407.out_ref) | copy-start | bytes 820
  17.8 89.7 %copy-start.1 = (s32[220]{0:T(256)}, s32[220]{0:T(256)S(1)}, u32[]{:S(2)}) copy-start(s32[220]{0:T(256)S(1)} %add.151.place_ref) | copy-start | bytes 2644
  18.0 89.5 %copy-start.2 = (s32[220]{0:T(256)}, s32[220]{0:T(256)S(1)}, u32[]{:S(2)}) copy-start(s32[220]{0:T(256)S(1)} %reshape.408.block_ref) | copy-start | bytes 2644
  18.8 88.7 %copy-start.4 = (s32[96]{0:T(128)}, s32[96]{0:T(128)S(1)}, u32[]{:S(2)}) copy-start(s32[96]{0:T(128)S(1)} %reshape.406.live_ref) | copy-start | bytes 1156
  24.3 17.2 %copy-start.8 = (f32[2,4,128,128]{3,2,1,0:T(8,128)}, f32[2,4,128,128]{3,2,1,0:T(8,128)S(1)}, u32[]{:S(2)}) copy-start(f32[2,4,128,128]{3,2,1,0:T(8,128)S(1)} %collective-permute-done.refs_2_.refs_4_) | copy-start | bytes 1572868
  28.7 1.0 copy-start.11
  29.8 1.0 copy-start.14
  41.5 20.1 %copy-start.16 = (f32[17,128,128]{2,1,0:T(8,128)}, f32[17,128,128]{2,1,0:T(8,128)S(1)}, u32[]{:S(2)}) copy-start(f32[17,128,128]{2,1,0:T(8,128)S(1)} %get-tuple-element.11.refs_0_) | copy-start | bytes 3342340
  41.5 18.9 %collective-permute-start.5 = (f32[17,128,128]{2,1,0:T(8,128)S(1)}, f32[17,128,128]{2,1,0:T(8,128)S(1)}, u32[]{:S(2)}, u32[]{:S(2)}) collective-permute-start(f32[17,128,128]{2,1,0:T(8,128)S(1)} %get-tuple-element.14), channel_id=1, source_target_pairs={{0,1},{1,2},{2,3},{3,4},{4,5},{5,6},{6,7},{7,8},{8,9},{9,10},{10,1... | collective-permute-start | bytes 3342344 | tf_op jit(solution)/shard_map/ppermute | solution.py:347
  43.6 29.1 %collective-permute-start.19 = (f32[17,128,128]{2,1,0:T(8,128)}, f32[17,128,128]{2,1,0:T(8,128)}, u32[]{:S(2)}, u32[]{:S(2)}) collective-permute-start(f32[17,128,128]{2,1,0:T(8,128)} %bitcast.14.refs_0_), channel_id=1, source_target_pairs={{8,0},{9,1},{10,2},{11,3},{12,4},{13,5},{14,6},{15,7},{16,8},{17,9... | collective-permute-start | bytes 3342344 | tf_op jit(solution)/shard_map/ppermute | solution.py:347
  45.5 30.5 %collective-permute-start.4 = (f32[17,128,128]{2,1,0:T(8,128)S(1)}, f32[17,128,128]{2,1,0:T(8,128)S(1)}, u32[]{:S(2)}, u32[]{:S(2)}) collective-permute-start(f32[17,128,128]{2,1,0:T(8,128)S(1)} %get-tuple-element.12), channel_id=1, source_target_pairs={{0,1},{1,2},{2,3},{3,4},{4,5},{5,6},{6,7},{7,8},{8,9},{9,10},{10,1... | collective-permute-start | bytes 3342344 | tf_op jit(solution)/shard_map/ppermute | solution.py:347
  61.6 45.9 %collective-permute-start.6 = (f32[17,128,128]{2,1,0:T(8,128)}, f32[17,128,128]{2,1,0:T(8,128)S(1)}, u32[]{:S(2)}, u32[]{:S(2)}) collective-permute-start(f32[17,128,128]{2,1,0:T(8,128)} %add.152), channel_id=1, source_target_pairs={{0,8},{1,9},{2,10},{3,11},{4,12},{5,13},{6,14},{7,15},{8,16},{9,17... | collective-permute-start | bytes 3342344 | tf_op jit(solution)/shard_map/ppermute | solution.py:347
  65.4 60.9 %collective-permute-start.13 = (f32[16,128,128]{2,1,0:T(8,128)}, f32[16,128,128]{2,1,0:T(8,128)}, u32[]{:S(2)}, u32[]{:S(2)}) collective-permute-start(f32[16,128,128]{2,1,0:T(8,128)} %bitcast.9), channel_id=1, source_target_pairs={{1,0},{2,1},{3,2},{4,3},{5,4},{6,5},{7,6},{8,7},{9,8},{10,9},{11,1... | collective-permute-start | bytes 3145736 | tf_op jit(solution)/shard_map/ppermute | solution.py:347
  67.4 64.1 %collective-permute-start.14 = (f32[16,128,128]{2,1,0:T(8,128)}, f32[16,128,128]{2,1,0:T(8,128)}, u32[]{:S(2)}, u32[]{:S(2)}) collective-permute-start(f32[16,128,128]{2,1,0:T(8,128)} %bitcast.9), channel_id=1, source_target_pairs={{0,1},{1,2},{2,3},{3,4},{4,5},{5,6},{6,7},{7,8},{8,9},{9,10},{10,1... | collective-permute-start | bytes 3145736 | tf_op jit(solution)/shard_map/ppermute | solution.py:347
  72.7 60.7 %collective-permute-start.22 = (f32[17,128,128]{2,1,0:T(8,128)}, f32[17,128,128]{2,1,0:T(8,128)S(1)}, u32[]{:S(2)}, u32[]{:S(2)}) collective-permute-start(f32[17,128,128]{2,1,0:T(8,128)} %collective-permute-done.19.refs_3_), channel_id=1, source_target_pairs={{8,0},{9,1},{10,2},{11,3},{12,4},{13,5},{14,6},{15,7},{16,8},{17,9... | collective-permute-start | bytes 3342344 | tf_op jit(solution)/shard_map/ppermute | solution.py:347
  107.5 1.0 copy-start.7
  108.6 1.0 copy-start.9
  109.6 1.0 copy-start.12
  110.7 1.0 copy-start.15
  111.7 1.2 copy-start.17
  113.0 30.4 %copy-start.23 = (s32[1,3,32]{2,0,1:T(1,128)S(1)}, s32[1,3,32]{2,0,1:T(1,128)}, u32[]{:S(2)}) copy-start(s32[1,3,32]{2,0,1:T(1,128)} %param.18) | copy-start | bytes 1156
  122.5 18.9 %collective-permute-start.8 = (f32[17,128,128]{2,1,0:T(8,128)S(1)}, f32[17,128,128]{2,1,0:T(8,128)S(1)}, u32[]{:S(2)}, u32[]{:S(2)}) collective-permute-start(f32[17,128,128]{2,1,0:T(8,128)S(1)} %get-tuple-element.18), channel_id=1, source_target_pairs={{0,1},{1,2},{2,3},{3,4},{4,5},{5,6},{6,7},{7,8},{8,9},{9,10},{10,1... | collective-permute-start | bytes 3342344 | tf_op jit(solution)/shard_map/ppermute | solution.py:347
  124.4 27.4 %collective-permute-start.15 = (f32[16,128,128]{2,1,0:T(8,128)}, f32[16,128,128]{2,1,0:T(8,128)S(1)}, u32[]{:S(2)}, u32[]{:S(2)}) collective-permute-start(f32[16,128,128]{2,1,0:T(8,128)} %bitcast.9), channel_id=1, source_target_pairs={{8,0},{9,1},{10,2},{11,3},{12,4},{13,5},{14,6},{15,7},{16,8},{17,9... | collective-permute-start | bytes 3145736 | tf_op jit(solution)/shard_map/ppermute | solution.py:347
  126.3 30.5 %collective-permute-start.17 = (f32[17,128,128]{2,1,0:T(8,128)}, f32[17,128,128]{2,1,0:T(8,128)}, u32[]{:S(2)}, u32[]{:S(2)}) collective-permute-start(f32[17,128,128]{2,1,0:T(8,128)} %bitcast.14.refs_0_), channel_id=1, source_target_pairs={{1,0},{2,1},{3,2},{4,3},{5,4},{6,5},{7,6},{8,7},{9,8},{10,9},{11,1... | collective-permute-start | bytes 3342344 | tf_op jit(solution)/shard_map/ppermute | solution.py:347
  131.5 27.5 %collective-permute-start.20 = (f32[17,128,128]{2,1,0:T(8,128)}, f32[17,128,128]{2,1,0:T(8,128)}, u32[]{:S(2)}, u32[]{:S(2)}) collective-permute-start(f32[17,128,128]{2,1,0:T(8,128)} %collective-permute-done.19.refs_3_), channel_id=1, source_target_pairs={{1,0},{2,1},{3,2},{4,3},{5,4},{6,5},{7,6},{8,7},{9,8},{10,9},{11,1... | collective-permute-start | bytes 3342344 | tf_op jit(solution)/shard_map/ppermute | solution.py:347
  133.4 10.7 %copy-start.24 = (f32[17,128,128]{2,1,0:T(8,128)}, f32[17,128,128]{2,1,0:T(8,128)S(1)}, u32[]{:S(2)}) copy-start(f32[17,128,128]{2,1,0:T(8,128)S(1)} %collective-permute-done.22.refs_6_) | copy-start | bytes 3342340
  133.4 35.2 %collective-permute-start.23 = (f32[17,128,128]{2,1,0:T(8,128)S(1)}, f32[17,128,128]{2,1,0:T(8,128)}, u32[]{:S(2)}, u32[]{:S(2)}) collective-permute-start(f32[17,128,128]{2,1,0:T(8,128)S(1)} %collective-permute-done.22.refs_6_), channel_id=1, source_target_pairs={{1,0},{2,1},{3,2},{4,3},{5,4},{6,5},{7,6},{8,7},{9,8},{10,9},{11,1... | collective-permute-start | bytes 3342344 | tf_op jit(solution)/shard_map/ppermute | solution.py:347
  141.4 51.6 %collective-permute-start.7 = (f32[17,128,128]{2,1,0:T(8,128)S(1)}, f32[17,128,128]{2,1,0:T(8,128)S(1)}, u32[]{:S(2)}, u32[]{:S(2)}) collective-permute-start(f32[17,128,128]{2,1,0:T(8,128)S(1)} %get-tuple-element.16), channel_id=1, source_target_pairs={{0,1},{1,2},{2,3},{3,4},{4,5},{5,6},{6,7},{7,8},{8,9},{9,10},{10,1... | collective-permute-start | bytes 3342344 | tf_op jit(solution)/shard_map/ppermute | solution.py:347
  151.8 45.3 %copy-start.20 = (f32[16,128,128]{2,1,0:T(8,128)}, f32[16,128,128]{2,1,0:T(8,128)S(1)}, u32[]{:S(2)}) copy-start(f32[16,128,128]{2,1,0:T(8,128)S(1)} %collective-permute-done.15) | copy-start | bytes 3145732
  151.8 43.2 %collective-permute-start.9 = (f32[9,128,128]{2,1,0:T(8,128)S(1)}, f32[9,128,128]{2,1,0:T(8,128)S(1)}, u32[]{:S(2)}, u32[]{:S(2)}) collective-permute-start(f32[9,128,128]{2,1,0:T(8,128)S(1)} %slice.63), channel_id=1, source_target_pairs={{0,8},{1,9},{2,10},{3,11},{4,12},{5,13},{6,14},{7,15},{8,16},{9,17... | collective-permute-start | bytes 1769480 | tf_op jit(solution)/shard_map/ppermute | solution.py:347
  156.9 53.3 %collective-permute-start.16 = (f32[16,128,128]{2,1,0:T(8,128)}, f32[16,128,128]{2,1,0:T(8,128)S(1)}, u32[]{:S(2)}, u32[]{:S(2)}) collective-permute-start(f32[16,128,128]{2,1,0:T(8,128)} %bitcast.9), channel_id=1, source_target_pairs={{0,8},{1,9},{2,10},{3,11},{4,12},{5,13},{6,14},{7,15},{8,16},{9,17... | collective-permute-start | bytes 3145736 | tf_op jit(solution)/shard_map/ppermute | solution.py:347
  159.0 47.7 %collective-permute-start.10 = (f32[8,128,128]{2,1,0:T(8,128)S(1)}, f32[8,128,128]{2,1,0:T(8,128)S(1)}, u32[]{:S(2)}, u32[]{:S(2)}) collective-permute-start(f32[8,128,128]{2,1,0:T(8,128)S(1)} %slice.66), channel_id=1, source_target_pairs={{0,8},{1,9},{2,10},{3,11},{4,12},{5,13},{6,14},{7,15},{8,16},{9,17... | collective-permute-start | bytes 1572872 | tf_op jit(solution)/shard_map/ppermute | solution.py:347
  168.6 57.0 %collective-permute-start.18 = (f32[17,128,128]{2,1,0:T(8,128)}, f32[17,128,128]{2,1,0:T(8,128)}, u32[]{:S(2)}, u32[]{:S(2)}) collective-permute-start(f32[17,128,128]{2,1,0:T(8,128)} %collective-permute-done.17.refs_1_), channel_id=1, source_target_pairs={{1,0},{2,1},{3,2},{4,3},{5,4},{6,5},{7,6},{8,7},{9,8},{10,9},{11,1... | collective-permute-start | bytes 3342344 | tf_op jit(solution)/shard_map/ppermute | solution.py:347
  193.0 32.6 %collective-permute-start.21 = (f32[17,128,128]{2,1,0:T(8,128)}, f32[17,128,128]{2,1,0:T(8,128)}, u32[]{:S(2)}, u32[]{:S(2)}) collective-permute-start(f32[17,128,128]{2,1,0:T(8,128)} %collective-permute-done.20.refs_4_), channel_id=1, source_target_pairs={{1,0},{2,1},{3,2},{4,3},{5,4},{6,5},{7,6},{8,7},{9,8},{10,9},{11,1... | collective-permute-start | bytes 3342344 | tf_op jit(solution)/shard_map/ppermute | solution.py:347
  194.9 35.2 %collective-permute-start.24 = (f32[17,128,128]{2,1,0:T(8,128)}, f32[17,128,128]{2,1,0:T(8,128)}, u32[]{:S(2)}, u32[]{:S(2)}) collective-permute-start(f32[17,128,128]{2,1,0:T(8,128)} %collective-permute-done.23.refs_7_), channel_id=1, source_target_pairs={{1,0},{2,1},{3,2},{4,3},{5,4},{6,5},{7,6},{8,7},{9,8},{10,9},{11,1... | collective-permute-start | bytes 3342344 | tf_op jit(solution)/shard_map/ppermute | solution.py:347
  197.0 13.2 %copy-start.18 = (f32[9,128,128]{2,1,0:T(8,128)}, f32[9,128,128]{2,1,0:T(8,128)S(1)}, u32[]{:S(2)}) copy-start(f32[9,128,128]{2,1,0:T(8,128)S(1)} %fusion.2.e0) | copy-start | bytes 1769476
  197.0 16.7 %copy-start.22 = (f32[1,2,17,17,4,4]{3,5,4,2,1,0:T(4,128)S(1)}, f32[1,2,17,17,4,4]{3,5,4,2,1,0:T(4,128)}, u32[]{:S(2)}) copy-start(f32[1,2,17,17,4,4]{3,5,4,2,1,0:T(4,128)} %param.16) | copy-start | bytes 110980
  206.7 27.4 %collective-permute-start.11 = (f32[9,128,128]{2,1,0:T(8,128)S(1)}, f32[9,128,128]{2,1,0:T(8,128)S(1)}, u32[]{:S(2)}, u32[]{:S(2)}) collective-permute-start(f32[9,128,128]{2,1,0:T(8,128)S(1)} %fusion.2.e0), channel_id=1, source_target_pairs={{0,32},{32,64},{64,96},{1,33},{33,65},{65,97},{2,34},{34,66},{66,9... | collective-permute-start | bytes 1769480 | tf_op jit(solution)/shard_map/ppermute | solution.py:347
  210.2 5.8 %copy-start.19 = (f32[8,128,128]{2,1,0:T(8,128)}, f32[8,128,128]{2,1,0:T(8,128)S(1)}, u32[]{:S(2)}) copy-start(f32[8,128,128]{2,1,0:T(8,128)S(1)} %fusion.5.e1) | copy-start | bytes 1572868
  210.2 3.5 %copy-start.21 = (f32[16,128,128]{2,1,0:T(8,128)}, f32[16,128,128]{2,1,0:T(8,128)S(1)}, u32[]{:S(2)}) copy-start(f32[16,128,128]{2,1,0:T(8,128)S(1)} %collective-permute-done.16) | copy-start | bytes 3145732
  210.3 23.8 %collective-permute-start.12 = (f32[8,128,128]{2,1,0:T(8,128)S(1)}, f32[8,128,128]{2,1,0:T(8,128)S(1)}, u32[]{:S(2)}, u32[]{:S(2)}) collective-permute-start(f32[8,128,128]{2,1,0:T(8,128)S(1)} %fusion.5.e1), channel_id=1, source_target_pairs={{0,32},{32,64},{64,96},{1,33},{33,65},{65,97},{2,34},{34,66},{66,9... | collective-permute-start | bytes 1572872 | tf_op jit(solution)/shard_map/ppermute | solution.py:347
  (4 other events, 3.4 us)

commit v2 on v1

--- a/solution.py
+++ b/solution.py
@@ -170,7 +170,7 @@
             pltpu.VMEM((4, 2 * TILE, 2 * TILE), BF16),
             pltpu.VMEM((2 * TILE, 2 * TILE), BF16),
         ],
-        compiler_params=pltpu.CompilerParams(vmem_limit_bytes=40 * 2**20),
+        compiler_params=pltpu.CompilerParams(vmem_limit_bytes=60 * 2**20),
         cost_estimate=pl.CostEstimate(flops=4 * 10**9, bytes_accessed=10**7, transcendentals=0),
     )(*scalars, *envs, *kets)
 
@@ -347,6 +347,13 @@
     return lax.ppermute(blocks, axis, pairs)
 
 
+def fetch_next(sector, blocks, above):
+    blocks, above = lax.optimization_barrier((blocks, above))
+    given = jnp.where(sector[0] % ND == 0, above, blocks)
+    pairs = [(i, i // ND * ND + (i - 1) % ND) for i in range(NSEC)]
+    return lax.ppermute(given, "block", pairs)
+
+
 def flat_rule(rule):
     return jnp.pad(rule.reshape(RULE), (0, PADDED - RULE))
 
@@ -377,13 +384,18 @@
     near = [tensors, near1, near2, near3, near4]
     rights = {(0, 0): right}
     rights[1, 0] = fetch(right, ND)
-    rights[0, 1] = fetch(right, 1)
-    rights[0, 2] = fetch(rights[0, 1], 1)
     rights[2, 0] = fetch(rights[1, 0], ND)
-    for up in (1, 2):
-        for down in (1, 2):
-            rights[up, down] = fetch(rights[up, down - 1], 1)
-    kets = [pairs] + [fetch(pairs, CLASS_STEPS[n]) for n in range(1, 5)]
+    rights[0, 1] = fetch_next(sector, right, rights[1, 0])
+    rights[1, 1] = fetch_next(sector, rights[1, 0], rights[2, 0])
+    rights[2, 1] = fetch(rights[2, 0], 1)
+    rights[0, 2] = fetch_next(sector, rights[0, 1], rights[1, 1])
+    rights[1, 2] = fetch_next(sector, rights[1, 1], rights[2, 1])
+    rights[2, 2] = fetch(rights[2, 1], 1)
+    pairs2 = fetch(pairs, -1)
+    pairs3 = fetch(pairs, ND)
+    pairs4 = fetch(pairs, -ND)
+    pairs1 = fetch_next(sector, pairs, pairs3)
+    kets = [pairs, pairs1, pairs2, pairs3, pairs4]
 
     tables = mix_tables(channel_class)
     scalars = (sector, channel_class, live, *tables)

time: 291 us -> 282 us (0.969)
  starting transfers between devices: 86.6 us -> 60.2 us
  waiting for transfers between devices: 85.9 us -> 99 us
  local copies, waits for them, and re-layouts: 23 us -> 13.9 us
  other arithmetic: 8.93 us -> 16.6 us
  Pallas kernels: 82.7 us -> 88.8 us
    ppermute x25 -> x20, starting transfers between devices: 86.6 us -> 57.2 us  [fetch(): return lax.ppermute(blocks, axis, pairs)]
    ppermute x25 -> x20, waiting for transfers between devices: 85.9 us -> 99 us  [fetch(): return lax.ppermute(blocks, axis, pairs)]
    unnamed x54 -> x32, local copies, waits for them, and re-layouts: 10.2 us -> 1.07 us
    select_n x0 -> x5, other arithmetic: none -> 6.14 us  [fetch_next(): given = jnp.where(sector[0] % ND == 0, above, blocks)]
    pallas_call x2, Pallas kernels: 20.2 us -> 26.3 us  [site(): pl.pallas_call(functools.partial(site_kernel, number), grid=(1,), out_sha...]
    ppermute x0 -> x5, starting transfers between devices: none -> 3.08 us  [fetch_next(): return lax.ppermute(given, 'block', pairs)]
  transfers between devices with their start and end apart: 25 -> 25, of which waited for: 9 -> 10; matrix products, arithmetic and copies ran while one was open for 8% -> 10% of each run, Pallas kernels for 6% -> 12%
where the time goes in v2:
time: 282 us; the launch traced here: 280 us
  waiting for transfers between devices  99 us (35%)
  Pallas kernels  88.8 us (31%)
  starting transfers between devices  60.2 us (21%)
  other arithmetic  16.6 us (6%)
  local copies, waits for them, and re-layouts  13.9 us (5%)
    ppermute x20, waiting for transfers between devices, fetch(): return lax.ppermute(blocks, axis, pairs)  99 us
    ppermute x20, starting transfers between devices, fetch(): return lax.ppermute(blocks, axis, pairs)  57.2 us
    pallas_call x1, Pallas kernels, pair(): pl.pallas_call(pair_kernel, out_shape=jax.ShapeDtypeStruct((16, TILE, TIL...  54 us
    pallas_call x2, Pallas kernels, site(): pl.pallas_call(functools.partial(site_kernel, number), grid=(1,), out_sha...  26.3 us
    select_n x5, other arithmetic, fetch_next(): given = jnp.where(sector[0] % ND == 0, above, blocks)  6.14 us
    pallas_call x1, Pallas kernels, split_kets(): pl.pallas_call(kets_kernel, grid=(4,), out_shape=jax.ShapeDtypeStruct((4,...  5.88 us
  transfers between devices with their start and end apart: 25, of which 10 were waited for; matrix products, arithmetic and copies ran while one was open for 10% of the time, Pallas kernels for 12%

profile of v2, /device:TPU:32, one launch (start us, length us, event | category | flops | bytes accessed | tf_op | source)
XLA Modules:
  0.0 280.4 jit_solution(10066231185555041119)
XLA Ops:
  0.6 3.9 %collective-permute-start = (f32[2,4,128,128]{3,2,1,0:T(8,128)}, f32[2,4,128,128]{3,2,1,0:T(8,128)S(1)}, u32[]{:S(2)}, u32[]{:S(2)}) collective-permute-start(f32[2,4,128,128]{3,2,1,0:T(8,128)} %bitcast.37), channel_id=1, source_target_pairs={{1,0},{2,1},{3,2},{4,3},{5,4},{6,5},{7,6},{8,7},{9,8},{10,9},{11,1... | collective-permute-start | bytes 1572872 | tf_op jit(solution)/shard_map/ppermute | solution.py:347
  4.5 1.9 collective-permute-start.1
  6.5 1.9 collective-permute-start.2
  8.4 3.9 %collective-permute-start.3 = (f32[2,4,128,128]{3,2,1,0:T(8,128)}, f32[2,4,128,128]{3,2,1,0:T(8,128)}, u32[]{:S(2)}, u32[]{:S(2)}) collective-permute-start(f32[2,4,128,128]{3,2,1,0:T(8,128)} %bitcast.40), channel_id=1, source_target_pairs={{0,8},{1,9},{2,10},{3,11},{4,12},{5,13},{6,14},{7,15},{8,16},{9,17... | collective-permute-start | bytes 1572872 | tf_op jit(solution)/shard_map/ppermute | solution.py:347
  12.3 2.7 collective-permute-start.17
  17.2 0.7 broadcast_add_fusion
  18.0 0.7 broadcast_add_fusion.2
  19.8 1.0 fusion.12
  21.2 0.7 reduce
  26.4 2.3 collective-permute-done.3.refs_5_.refs_7_
  28.7 13.3 %shard_map.122 = (f32[17,128,128]{2,1,0:T(8,128)}, f32[17,128,128]{2,1,0:T(8,128)}, f32[17,128,128]{2,1,0:T(8,128)}, f32[17,128,128]{2,1,0:T(8,128)}) custom-call(s32[1]{0:T(128)} %bitcast.2.sector_ref, s32[17]{0:T(128)} %class_ref.5, s32[96]{0:T(128)} %reshape.406.live_ref, s32[68]{0:T(128)} %reshape.407.out_ref, s32[220]{0:T(256)} %reshape.408.block_ref, ...), custom_call_target="tpu_custom_call" | custom-call | flops 4000000000 | bytes 10000000 | tf_op jit(solution)/shard_map/pallas_call | solution.py:161
  42.1 2.0 collective-permute-start.5
  44.1 2.1 collective-permute-done.17.refs_3_
  46.2 2.0 collective-permute-start.19
  48.2 1.9 collective-permute-start.4
  50.1 11.1 %collective-permute-done.5 = f32[17,128,128]{2,1,0:T(8,128)S(1)} collective-permute-done((f32[17,128,128]{2,1,0:T(8,128)}, f32[17,128,128]{2,1,0:T(8,128)S(1)}, u32[]{:S(2)}, u32[]{:S(2)}) %collective-permute-start.5) | collective-permute-done | bytes 1114144 | tf_op jit(solution)/shard_map/ppermute | solution.py:347
  61.2 2.5 add.160
  63.7 3.8 %collective-permute-start.6 = (f32[17,128,128]{2,1,0:T(8,128)}, f32[17,128,128]{2,1,0:T(8,128)}, u32[]{:S(2)}, u32[]{:S(2)}) collective-permute-start(f32[17,128,128]{2,1,0:T(8,128)} %add.160), channel_id=1, source_target_pairs={{0,8},{1,9},{2,10},{3,11},{4,12},{5,13},{6,14},{7,15},{8,16},{9,17... | collective-permute-start | bytes 3342344 | tf_op jit(solution)/shard_map/ppermute | solution.py:347
  67.5 3.0 %collective-permute-start.13 = (f32[16,128,128]{2,1,0:T(8,128)S(1)}, f32[16,128,128]{2,1,0:T(8,128)S(1)}, u32[]{:S(2)}, u32[]{:S(2)}) collective-permute-start(f32[16,128,128]{2,1,0:T(8,128)S(1)} %bitcast.23), channel_id=1, source_target_pairs={{8,0},{9,1},{10,2},{11,3},{12,4},{13,5},{14,6},{15,7},{16,8},{17,9... | collective-permute-start | bytes 3145736 | tf_op jit(solution)/shard_map/ppermute | solution.py:347
  70.5 1.3 copy.37
  71.8 1.6 reshape_squeeze.15
  74.0 1.1 broadcast_select_fusion.3
  75.7 2.4 broadcast_select_fusion.2
  78.1 2.5 collective-permute-start.20
  80.6 0.7 fusion.10
  81.3 3.2 %collective-permute-start.22 = (f32[17,128,128]{2,1,0:T(8,128)}, f32[17,128,128]{2,1,0:T(8,128)}, u32[]{:S(2)}, u32[]{:S(2)}) collective-permute-start(f32[17,128,128]{2,1,0:T(8,128)} %collective-permute-done.19.refs_6_), channel_id=1, source_target_pairs={{1,0},{2,1},{3,2},{4,3},{5,4},{6,5},{7,6},{8,7},{9,8},{10,9},{11,1... | collective-permute-start | bytes 3342344 | tf_op jit(solution)/shard_map/ppermute | solution.py:347
  84.5 12.6 %collective-permute-done.6.refs_2_ = f32[17,128,128]{2,1,0:T(8,128)} collective-permute-done((f32[17,128,128]{2,1,0:T(8,128)}, f32[17,128,128]{2,1,0:T(8,128)}, u32[]{:S(2)}, u32[]{:S(2)}) %collective-permute-start.6) | collective-permute-done | bytes 1114144 | tf_op jit(solution)/shard_map/ppermute | solution.py:347
  97.1 12.9 %shard_map.123 = (f32[17,128,128]{2,1,0:T(8,128)}, f32[17,128,128]{2,1,0:T(8,128)}, f32[17,128,128]{2,1,0:T(8,128)}, f32[17,128,128]{2,1,0:T(8,128)}, f32[17,128,128]{2,1,0:T(8,128)}) custom-call(s32[1]{0:T(128)} %bitcast.2.sector_ref, s32[17]{0:T(128)} %class_ref.5, s32[96]{0:T(128)} %reshape.406.live_ref, s32[68]{0:T(128)} %reshape.407.out_ref, ...), custom_call_target="tpu_custom_call" | custom-call | flops 4000000000 | bytes 10000000 | tf_op jit(solution)/shard_map/pallas_call | solution.py:161
  110.0 1.9 collective-permute-start.8
  113.5 1.9 collective-permute-start.15
  115.5 3.8 %collective-permute-start.16 = (f32[16,128,128]{2,1,0:T(8,128)S(1)}, f32[16,128,128]{2,1,0:T(8,128)S(1)}, u32[]{:S(2)}, u32[]{:S(2)}) collective-permute-start(f32[16,128,128]{2,1,0:T(8,128)S(1)} %bitcast.25), channel_id=1, source_target_pairs={{0,8},{1,9},{2,10},{3,11},{4,12},{5,13},{6,14},{7,15},{8,16},{9,17... | collective-permute-start | bytes 3145736 | tf_op jit(solution)/shard_map/ppermute | solution.py:347
  119.4 1.9 collective-permute-start.7
  121.9 7.4 %collective-permute-done.8 = f32[17,128,128]{2,1,0:T(8,128)S(1)} collective-permute-done((f32[17,128,128]{2,1,0:T(8,128)}, f32[17,128,128]{2,1,0:T(8,128)S(1)}, u32[]{:S(2)}, u32[]{:S(2)}) %collective-permute-start.8) | collective-permute-done | bytes 1114144 | tf_op jit(solution)/shard_map/ppermute | solution.py:347
  129.5 3.8 %collective-permute-start.9 = (f32[9,128,128]{2,1,0:T(8,128)S(1)}, f32[9,128,128]{2,1,0:T(8,128)S(1)}, u32[]{:S(2)}, u32[]{:S(2)}) collective-permute-start(f32[9,128,128]{2,1,0:T(8,128)S(1)} %slice.63), channel_id=1, source_target_pairs={{0,8},{1,9},{2,10},{3,11},{4,12},{5,13},{6,14},{7,15},{8,16},{9,17... | collective-permute-start | bytes 1769480 | tf_op jit(solution)/shard_map/ppermute | solution.py:347
  133.5 7.0 %collective-permute-done.15 = f32[16,128,128]{2,1,0:T(8,128)S(1)} collective-permute-done((f32[16,128,128]{2,1,0:T(8,128)S(1)}, f32[16,128,128]{2,1,0:T(8,128)S(1)}, u32[]{:S(2)}, u32[]{:S(2)}) %collective-permute-start.15) | collective-permute-done | bytes 1048608 | tf_op jit(solution)/shard_map/ppermute | solution.py:347
  140.5 3.8 %collective-permute-start.10 = (f32[8,128,128]{2,1,0:T(8,128)S(1)}, f32[8,128,128]{2,1,0:T(8,128)S(1)}, u32[]{:S(2)}, u32[]{:S(2)}) collective-permute-start(f32[8,128,128]{2,1,0:T(8,128)S(1)} %slice.66), channel_id=1, source_target_pairs={{0,8},{1,9},{2,10},{3,11},{4,12},{5,13},{6,14},{7,15},{8,16},{9,17... | collective-permute-start | bytes 1572872 | tf_op jit(solution)/shard_map/ppermute | solution.py:347
  144.3 2.4 broadcast_select_fusion
  146.8 28.2 %collective-permute-done.16 = f32[16,128,128]{2,1,0:T(8,128)S(1)} collective-permute-done((f32[16,128,128]{2,1,0:T(8,128)S(1)}, f32[16,128,128]{2,1,0:T(8,128)S(1)}, u32[]{:S(2)}, u32[]{:S(2)}) %collective-permute-start.16) | collective-permute-done | bytes 1048608 | tf_op jit(solution)/shard_map/ppermute | solution.py:347
  174.9 12.6 %collective-permute-done.9 = f32[9,128,128]{2,1,0:T(8,128)S(1)} collective-permute-done((f32[9,128,128]{2,1,0:T(8,128)S(1)}, f32[9,128,128]{2,1,0:T(8,128)S(1)}, u32[]{:S(2)}, u32[]{:S(2)}) %collective-permute-start.9) | collective-permute-done | bytes 589856 | tf_op jit(solution)/shard_map/ppermute | solution.py:347
  187.5 1.9 collective-permute-start.24
  189.7 9.0 %collective-permute-done.10 = f32[8,128,128]{2,1,0:T(8,128)S(1)} collective-permute-done((f32[8,128,128]{2,1,0:T(8,128)S(1)}, f32[8,128,128]{2,1,0:T(8,128)S(1)}, u32[]{:S(2)}, u32[]{:S(2)}) %collective-permute-start.10) | collective-permute-done | bytes 524320 | tf_op jit(solution)/shard_map/ppermute | solution.py:347
  198.7 4.3 %collective-permute-start.11 = (f32[9,128,128]{2,1,0:T(8,128)S(1)}, f32[9,128,128]{2,1,0:T(8,128)}, u32[]{:S(2)}, u32[]{:S(2)}) collective-permute-start(f32[9,128,128]{2,1,0:T(8,128)S(1)} %fusion.2.e0), channel_id=1, source_target_pairs={{0,32},{32,64},{64,96},{1,33},{33,65},{65,97},{2,34},{34,66},{66,9... | collective-permute-start | bytes 1769480 | tf_op jit(solution)/shard_map/ppermute | solution.py:347
  203.2 1.0 copy-done.11
  204.2 3.4 %collective-permute-start.12 = (f32[8,128,128]{2,1,0:T(8,128)S(1)}, f32[8,128,128]{2,1,0:T(8,128)}, u32[]{:S(2)}, u32[]{:S(2)}) collective-permute-start(f32[8,128,128]{2,1,0:T(8,128)S(1)} %fusion.5.e1), channel_id=1, source_target_pairs={{0,32},{32,64},{64,96},{1,33},{33,65},{65,97},{2,34},{34,66},{66,9... | collective-permute-start | bytes 1572872 | tf_op jit(solution)/shard_map/ppermute | solution.py:347
  211.0 5.9 %split_kets.1.kets_hbm = bf16[4,5,512,256]{3,2,1,0:T(8,128)(2,1)} custom-call(s32[1]{0:T(128)} %bitcast.2.sector_ref, f32[4,4,128,128]{3,2,1,0:T(8,128)} %bitcast.22, f32[4,4,128,128]{3,2,1,0:T(8,128)} %bitcast.34, f32[4,4,128,128]{3,2,1,0:T(8,128)} %bitcast.32, f32[4,4,128,128]{3,2,1,0:T(8,128)} %bitcast.27, f32[4,4,128,128]{3,2,1,0:T(8,128)} %bitcast.33), custom_call_target="tpu_custom_call" | custom-call | flops 5000000 | bytes 10000000 | tf_op jit(solution)/shard_map/split_kets/pallas_call | solution.py:190
  216.9 2.6 turn.1
  219.5 6.7 %collective-permute-done.12.passed1_ref = f32[8,128,128]{2,1,0:T(8,128)} collective-permute-done((f32[8,128,128]{2,1,0:T(8,128)S(1)}, f32[8,128,128]{2,1,0:T(8,128)}, u32[]{:S(2)}, u32[]{:S(2)}) %collective-permute-start.12) | collective-permute-done | bytes 524320 | tf_op jit(solution)/shard_map/ppermute | solution.py:347
  226.2 54.0 %pair.1 = f32[16,128,128]{2,1,0:T(8,128)} custom-call(s32[1]{0:T(128)} %bitcast.2.sector_ref, s32[1]{0:T(128)} %bitcast.7.region_ref, s32[17]{0:T(128)} %class_ref.5, s32[96]{0:T(128)} %reshape.406.live_ref, s32[68]{0:T(128)} %reshape.407.out_ref, s32[220]{0:T(256)} %reshape.408.block_ref, s32[220]{0:T(256)} %add.159.place_ref, f32[4896]{0:T(1024)} %pad.15.left_ref, ...), custom_call_target="tpu_custom_call" | custom-call | flops 20000000000 | bytes 18000000 | tf_op jit(solution)/shard_map/pair/pallas_call | solution.py:305
  (97 shorter events, 14.9 us)
Async XLA Ops:
  0.6 25.7 %collective-permute-start = (f32[2,4,128,128]{3,2,1,0:T(8,128)}, f32[2,4,128,128]{3,2,1,0:T(8,128)S(1)}, u32[]{:S(2)}, u32[]{:S(2)}) collective-permute-start(f32[2,4,128,128]{3,2,1,0:T(8,128)} %bitcast.37), channel_id=1, source_target_pairs={{1,0},{2,1},{3,2},{4,3},{5,4},{6,5},{7,6},{8,7},{9,8},{10,9},{11,1... | collective-permute-start | bytes 1572872 | tf_op jit(solution)/shard_map/ppermute | solution.py:347
  4.5 21.8 %collective-permute-start.1 = (f32[2,4,128,128]{3,2,1,0:T(8,128)}, f32[2,4,128,128]{3,2,1,0:T(8,128)S(1)}, u32[]{:S(2)}, u32[]{:S(2)}) collective-permute-start(f32[2,4,128,128]{3,2,1,0:T(8,128)} %bitcast.38), channel_id=1, source_target_pairs={{0,1},{1,2},{2,3},{3,4},{4,5},{5,6},{6,7},{7,8},{8,9},{9,10},{10,1... | collective-permute-start | bytes 1572872 | tf_op jit(solution)/shard_map/ppermute | solution.py:347
  6.5 19.9 %collective-permute-start.2 = (f32[2,4,128,128]{3,2,1,0:T(8,128)}, f32[2,4,128,128]{3,2,1,0:T(8,128)}, u32[]{:S(2)}, u32[]{:S(2)}) collective-permute-start(f32[2,4,128,128]{3,2,1,0:T(8,128)} %bitcast.39), channel_id=1, source_target_pairs={{8,0},{9,1},{10,2},{11,3},{12,4},{13,5},{14,6},{15,7},{16,8},{17,9... | collective-permute-start | bytes 1572872 | tf_op jit(solution)/shard_map/ppermute | solution.py:347
  8.4 20.3 %collective-permute-start.3 = (f32[2,4,128,128]{3,2,1,0:T(8,128)}, f32[2,4,128,128]{3,2,1,0:T(8,128)}, u32[]{:S(2)}, u32[]{:S(2)}) collective-permute-start(f32[2,4,128,128]{3,2,1,0:T(8,128)} %bitcast.40), channel_id=1, source_target_pairs={{0,8},{1,9},{2,10},{3,11},{4,12},{5,13},{6,14},{7,15},{8,16},{9,17... | collective-permute-start | bytes 1572872 | tf_op jit(solution)/shard_map/ppermute | solution.py:347
  12.3 33.8 %collective-permute-start.17 = (f32[17,128,128]{2,1,0:T(8,128)}, f32[17,128,128]{2,1,0:T(8,128)S(1)}, u32[]{:S(2)}, u32[]{:S(2)}) collective-permute-start(f32[17,128,128]{2,1,0:T(8,128)} %bitcast.29), channel_id=1, source_target_pairs={{8,0},{9,1},{10,2},{11,3},{12,4},{13,5},{14,6},{15,7},{16,8},{17,9... | collective-permute-start | bytes 3342344 | tf_op jit(solution)/shard_map/ppermute | solution.py:347
  26.4 2.3 copy-start.14
  26.4 2.3 copy-start.15
  42.1 19.1 %collective-permute-start.5 = (f32[17,128,128]{2,1,0:T(8,128)}, f32[17,128,128]{2,1,0:T(8,128)S(1)}, u32[]{:S(2)}, u32[]{:S(2)}) collective-permute-start(f32[17,128,128]{2,1,0:T(8,128)} %get-tuple-element.24), channel_id=1, source_target_pairs={{0,1},{1,2},{2,3},{3,4},{4,5},{5,6},{6,7},{7,8},{8,9},{9,10},{10,1... | collective-permute-start | bytes 3342344 | tf_op jit(solution)/shard_map/ppermute | solution.py:347
  46.2 29.5 %copy-start = (f32[17,128,128]{2,1,0:T(8,128)}, f32[17,128,128]{2,1,0:T(8,128)S(1)}, u32[]{:S(2)}) copy-start(f32[17,128,128]{2,1,0:T(8,128)S(1)} %collective-permute-done.17.refs_3_) | copy-start | bytes 3342340
  46.2 29.5 %collective-permute-start.19 = (f32[17,128,128]{2,1,0:T(8,128)S(1)}, f32[17,128,128]{2,1,0:T(8,128)}, u32[]{:S(2)}, u32[]{:S(2)}) collective-permute-start(f32[17,128,128]{2,1,0:T(8,128)S(1)} %collective-permute-done.17.refs_3_), channel_id=1, source_target_pairs={{8,0},{9,1},{10,2},{11,3},{12,4},{13,5},{14,6},{15,7},{16,8},{17,9... | collective-permute-start | bytes 3342344 | tf_op jit(solution)/shard_map/ppermute | solution.py:347
  48.2 33.1 %collective-permute-start.4 = (f32[17,128,128]{2,1,0:T(8,128)}, f32[17,128,128]{2,1,0:T(8,128)}, u32[]{:S(2)}, u32[]{:S(2)}) collective-permute-start(f32[17,128,128]{2,1,0:T(8,128)} %get-tuple-element.22), channel_id=1, source_target_pairs={{0,1},{1,2},{2,3},{3,4},{4,5},{5,6},{6,7},{7,8},{8,9},{9,10},{10,1... | collective-permute-start | bytes 3342344 | tf_op jit(solution)/shard_map/ppermute | solution.py:347
  61.2 6.3 %copy-start.2 = (f32[1,16,1,128,128]{4,3,2,1,0:T(8,128)S(1)}, f32[1,16,1,128,128]{4,3,2,1,0:T(8,128)}, u32[]{:S(2)}) copy-start(f32[1,16,1,128,128]{4,3,2,1,0:T(8,128)} %param.14) | copy-start | bytes 3145732
  63.7 33.4 %collective-permute-start.6 = (f32[17,128,128]{2,1,0:T(8,128)}, f32[17,128,128]{2,1,0:T(8,128)}, u32[]{:S(2)}, u32[]{:S(2)}) collective-permute-start(f32[17,128,128]{2,1,0:T(8,128)} %add.160), channel_id=1, source_target_pairs={{0,8},{1,9},{2,10},{3,11},{4,12},{5,13},{6,14},{7,15},{8,16},{9,17... | collective-permute-start | bytes 3342344 | tf_op jit(solution)/shard_map/ppermute | solution.py:347
  67.5 46.0 %collective-permute-start.13 = (f32[16,128,128]{2,1,0:T(8,128)S(1)}, f32[16,128,128]{2,1,0:T(8,128)S(1)}, u32[]{:S(2)}, u32[]{:S(2)}) collective-permute-start(f32[16,128,128]{2,1,0:T(8,128)S(1)} %bitcast.23), channel_id=1, source_target_pairs={{8,0},{9,1},{10,2},{11,3},{12,4},{13,5},{14,6},{15,7},{16,8},{17,9... | collective-permute-start | bytes 3145736 | tf_op jit(solution)/shard_map/ppermute | solution.py:347
  75.2 5.4 %copy-start.13 = (s32[1,3,32]{2,0,1:T(1,128)S(1)}, s32[1,3,32]{2,0,1:T(1,128)}, u32[]{:S(2)}) copy-start(s32[1,3,32]{2,0,1:T(1,128)} %param.18) | copy-start | bytes 1156
  75.2 40.3 %collective-permute-start.18 = (f32[17,128,128]{2,1,0:T(8,128)}, f32[17,128,128]{2,1,0:T(8,128)}, u32[]{:S(2)}, u32[]{:S(2)}) collective-permute-start(f32[17,128,128]{2,1,0:T(8,128)} %broadcast_select_fusion.3), channel_id=1, source_target_pairs={{0,7},{1,0},{2,1},{3,2},{4,3},{5,4},{6,5},{7,6},{8,15},{9,8},{10,9... | collective-permute-start | bytes 3342344 | tf_op jit(solution)/shard_map/ppermute | solution.py:354
  78.1 41.3 %collective-permute-start.20 = (f32[17,128,128]{2,1,0:T(8,128)}, f32[17,128,128]{2,1,0:T(8,128)S(1)}, u32[]{:S(2)}, u32[]{:S(2)}) collective-permute-start(f32[17,128,128]{2,1,0:T(8,128)} %broadcast_select_fusion.2), channel_id=1, source_target_pairs={{0,7},{1,0},{2,1},{3,2},{4,3},{5,4},{6,5},{7,6},{8,15},{9,8},{10,9... | collective-permute-start | bytes 3342344 | tf_op jit(solution)/shard_map/ppermute | solution.py:354
  81.3 48.2 %collective-permute-start.22 = (f32[17,128,128]{2,1,0:T(8,128)}, f32[17,128,128]{2,1,0:T(8,128)}, u32[]{:S(2)}, u32[]{:S(2)}) collective-permute-start(f32[17,128,128]{2,1,0:T(8,128)} %collective-permute-done.19.refs_6_), channel_id=1, source_target_pairs={{1,0},{2,1},{3,2},{4,3},{5,4},{6,5},{7,6},{8,7},{9,8},{10,9},{11,1... | collective-permute-start | bytes 3342344 | tf_op jit(solution)/shard_map/ppermute | solution.py:347
  110.0 19.2 %collective-permute-start.8 = (f32[17,128,128]{2,1,0:T(8,128)}, f32[17,128,128]{2,1,0:T(8,128)S(1)}, u32[]{:S(2)}, u32[]{:S(2)}) collective-permute-start(f32[17,128,128]{2,1,0:T(8,128)} %get-tuple-element.28), channel_id=1, source_target_pairs={{0,1},{1,2},{2,3},{3,4},{4,5},{5,6},{6,7},{7,8},{8,9},{9,10},{10,1... | collective-permute-start | bytes 3342344 | tf_op jit(solution)/shard_map/ppermute | solution.py:347
  113.5 8.4 %copy-start.3 = (f32[16,128,128]{2,1,0:T(8,128)}, f32[16,128,128]{2,1,0:T(8,128)S(1)}, u32[]{:S(2)}) copy-start(f32[16,128,128]{2,1,0:T(8,128)S(1)} %collective-permute-done.13) | copy-start | bytes 3145732
  113.5 27.0 %collective-permute-start.15 = (f32[16,128,128]{2,1,0:T(8,128)S(1)}, f32[16,128,128]{2,1,0:T(8,128)S(1)}, u32[]{:S(2)}, u32[]{:S(2)}) collective-permute-start(f32[16,128,128]{2,1,0:T(8,128)S(1)} %bitcast.24), channel_id=1, source_target_pairs={{0,1},{1,2},{2,3},{3,4},{4,5},{5,6},{6,7},{7,8},{8,9},{9,10},{10,1... | collective-permute-start | bytes 3145736 | tf_op jit(solution)/shard_map/ppermute | solution.py:347
  115.5 59.4 %collective-permute-start.16 = (f32[16,128,128]{2,1,0:T(8,128)S(1)}, f32[16,128,128]{2,1,0:T(8,128)S(1)}, u32[]{:S(2)}, u32[]{:S(2)}) collective-permute-start(f32[16,128,128]{2,1,0:T(8,128)S(1)} %bitcast.25), channel_id=1, source_target_pairs={{0,8},{1,9},{2,10},{3,11},{4,12},{5,13},{6,14},{7,15},{8,16},{9,17... | collective-permute-start | bytes 3145736 | tf_op jit(solution)/shard_map/ppermute | solution.py:347
  119.4 25.0 %copy-start.1 = (f32[17,128,128]{2,1,0:T(8,128)}, f32[17,128,128]{2,1,0:T(8,128)S(1)}, u32[]{:S(2)}) copy-start(f32[17,128,128]{2,1,0:T(8,128)S(1)} %collective-permute-done.20.refs_4_) | copy-start | bytes 3342340
  119.4 55.6 %collective-permute-start.7 = (f32[17,128,128]{2,1,0:T(8,128)}, f32[17,128,128]{2,1,0:T(8,128)S(1)}, u32[]{:S(2)}, u32[]{:S(2)}) collective-permute-start(f32[17,128,128]{2,1,0:T(8,128)} %get-tuple-element.26), channel_id=1, source_target_pairs={{0,1},{1,2},{2,3},{3,4},{4,5},{5,6},{6,7},{7,8},{8,9},{9,10},{10,1... | collective-permute-start | bytes 3342344 | tf_op jit(solution)/shard_map/ppermute | solution.py:347
  121.8 7.5 %copy-start.8 = (f32[17,128,128]{2,1,0:T(8,128)S(1)}, f32[17,128,128]{2,1,0:T(8,128)}, u32[]{:S(2)}) copy-start(f32[17,128,128]{2,1,0:T(8,128)} %get-tuple-element.27) | copy-start | bytes 3342340
  129.3 73.9 %collective-permute-start.14 = (f32[16,128,128]{2,1,0:T(8,128)S(1)}, f32[16,128,128]{2,1,0:T(8,128)S(1)}, u32[]{:S(2)}, u32[]{:S(2)}) collective-permute-start(f32[16,128,128]{2,1,0:T(8,128)S(1)} %broadcast_select_fusion.4), channel_id=1, source_target_pairs={{0,7},{1,0},{2,1},{3,2},{4,3},{5,4},{6,5},{7,6},{8,15},{9,8},{10,9... | collective-permute-start | bytes 3145736 | tf_op jit(solution)/shard_map/ppermute | solution.py:354
  129.5 58.1 %collective-permute-start.9 = (f32[9,128,128]{2,1,0:T(8,128)S(1)}, f32[9,128,128]{2,1,0:T(8,128)S(1)}, u32[]{:S(2)}, u32[]{:S(2)}) collective-permute-start(f32[9,128,128]{2,1,0:T(8,128)S(1)} %slice.63), channel_id=1, source_target_pairs={{0,8},{1,9},{2,10},{3,11},{4,12},{5,13},{6,14},{7,15},{8,16},{9,17... | collective-permute-start | bytes 1769480 | tf_op jit(solution)/shard_map/ppermute | solution.py:347
  133.5 56.0 %copy-start.6 = (f32[17,128,128]{2,1,0:T(8,128)S(1)}, f32[17,128,128]{2,1,0:T(8,128)}, u32[]{:S(2)}) copy-start(f32[17,128,128]{2,1,0:T(8,128)} %get-tuple-element.25) | copy-start | bytes 3342340
  133.5 56.0 %copy-start.7 = (f32[17,128,128]{2,1,0:T(8,128)S(1)}, f32[17,128,128]{2,1,0:T(8,128)}, u32[]{:S(2)}) copy-start(f32[17,128,128]{2,1,0:T(8,128)} %get-tuple-element.29) | copy-start | bytes 3342340
  140.5 6.2 %copy-start.9 = (f32[16,128,128]{2,1,0:T(8,128)}, f32[16,128,128]{2,1,0:T(8,128)S(1)}, u32[]{:S(2)}) copy-start(f32[16,128,128]{2,1,0:T(8,128)S(1)} %collective-permute-done.15) | copy-start | bytes 3145732
  140.5 58.2 %collective-permute-start.10 = (f32[8,128,128]{2,1,0:T(8,128)S(1)}, f32[8,128,128]{2,1,0:T(8,128)S(1)}, u32[]{:S(2)}, u32[]{:S(2)}) collective-permute-start(f32[8,128,128]{2,1,0:T(8,128)S(1)} %slice.66), channel_id=1, source_target_pairs={{0,8},{1,9},{2,10},{3,11},{4,12},{5,13},{6,14},{7,15},{8,16},{9,17... | collective-permute-start | bytes 1572872 | tf_op jit(solution)/shard_map/ppermute | solution.py:347
  174.9 14.7 %copy-start.10 = (f32[16,128,128]{2,1,0:T(8,128)}, f32[16,128,128]{2,1,0:T(8,128)S(1)}, u32[]{:S(2)}) copy-start(f32[16,128,128]{2,1,0:T(8,128)S(1)} %collective-permute-done.16) | copy-start | bytes 3145732
  174.9 44.5 %collective-permute-start.21 = (f32[17,128,128]{2,1,0:T(8,128)S(1)}, f32[17,128,128]{2,1,0:T(8,128)}, u32[]{:S(2)}, u32[]{:S(2)}) collective-permute-start(f32[17,128,128]{2,1,0:T(8,128)S(1)} %broadcast_select_fusion.1), channel_id=1, source_target_pairs={{0,7},{1,0},{2,1},{3,2},{4,3},{5,4},{6,5},{7,6},{8,15},{9,8},{10,9... | collective-permute-start | bytes 3342344 | tf_op jit(solution)/shard_map/ppermute | solution.py:354
  174.9 44.5 %collective-permute-start.23 = (f32[17,128,128]{2,1,0:T(8,128)}, f32[17,128,128]{2,1,0:T(8,128)}, u32[]{:S(2)}, u32[]{:S(2)}) collective-permute-start(f32[17,128,128]{2,1,0:T(8,128)} %broadcast_select_fusion), channel_id=1, source_target_pairs={{0,7},{1,0},{2,1},{3,2},{4,3},{5,4},{6,5},{7,6},{8,15},{9,8},{10,9... | collective-permute-start | bytes 3342344 | tf_op jit(solution)/shard_map/ppermute | solution.py:354
  187.5 31.9 %collective-permute-start.24 = (f32[17,128,128]{2,1,0:T(8,128)}, f32[17,128,128]{2,1,0:T(8,128)}, u32[]{:S(2)}, u32[]{:S(2)}) collective-permute-start(f32[17,128,128]{2,1,0:T(8,128)} %collective-permute-done.22.refs_7_), channel_id=1, source_target_pairs={{1,0},{2,1},{3,2},{4,3},{5,4},{6,5},{7,6},{8,7},{9,8},{10,9},{11,1... | collective-permute-start | bytes 3342344 | tf_op jit(solution)/shard_map/ppermute | solution.py:347
  189.7 13.5 %copy-start.4 = (f32[9,128,128]{2,1,0:T(8,128)}, f32[9,128,128]{2,1,0:T(8,128)S(1)}, u32[]{:S(2)}) copy-start(f32[9,128,128]{2,1,0:T(8,128)S(1)} %fusion.2.e0) | copy-start | bytes 1769476
  189.7 17.9 %copy-start.12 = (f32[1,2,17,17,4,4]{3,5,4,2,1,0:T(4,128)S(1)}, f32[1,2,17,17,4,4]{3,5,4,2,1,0:T(4,128)}, u32[]{:S(2)}) copy-start(f32[1,2,17,17,4,4]{3,5,4,2,1,0:T(4,128)} %param.16) | copy-start | bytes 110980
  198.7 27.5 %collective-permute-start.11 = (f32[9,128,128]{2,1,0:T(8,128)S(1)}, f32[9,128,128]{2,1,0:T(8,128)}, u32[]{:S(2)}, u32[]{:S(2)}) collective-permute-start(f32[9,128,128]{2,1,0:T(8,128)S(1)} %fusion.2.e0), channel_id=1, source_target_pairs={{0,32},{32,64},{64,96},{1,33},{33,65},{65,97},{2,34},{34,66},{66,9... | collective-permute-start | bytes 1769480 | tf_op jit(solution)/shard_map/ppermute | solution.py:347
  203.2 6.7 %copy-start.5 = (f32[8,128,128]{2,1,0:T(8,128)}, f32[8,128,128]{2,1,0:T(8,128)S(1)}, u32[]{:S(2)}) copy-start(f32[8,128,128]{2,1,0:T(8,128)S(1)} %fusion.5.e1) | copy-start | bytes 1572868
  203.2 1.0 copy-start.11
  204.2 22.0 %collective-permute-start.12 = (f32[8,128,128]{2,1,0:T(8,128)S(1)}, f32[8,128,128]{2,1,0:T(8,128)}, u32[]{:S(2)}, u32[]{:S(2)}) collective-permute-start(f32[8,128,128]{2,1,0:T(8,128)S(1)} %fusion.5.e1), channel_id=1, source_target_pairs={{0,32},{32,64},{64,96},{1,33},{33,65},{65,97},{2,34},{34,66},{66,9... | collective-permute-start | bytes 1572872 | tf_op jit(solution)/shard_map/ppermute | solution.py:347

commit v3 on v2

--- a/solution.py
+++ b/solution.py
@@ -48,7 +48,7 @@
     key = jnp.where(three, 0, NW) + channels[None, :]
     position = (key[:, None, :] < key[:, :, None]).astype(jnp.int32).sum(-1)
     out = jnp.where(position[:, None, :] == channels[:, None], channels, 0).sum(-1)
-    return out.reshape(-1), block.reshape(-1), place.reshape(-1)
+    return out, block, place
 
 
 def class_shift(kind):
@@ -65,11 +65,11 @@
 
 
 def mix(blocks, base, block_ref, place_ref, rule_ref, v, kind, s, terms):
-    first = (4 * kind + s) * LONG
+    row = 4 * kind + s
     shift = 16 * v + 4 * s
     total = None
     for k in range(terms):
-        term = blocks[base + block_ref[first + k]] * rule_ref[place_ref[first + k] + shift]
+        term = blocks[base + block_ref[row, k]] * rule_ref[place_ref[row, k] + shift]
         total = term if total is None else total + term
     return total
 
@@ -122,8 +122,8 @@
         keep = inside(ket)
         if number == 0:
             return (env_ref[w] * keep).T
-        count = jnp.where(keep > 0, live_ref[(number - 1) * NSEC + jnp.clip(ket, 0, NSEC - 1)], 0)
-        own = live_ref[(number - 1) * NSEC + sector]
+        count = jnp.where(keep > 0, live_ref[0, number - 1, jnp.clip(ket, 0, NSEC - 1)], 0)
+        own = live_ref[0, number - 1, sector]
         total = low_ref[w] + below_ref[w] + above_ref[w]
         total = jnp.where((rows < own) & (columns < count), total, 0.0)
         first_ref[w] = total
@@ -138,7 +138,7 @@
     for s in (3, 2, 1, 0):
 
         def close(terms, i):
-            v = out_ref[s * NW + i]
+            v = out_ref[s, i]
             total = mix(product, 0, block_ref, place_ref, rule_ref, v, class_ref[v], s, terms)
             result = folded(dot(jnp.concatenate(split(total), axis=1), bras[s]))
             closed_refs[s][v] = result
@@ -203,7 +203,8 @@
     start_ref, passed0_ref, passed1_ref, kets_hbm, *refs,
 ):
     rights_hbm = refs[:9]
-    image_ref, kets, arrived, rights, envs, even, odd, middle, outer, sems = refs[9:]
+    image_ref, kets, arrived, rights, envs, even, odd, middle, *rest = refs[9:]
+    outer_even, outer_odd, sems = rest
     sector = sector_ref[0]
 
     def kets_copy(t):
@@ -236,7 +237,7 @@
         product[pl.ds(4 * w, 4)] = result.reshape(4, TILE, TILE)
 
     def left(product, t2, s, i):
-        v = out_ref[s * NW + i]
+        v = out_ref[s, i]
         terms = LONG if i < LONG else SHORT
         total = mix(product, 0, block_ref, place_ref, left_ref, v, class_ref[v], s, terms)
         middle[s * 4 * NW + 4 * v + t2] = total
@@ -251,7 +252,8 @@
             keep = inside(sector + ND * ups + downs + class_shift(class_ref[x]))
             rights[n, x] = jnp.concatenate(split(arrived[n % 2, x] * keep), axis=0)
 
-        loop(0, NW, cut, 1)
+        loop(0, NW - 1, cut, 4)
+        cut(NW - 1)
         if n + 2 < 9:
             rights_copy(n + 2).start()
     for t in range(1, 4):
@@ -276,29 +278,43 @@
 
     rows = lax.broadcasted_iota(jnp.int32, (TILE, TILE), 0)
     columns = lax.broadcasted_iota(jnp.int32, (TILE, TILE), 1)
-    own = live_ref[MAXLEN * NSEC + sector]
-
-    def right_half(p):
+    own = live_ref[0, MAXLEN, sector]
+
+    def place_of(p):
         s1 = p // 4
         s2 = p % 4
         ups = s1 % 2 + s2 % 2
         downs = s1 // 2 + s2 // 2
-        far = sector + ND * ups + downs
-        lhs = []
+        return s1, s2, 3 * ups + downs, sector + ND * ups + downs
+
+    def close(outer, p):
+        _, s2, step, far = place_of(p)
+        lhs = [rights[step, out_ref[s2, i]] for i in range(NW)]
+        total = dot(jnp.concatenate(lhs, axis=1), outer[...])
+        total = folded(total[:TILE] + total[TILE:]).T
+        count = jnp.where(far < NSEC, live_ref[0, MAXLEN, jnp.minimum(far, NSEC - 1)], 0)
+        image_ref[p] = jnp.where((rows < own) & (columns < count), total, 0.0)
+
+    def right(outer, p):
+        s1, s2, _, _ = place_of(p)
         for i in range(NW):
-            x = out_ref[s2 * NW + i]
-            lhs.append(rights[3 * ups + downs, x])
+            x = out_ref[s2, i]
             terms = LONG if i < LONG else SHORT
             total = mix(middle, s1 * 4 * NW, block_ref, place_ref, right_ref, x, class_ref[x], s2, terms)
             high, low = split(total)
             outer[i * TILE : (i + 1) * TILE, :TILE] = high
             outer[i * TILE : (i + 1) * TILE, TILE:] = low
-        total = dot(jnp.concatenate(lhs, axis=1), outer[...])
-        total = folded(total[:TILE] + total[TILE:]).T
-        count = jnp.where(far < NSEC, live_ref[MAXLEN * NSEC + jnp.minimum(far, NSEC - 1)], 0)
-        image_ref[p] = jnp.where((rows < own) & (columns < count), total, 0.0)
-
-    loop(0, 16, right_half, 1)
+
+    right(outer_even, 0)
+
+    def right_stages(half):
+        p = 2 * half
+        close(outer_even, p)
+        right(outer_odd, p + 1)
+        close(outer_odd, p + 1)
+        right(outer_even, jnp.minimum(p + 2, 15))
+
+    loop(0, 8, right_stages, 1)
 
 
 def pair(scalars, start, passed, kets, rights):
@@ -315,6 +331,7 @@
             pltpu.VMEM((4 * NW, TILE, TILE), F32),
             pltpu.VMEM((4 * NW, TILE, TILE), F32),
             pltpu.VMEM((16 * NW, TILE, TILE), F32),
+            pltpu.VMEM((NW * TILE, 2 * TILE), BF16),
             pltpu.VMEM((NW * TILE, 2 * TILE), BF16),
             pltpu.SemaphoreType.DMA((6,)),
         ],
@@ -375,7 +392,6 @@
     pairs = pair_state[0, :, 0]
     sector = lax.axis_index("block").astype(jnp.int32).reshape(1)
     region = lax.axis_index("region").astype(jnp.int32).reshape(1)
-    live = live_rows.reshape(-1)
 
     near3 = fetch(tensors, ND)
     near4 = fetch(tensors, -ND)
@@ -398,7 +414,7 @@
     kets = [pairs, pairs1, pairs2, pairs3, pairs4]
 
     tables = mix_tables(channel_class)
-    scalars = (sector, channel_class, live, *tables)
+    scalars = (sector, channel_class, live_rows, *tables)
     h0, h1, h2, h3 = site(0, (*scalars, flat_rule(mpo_sites[0, 0])), [start], near)
     below3 = fetch(h3, -1)
     below2 = fetch(h2, -1)
@@ -425,7 +441,7 @@
 
     environment = turned(parts)
     split = split_kets(sector, kets)
-    scalars = (sector, region, channel_class, live, *tables, flat_rule(mpo_pair[0, 0]), flat_rule(mpo_pair[0, 1]))
+    scalars = (sector, region, channel_class, live_rows, *tables, flat_rule(mpo_pair[0, 0]), flat_rule(mpo_pair[0, 1]))
     images = pair(scalars, start, passed, split, [rights[u, d] for u in range(3) for d in range(3)])
     return environment[None, :, None], images[None, :, None]
 

time: 282 us -> 279 us (0.989)
  Pallas kernels: 88.8 us -> 85.1 us
    pallas_call x1, Pallas kernels: 54 us -> 50.4 us  [pair(): pl.pallas_call(pair_kernel, out_shape=jax.ShapeDtypeStruct((16, TILE, TIL...]
  transfers between devices with their start and end apart: 25 -> 25, of which waited for: 10 -> 10; matrix products, arithmetic and copies ran while one was open for 10% -> 11% of each run, Pallas kernels for 12% -> 13%
where the time goes in v3:
time: 279 us; the launch traced here: 277 us
  waiting for transfers between devices  99.3 us (36%)
  Pallas kernels  85.1 us (31%)
  starting transfers between devices  60.2 us (22%)
  other arithmetic  16.4 us (6%)
  local copies, waits for them, and re-layouts  13.8 us (5%)
    ppermute x20, waiting for transfers between devices, fetch(): return lax.ppermute(blocks, axis, pairs)  99.3 us
    ppermute x20, starting transfers between devices, fetch(): return lax.ppermute(blocks, axis, pairs)  57.1 us
    pallas_call x1, Pallas kernels, pair(): pl.pallas_call(pair_kernel, out_shape=jax.ShapeDtypeStruct((16, TILE, TIL...  50.4 us
    pallas_call x2, Pallas kernels, site(): pl.pallas_call(functools.partial(site_kernel, number), grid=(1,), out_sha...  26.3 us
    select_n x5, other arithmetic, fetch_next(): given = jnp.where(sector[0] % ND == 0, above, blocks)  6.13 us
    pallas_call x1, Pallas kernels, split_kets(): pl.pallas_call(kets_kernel, grid=(4,), out_shape=jax.ShapeDtypeStruct((4,...  5.87 us
  transfers between devices with their start and end apart: 25, of which 10 were waited for; matrix products, arithmetic and copies ran while one was open for 11% of the time, Pallas kernels for 13%

profile of v3, /device:TPU:32, one launch (start us, length us, event | category | flops | bytes accessed | tf_op | source)
XLA Modules:
  0.0 276.7 jit_solution(5730021028666222423)
XLA Ops:
  0.6 3.9 %collective-permute-start = (f32[2,4,128,128]{3,2,1,0:T(8,128)}, f32[2,4,128,128]{3,2,1,0:T(8,128)S(1)}, u32[]{:S(2)}, u32[]{:S(2)}) collective-permute-start(f32[2,4,128,128]{3,2,1,0:T(8,128)} %bitcast.37), channel_id=1, source_target_pairs={{1,0},{2,1},{3,2},{4,3},{5,4},{6,5},{7,6},{8,7},{9,8},{10,9},{11,1... | collective-permute-start | bytes 1572872 | tf_op jit(solution)/shard_map/ppermute | solution.py:364
  4.5 1.9 collective-permute-start.1
  6.5 1.9 collective-permute-start.2
  8.4 3.9 %collective-permute-start.3 = (f32[2,4,128,128]{3,2,1,0:T(8,128)}, f32[2,4,128,128]{3,2,1,0:T(8,128)}, u32[]{:S(2)}, u32[]{:S(2)}) collective-permute-start(f32[2,4,128,128]{3,2,1,0:T(8,128)} %bitcast.40), channel_id=1, source_target_pairs={{0,8},{1,9},{2,10},{3,11},{4,12},{5,13},{6,14},{7,15},{8,16},{9,17... | collective-permute-start | bytes 1572872 | tf_op jit(solution)/shard_map/ppermute | solution.py:364
  12.3 2.7 collective-permute-start.17
  17.2 0.7 broadcast_add_fusion.1
  18.0 0.7 broadcast_add_fusion.2
  20.5 1.0 fusion.12
  21.8 1.3 copy.53.live_ref
  23.8 0.7 copy.55.block_ref
  26.2 2.5 collective-permute-done.3.refs_5_.refs_7_
  28.7 13.4 %shard_map.122 = (f32[17,128,128]{2,1,0:T(8,128)}, f32[17,128,128]{2,1,0:T(8,128)}, f32[17,128,128]{2,1,0:T(8,128)}, f32[17,128,128]{2,1,0:T(8,128)}) custom-call(s32[1]{0:T(128)} %bitcast.2.sector_ref, s32[17]{0:T(128)} %class_ref.5, s32[1,3,32]{2,1,0:T(4,128)} %copy.53.live_ref, s32[4,17]{1,0:T(4,128)} %copy.54.out_ref, s32[20,11]{1,0:T(8,128)} %copy.55.block_ref, ...), custom_call_target="tpu_custom_call" | custom-call | flops 4000000000 | bytes 10000000 | tf_op jit(solution)/shard_map/pallas_call | solution.py:161
  42.1 1.9 collective-permute-start.5
  44.0 2.1 collective-permute-done.17.refs_3_
  46.2 2.0 collective-permute-start.19
  48.2 1.9 collective-permute-start.4
  50.1 11.1 %collective-permute-done.5 = f32[17,128,128]{2,1,0:T(8,128)S(1)} collective-permute-done((f32[17,128,128]{2,1,0:T(8,128)}, f32[17,128,128]{2,1,0:T(8,128)S(1)}, u32[]{:S(2)}, u32[]{:S(2)}) %collective-permute-start.5) | collective-permute-done | bytes 1114144 | tf_op jit(solution)/shard_map/ppermute | solution.py:364
  61.2 2.5 add.155
  63.7 3.8 %collective-permute-start.6 = (f32[17,128,128]{2,1,0:T(8,128)}, f32[17,128,128]{2,1,0:T(8,128)}, u32[]{:S(2)}, u32[]{:S(2)}) collective-permute-start(f32[17,128,128]{2,1,0:T(8,128)} %add.155), channel_id=1, source_target_pairs={{0,8},{1,9},{2,10},{3,11},{4,12},{5,13},{6,14},{7,15},{8,16},{9,17... | collective-permute-start | bytes 3342344 | tf_op jit(solution)/shard_map/ppermute | solution.py:364
  67.6 3.0 %collective-permute-start.13 = (f32[16,128,128]{2,1,0:T(8,128)S(1)}, f32[16,128,128]{2,1,0:T(8,128)S(1)}, u32[]{:S(2)}, u32[]{:S(2)}) collective-permute-start(f32[16,128,128]{2,1,0:T(8,128)S(1)} %bitcast.23), channel_id=1, source_target_pairs={{8,0},{9,1},{10,2},{11,3},{12,4},{13,5},{14,6},{15,7},{16,8},{17,9... | collective-permute-start | bytes 3145736 | tf_op jit(solution)/shard_map/ppermute | solution.py:364
  70.5 1.3 copy.48
  71.9 1.6 reshape_squeeze.15
  74.1 1.1 broadcast_select_fusion.3
  75.7 2.4 broadcast_select_fusion.2
  78.1 2.5 collective-permute-start.20
  81.3 3.2 %collective-permute-start.22 = (f32[17,128,128]{2,1,0:T(8,128)}, f32[17,128,128]{2,1,0:T(8,128)}, u32[]{:S(2)}, u32[]{:S(2)}) collective-permute-start(f32[17,128,128]{2,1,0:T(8,128)} %collective-permute-done.19.refs_6_), channel_id=1, source_target_pairs={{1,0},{2,1},{3,2},{4,3},{5,4},{6,5},{7,6},{8,7},{9,8},{10,9},{11,1... | collective-permute-start | bytes 3342344 | tf_op jit(solution)/shard_map/ppermute | solution.py:364
  84.4 12.7 %collective-permute-done.6.refs_2_ = f32[17,128,128]{2,1,0:T(8,128)} collective-permute-done((f32[17,128,128]{2,1,0:T(8,128)}, f32[17,128,128]{2,1,0:T(8,128)}, u32[]{:S(2)}, u32[]{:S(2)}) %collective-permute-start.6) | collective-permute-done | bytes 1114144 | tf_op jit(solution)/shard_map/ppermute | solution.py:364
  97.1 12.9 %shard_map.123 = (f32[17,128,128]{2,1,0:T(8,128)}, f32[17,128,128]{2,1,0:T(8,128)}, f32[17,128,128]{2,1,0:T(8,128)}, f32[17,128,128]{2,1,0:T(8,128)}, f32[17,128,128]{2,1,0:T(8,128)}) custom-call(s32[1]{0:T(128)} %bitcast.2.sector_ref, s32[17]{0:T(128)} %class_ref.5, s32[1,3,32]{2,1,0:T(4,128)} %copy.53.live_ref, s32[4,17]{1,0:T(4,128)} %copy.54.out_ref, ...), custom_call_target="tpu_custom_call" | custom-call | flops 4000000000 | bytes 10000000 | tf_op jit(solution)/shard_map/pallas_call | solution.py:161
  110.1 2.0 collective-permute-start.8
  113.5 1.9 collective-permute-start.15
  115.5 3.8 %collective-permute-start.16 = (f32[16,128,128]{2,1,0:T(8,128)S(1)}, f32[16,128,128]{2,1,0:T(8,128)S(1)}, u32[]{:S(2)}, u32[]{:S(2)}) collective-permute-start(f32[16,128,128]{2,1,0:T(8,128)S(1)} %bitcast.25), channel_id=1, source_target_pairs={{0,8},{1,9},{2,10},{3,11},{4,12},{5,13},{6,14},{7,15},{8,16},{9,17... | collective-permute-start | bytes 3145736 | tf_op jit(solution)/shard_map/ppermute | solution.py:364
  119.4 1.9 collective-permute-start.7
  121.9 7.4 %collective-permute-done.8 = f32[17,128,128]{2,1,0:T(8,128)S(1)} collective-permute-done((f32[17,128,128]{2,1,0:T(8,128)}, f32[17,128,128]{2,1,0:T(8,128)S(1)}, u32[]{:S(2)}, u32[]{:S(2)}) %collective-permute-start.8) | collective-permute-done | bytes 1114144 | tf_op jit(solution)/shard_map/ppermute | solution.py:364
  129.5 3.9 %collective-permute-start.9 = (f32[9,128,128]{2,1,0:T(8,128)S(1)}, f32[9,128,128]{2,1,0:T(8,128)S(1)}, u32[]{:S(2)}, u32[]{:S(2)}) collective-permute-start(f32[9,128,128]{2,1,0:T(8,128)S(1)} %slice.63), channel_id=1, source_target_pairs={{0,8},{1,9},{2,10},{3,11},{4,12},{5,13},{6,14},{7,15},{8,16},{9,17... | collective-permute-start | bytes 1769480 | tf_op jit(solution)/shard_map/ppermute | solution.py:364
  133.6 6.9 %collective-permute-done.15 = f32[16,128,128]{2,1,0:T(8,128)S(1)} collective-permute-done((f32[16,128,128]{2,1,0:T(8,128)S(1)}, f32[16,128,128]{2,1,0:T(8,128)S(1)}, u32[]{:S(2)}, u32[]{:S(2)}) %collective-permute-start.15) | collective-permute-done | bytes 1048608 | tf_op jit(solution)/shard_map/ppermute | solution.py:364
  140.5 3.9 %collective-permute-start.10 = (f32[8,128,128]{2,1,0:T(8,128)S(1)}, f32[8,128,128]{2,1,0:T(8,128)S(1)}, u32[]{:S(2)}, u32[]{:S(2)}) collective-permute-start(f32[8,128,128]{2,1,0:T(8,128)S(1)} %slice.66), channel_id=1, source_target_pairs={{0,8},{1,9},{2,10},{3,11},{4,12},{5,13},{6,14},{7,15},{8,16},{9,17... | collective-permute-start | bytes 1572872 | tf_op jit(solution)/shard_map/ppermute | solution.py:364
  144.4 2.4 broadcast_select_fusion
  146.8 28.1 %collective-permute-done.16 = f32[16,128,128]{2,1,0:T(8,128)S(1)} collective-permute-done((f32[16,128,128]{2,1,0:T(8,128)S(1)}, f32[16,128,128]{2,1,0:T(8,128)S(1)}, u32[]{:S(2)}, u32[]{:S(2)}) %collective-permute-start.16) | collective-permute-done | bytes 1048608 | tf_op jit(solution)/shard_map/ppermute | solution.py:364
  175.0 12.6 %collective-permute-done.9 = f32[9,128,128]{2,1,0:T(8,128)S(1)} collective-permute-done((f32[9,128,128]{2,1,0:T(8,128)S(1)}, f32[9,128,128]{2,1,0:T(8,128)S(1)}, u32[]{:S(2)}, u32[]{:S(2)}) %collective-permute-start.9) | collective-permute-done | bytes 589856 | tf_op jit(solution)/shard_map/ppermute | solution.py:364
  187.6 1.9 collective-permute-start.24
  189.7 9.0 %collective-permute-done.10 = f32[8,128,128]{2,1,0:T(8,128)S(1)} collective-permute-done((f32[8,128,128]{2,1,0:T(8,128)S(1)}, f32[8,128,128]{2,1,0:T(8,128)S(1)}, u32[]{:S(2)}, u32[]{:S(2)}) %collective-permute-start.10) | collective-permute-done | bytes 524320 | tf_op jit(solution)/shard_map/ppermute | solution.py:364
  198.7 4.3 %collective-permute-start.11 = (f32[9,128,128]{2,1,0:T(8,128)S(1)}, f32[9,128,128]{2,1,0:T(8,128)}, u32[]{:S(2)}, u32[]{:S(2)}) collective-permute-start(f32[9,128,128]{2,1,0:T(8,128)S(1)} %fusion.2.e0), channel_id=1, source_target_pairs={{0,32},{32,64},{64,96},{1,33},{33,65},{65,97},{2,34},{34,66},{66,9... | collective-permute-start | bytes 1769480 | tf_op jit(solution)/shard_map/ppermute | solution.py:364
  203.2 1.0 copy-done.11
  204.2 3.4 %collective-permute-start.12 = (f32[8,128,128]{2,1,0:T(8,128)S(1)}, f32[8,128,128]{2,1,0:T(8,128)}, u32[]{:S(2)}, u32[]{:S(2)}) collective-permute-start(f32[8,128,128]{2,1,0:T(8,128)S(1)} %fusion.5.e1), channel_id=1, source_target_pairs={{0,32},{32,64},{64,96},{1,33},{33,65},{65,97},{2,34},{34,66},{66,9... | collective-permute-start | bytes 1572872 | tf_op jit(solution)/shard_map/ppermute | solution.py:364
  210.9 5.9 %split_kets.1.kets_hbm = bf16[4,5,512,256]{3,2,1,0:T(8,128)(2,1)} custom-call(s32[1]{0:T(128)} %bitcast.2.sector_ref, f32[4,4,128,128]{3,2,1,0:T(8,128)} %bitcast.22, f32[4,4,128,128]{3,2,1,0:T(8,128)} %bitcast.34, f32[4,4,128,128]{3,2,1,0:T(8,128)} %bitcast.32, f32[4,4,128,128]{3,2,1,0:T(8,128)} %bitcast.27, f32[4,4,128,128]{3,2,1,0:T(8,128)} %bitcast.33), custom_call_target="tpu_custom_call" | custom-call | flops 5000000 | bytes 10000000 | tf_op jit(solution)/shard_map/split_kets/pallas_call | solution.py:190
  216.8 2.6 turn.1
  219.4 6.8 %collective-permute-done.12.passed1_ref = f32[8,128,128]{2,1,0:T(8,128)} collective-permute-done((f32[8,128,128]{2,1,0:T(8,128)S(1)}, f32[8,128,128]{2,1,0:T(8,128)}, u32[]{:S(2)}, u32[]{:S(2)}) %collective-permute-start.12) | collective-permute-done | bytes 524320 | tf_op jit(solution)/shard_map/ppermute | solution.py:364
  226.2 50.4 %pair.1 = f32[16,128,128]{2,1,0:T(8,128)} custom-call(s32[1]{0:T(128)} %bitcast.2.sector_ref, s32[1]{0:T(128)} %bitcast.7.region_ref, s32[17]{0:T(128)} %class_ref.5, s32[1,3,32]{2,1,0:T(4,128)} %copy.53.live_ref, s32[4,17]{1,0:T(4,128)} %copy.54.out_ref, s32[20,11]{1,0:T(8,128)} %copy.55.block_ref, s32[20,11]{1,0:T(8,128)} %broadcast_add_fusion.place_ref, ...), custom_call_target="tpu_custom_call" | custom-call | flops 20000000000 | bytes 18000000 | tf_op jit(solution)/shard_map/pair/pallas_call | solution.py:321
  (93 shorter events, 14.0 us)
Async XLA Ops:
  0.6 25.5 %collective-permute-start = (f32[2,4,128,128]{3,2,1,0:T(8,128)}, f32[2,4,128,128]{3,2,1,0:T(8,128)S(1)}, u32[]{:S(2)}, u32[]{:S(2)}) collective-permute-start(f32[2,4,128,128]{3,2,1,0:T(8,128)} %bitcast.37), channel_id=1, source_target_pairs={{1,0},{2,1},{3,2},{4,3},{5,4},{6,5},{7,6},{8,7},{9,8},{10,9},{11,1... | collective-permute-start | bytes 1572872 | tf_op jit(solution)/shard_map/ppermute | solution.py:364
  4.5 21.6 %collective-permute-start.1 = (f32[2,4,128,128]{3,2,1,0:T(8,128)}, f32[2,4,128,128]{3,2,1,0:T(8,128)S(1)}, u32[]{:S(2)}, u32[]{:S(2)}) collective-permute-start(f32[2,4,128,128]{3,2,1,0:T(8,128)} %bitcast.38), channel_id=1, source_target_pairs={{0,1},{1,2},{2,3},{3,4},{4,5},{5,6},{6,7},{7,8},{8,9},{9,10},{10,1... | collective-permute-start | bytes 1572872 | tf_op jit(solution)/shard_map/ppermute | solution.py:364
  6.5 19.7 %collective-permute-start.2 = (f32[2,4,128,128]{3,2,1,0:T(8,128)}, f32[2,4,128,128]{3,2,1,0:T(8,128)}, u32[]{:S(2)}, u32[]{:S(2)}) collective-permute-start(f32[2,4,128,128]{3,2,1,0:T(8,128)} %bitcast.39), channel_id=1, source_target_pairs={{8,0},{9,1},{10,2},{11,3},{12,4},{13,5},{14,6},{15,7},{16,8},{17,9... | collective-permute-start | bytes 1572872 | tf_op jit(solution)/shard_map/ppermute | solution.py:364
  8.4 20.3 %collective-permute-start.3 = (f32[2,4,128,128]{3,2,1,0:T(8,128)}, f32[2,4,128,128]{3,2,1,0:T(8,128)}, u32[]{:S(2)}, u32[]{:S(2)}) collective-permute-start(f32[2,4,128,128]{3,2,1,0:T(8,128)} %bitcast.40), channel_id=1, source_target_pairs={{0,8},{1,9},{2,10},{3,11},{4,12},{5,13},{6,14},{7,15},{8,16},{9,17... | collective-permute-start | bytes 1572872 | tf_op jit(solution)/shard_map/ppermute | solution.py:364
  12.3 33.8 %collective-permute-start.17 = (f32[17,128,128]{2,1,0:T(8,128)}, f32[17,128,128]{2,1,0:T(8,128)S(1)}, u32[]{:S(2)}, u32[]{:S(2)}) collective-permute-start(f32[17,128,128]{2,1,0:T(8,128)} %bitcast.29), channel_id=1, source_target_pairs={{8,0},{9,1},{10,2},{11,3},{12,4},{13,5},{14,6},{15,7},{16,8},{17,9... | collective-permute-start | bytes 3342344 | tf_op jit(solution)/shard_map/ppermute | solution.py:364
  26.1 2.6 copy-start.14
  26.2 2.6 copy-start.15
  42.1 19.1 %collective-permute-start.5 = (f32[17,128,128]{2,1,0:T(8,128)}, f32[17,128,128]{2,1,0:T(8,128)S(1)}, u32[]{:S(2)}, u32[]{:S(2)}) collective-permute-start(f32[17,128,128]{2,1,0:T(8,128)} %get-tuple-element.24), channel_id=1, source_target_pairs={{0,1},{1,2},{2,3},{3,4},{4,5},{5,6},{6,7},{7,8},{8,9},{9,10},{10,1... | collective-permute-start | bytes 3342344 | tf_op jit(solution)/shard_map/ppermute | solution.py:364
  46.2 29.6 %copy-start = (f32[17,128,128]{2,1,0:T(8,128)}, f32[17,128,128]{2,1,0:T(8,128)S(1)}, u32[]{:S(2)}) copy-start(f32[17,128,128]{2,1,0:T(8,128)S(1)} %collective-permute-done.17.refs_3_) | copy-start | bytes 3342340
  46.2 29.6 %collective-permute-start.19 = (f32[17,128,128]{2,1,0:T(8,128)S(1)}, f32[17,128,128]{2,1,0:T(8,128)}, u32[]{:S(2)}, u32[]{:S(2)}) collective-permute-start(f32[17,128,128]{2,1,0:T(8,128)S(1)} %collective-permute-done.17.refs_3_), channel_id=1, source_target_pairs={{8,0},{9,1},{10,2},{11,3},{12,4},{13,5},{14,6},{15,7},{16,8},{17,9... | collective-permute-start | bytes 3342344 | tf_op jit(solution)/shard_map/ppermute | solution.py:364
  48.2 33.1 %collective-permute-start.4 = (f32[17,128,128]{2,1,0:T(8,128)}, f32[17,128,128]{2,1,0:T(8,128)}, u32[]{:S(2)}, u32[]{:S(2)}) collective-permute-start(f32[17,128,128]{2,1,0:T(8,128)} %get-tuple-element.22), channel_id=1, source_target_pairs={{0,1},{1,2},{2,3},{3,4},{4,5},{5,6},{6,7},{7,8},{8,9},{9,10},{10,1... | collective-permute-start | bytes 3342344 | tf_op jit(solution)/shard_map/ppermute | solution.py:364
  61.2 6.3 %copy-start.2 = (f32[1,16,1,128,128]{4,3,2,1,0:T(8,128)S(1)}, f32[1,16,1,128,128]{4,3,2,1,0:T(8,128)}, u32[]{:S(2)}) copy-start(f32[1,16,1,128,128]{4,3,2,1,0:T(8,128)} %param.14) | copy-start | bytes 3145732
  63.7 33.4 %collective-permute-start.6 = (f32[17,128,128]{2,1,0:T(8,128)}, f32[17,128,128]{2,1,0:T(8,128)}, u32[]{:S(2)}, u32[]{:S(2)}) collective-permute-start(f32[17,128,128]{2,1,0:T(8,128)} %add.155), channel_id=1, source_target_pairs={{0,8},{1,9},{2,10},{3,11},{4,12},{5,13},{6,14},{7,15},{8,16},{9,17... | collective-permute-start | bytes 3342344 | tf_op jit(solution)/shard_map/ppermute | solution.py:364
  67.6 46.0 %collective-permute-start.13 = (f32[16,128,128]{2,1,0:T(8,128)S(1)}, f32[16,128,128]{2,1,0:T(8,128)S(1)}, u32[]{:S(2)}, u32[]{:S(2)}) collective-permute-start(f32[16,128,128]{2,1,0:T(8,128)S(1)} %bitcast.23), channel_id=1, source_target_pairs={{8,0},{9,1},{10,2},{11,3},{12,4},{13,5},{14,6},{15,7},{16,8},{17,9... | collective-permute-start | bytes 3145736 | tf_op jit(solution)/shard_map/ppermute | solution.py:364
  75.2 5.4 %copy-start.13 = (s32[1,3,32]{2,0,1:T(1,128)S(1)}, s32[1,3,32]{2,0,1:T(1,128)}, u32[]{:S(2)}) copy-start(s32[1,3,32]{2,0,1:T(1,128)} %param.18) | copy-start | bytes 1156
  75.2 40.3 %collective-permute-start.18 = (f32[17,128,128]{2,1,0:T(8,128)}, f32[17,128,128]{2,1,0:T(8,128)}, u32[]{:S(2)}, u32[]{:S(2)}) collective-permute-start(f32[17,128,128]{2,1,0:T(8,128)} %broadcast_select_fusion.3), channel_id=1, source_target_pairs={{0,7},{1,0},{2,1},{3,2},{4,3},{5,4},{6,5},{7,6},{8,15},{9,8},{10,9... | collective-permute-start | bytes 3342344 | tf_op jit(solution)/shard_map/ppermute | solution.py:371
  78.1 41.3 %collective-permute-start.20 = (f32[17,128,128]{2,1,0:T(8,128)}, f32[17,128,128]{2,1,0:T(8,128)S(1)}, u32[]{:S(2)}, u32[]{:S(2)}) collective-permute-start(f32[17,128,128]{2,1,0:T(8,128)} %broadcast_select_fusion.2), channel_id=1, source_target_pairs={{0,7},{1,0},{2,1},{3,2},{4,3},{5,4},{6,5},{7,6},{8,15},{9,8},{10,9... | collective-permute-start | bytes 3342344 | tf_op jit(solution)/shard_map/ppermute | solution.py:371
  81.3 48.2 %collective-permute-start.22 = (f32[17,128,128]{2,1,0:T(8,128)}, f32[17,128,128]{2,1,0:T(8,128)}, u32[]{:S(2)}, u32[]{:S(2)}) collective-permute-start(f32[17,128,128]{2,1,0:T(8,128)} %collective-permute-done.19.refs_6_), channel_id=1, source_target_pairs={{1,0},{2,1},{3,2},{4,3},{5,4},{6,5},{7,6},{8,7},{9,8},{10,9},{11,1... | collective-permute-start | bytes 3342344 | tf_op jit(solution)/shard_map/ppermute | solution.py:364
  110.1 19.2 %collective-permute-start.8 = (f32[17,128,128]{2,1,0:T(8,128)}, f32[17,128,128]{2,1,0:T(8,128)S(1)}, u32[]{:S(2)}, u32[]{:S(2)}) collective-permute-start(f32[17,128,128]{2,1,0:T(8,128)} %get-tuple-element.28), channel_id=1, source_target_pairs={{0,1},{1,2},{2,3},{3,4},{4,5},{5,6},{6,7},{7,8},{8,9},{9,10},{10,1... | collective-permute-start | bytes 3342344 | tf_op jit(solution)/shard_map/ppermute | solution.py:364
  113.5 8.4 %copy-start.3 = (f32[16,128,128]{2,1,0:T(8,128)}, f32[16,128,128]{2,1,0:T(8,128)S(1)}, u32[]{:S(2)}) copy-start(f32[16,128,128]{2,1,0:T(8,128)S(1)} %collective-permute-done.13) | copy-start | bytes 3145732
  113.5 27.0 %collective-permute-start.15 = (f32[16,128,128]{2,1,0:T(8,128)S(1)}, f32[16,128,128]{2,1,0:T(8,128)S(1)}, u32[]{:S(2)}, u32[]{:S(2)}) collective-permute-start(f32[16,128,128]{2,1,0:T(8,128)S(1)} %bitcast.24), channel_id=1, source_target_pairs={{0,1},{1,2},{2,3},{3,4},{4,5},{5,6},{6,7},{7,8},{8,9},{9,10},{10,1... | collective-permute-start | bytes 3145736 | tf_op jit(solution)/shard_map/ppermute | solution.py:364
  115.5 59.4 %collective-permute-start.16 = (f32[16,128,128]{2,1,0:T(8,128)S(1)}, f32[16,128,128]{2,1,0:T(8,128)S(1)}, u32[]{:S(2)}, u32[]{:S(2)}) collective-permute-start(f32[16,128,128]{2,1,0:T(8,128)S(1)} %bitcast.25), channel_id=1, source_target_pairs={{0,8},{1,9},{2,10},{3,11},{4,12},{5,13},{6,14},{7,15},{8,16},{9,17... | collective-permute-start | bytes 3145736 | tf_op jit(solution)/shard_map/ppermute | solution.py:364
  119.4 25.0 %copy-start.1 = (f32[17,128,128]{2,1,0:T(8,128)}, f32[17,128,128]{2,1,0:T(8,128)S(1)}, u32[]{:S(2)}) copy-start(f32[17,128,128]{2,1,0:T(8,128)S(1)} %collective-permute-done.20.refs_4_) | copy-start | bytes 3342340
  119.4 55.5 %collective-permute-start.7 = (f32[17,128,128]{2,1,0:T(8,128)}, f32[17,128,128]{2,1,0:T(8,128)S(1)}, u32[]{:S(2)}, u32[]{:S(2)}) collective-permute-start(f32[17,128,128]{2,1,0:T(8,128)} %get-tuple-element.26), channel_id=1, source_target_pairs={{0,1},{1,2},{2,3},{3,4},{4,5},{5,6},{6,7},{7,8},{8,9},{9,10},{10,1... | collective-permute-start | bytes 3342344 | tf_op jit(solution)/shard_map/ppermute | solution.py:364
  121.8 7.5 %copy-start.8 = (f32[17,128,128]{2,1,0:T(8,128)S(1)}, f32[17,128,128]{2,1,0:T(8,128)}, u32[]{:S(2)}) copy-start(f32[17,128,128]{2,1,0:T(8,128)} %get-tuple-element.27) | copy-start | bytes 3342340
  129.3 73.9 %collective-permute-start.14 = (f32[16,128,128]{2,1,0:T(8,128)S(1)}, f32[16,128,128]{2,1,0:T(8,128)S(1)}, u32[]{:S(2)}, u32[]{:S(2)}) collective-permute-start(f32[16,128,128]{2,1,0:T(8,128)S(1)} %broadcast_select_fusion.4), channel_id=1, source_target_pairs={{0,7},{1,0},{2,1},{3,2},{4,3},{5,4},{6,5},{7,6},{8,15},{9,8},{10,9... | collective-permute-start | bytes 3145736 | tf_op jit(solution)/shard_map/ppermute | solution.py:371
  129.5 58.1 %collective-permute-start.9 = (f32[9,128,128]{2,1,0:T(8,128)S(1)}, f32[9,128,128]{2,1,0:T(8,128)S(1)}, u32[]{:S(2)}, u32[]{:S(2)}) collective-permute-start(f32[9,128,128]{2,1,0:T(8,128)S(1)} %slice.63), channel_id=1, source_target_pairs={{0,8},{1,9},{2,10},{3,11},{4,12},{5,13},{6,14},{7,15},{8,16},{9,17... | collective-permute-start | bytes 1769480 | tf_op jit(solution)/shard_map/ppermute | solution.py:364
  133.6 55.9 %copy-start.6 = (f32[17,128,128]{2,1,0:T(8,128)S(1)}, f32[17,128,128]{2,1,0:T(8,128)}, u32[]{:S(2)}) copy-start(f32[17,128,128]{2,1,0:T(8,128)} %get-tuple-element.25) | copy-start | bytes 3342340
  133.6 55.9 %copy-start.7 = (f32[17,128,128]{2,1,0:T(8,128)S(1)}, f32[17,128,128]{2,1,0:T(8,128)}, u32[]{:S(2)}) copy-start(f32[17,128,128]{2,1,0:T(8,128)} %get-tuple-element.29) | copy-start | bytes 3342340
  140.5 6.3 %copy-start.9 = (f32[16,128,128]{2,1,0:T(8,128)}, f32[16,128,128]{2,1,0:T(8,128)S(1)}, u32[]{:S(2)}) copy-start(f32[16,128,128]{2,1,0:T(8,128)S(1)} %collective-permute-done.15) | copy-start | bytes 3145732
  140.5 58.2 %collective-permute-start.10 = (f32[8,128,128]{2,1,0:T(8,128)S(1)}, f32[8,128,128]{2,1,0:T(8,128)S(1)}, u32[]{:S(2)}, u32[]{:S(2)}) collective-permute-start(f32[8,128,128]{2,1,0:T(8,128)S(1)} %slice.66), channel_id=1, source_target_pairs={{0,8},{1,9},{2,10},{3,11},{4,12},{5,13},{6,14},{7,15},{8,16},{9,17... | collective-permute-start | bytes 1572872 | tf_op jit(solution)/shard_map/ppermute | solution.py:364
  174.9 14.7 %copy-start.10 = (f32[16,128,128]{2,1,0:T(8,128)}, f32[16,128,128]{2,1,0:T(8,128)S(1)}, u32[]{:S(2)}) copy-start(f32[16,128,128]{2,1,0:T(8,128)S(1)} %collective-permute-done.16) | copy-start | bytes 3145732
  174.9 44.4 %collective-permute-start.21 = (f32[17,128,128]{2,1,0:T(8,128)S(1)}, f32[17,128,128]{2,1,0:T(8,128)}, u32[]{:S(2)}, u32[]{:S(2)}) collective-permute-start(f32[17,128,128]{2,1,0:T(8,128)S(1)} %broadcast_select_fusion.1), channel_id=1, source_target_pairs={{0,7},{1,0},{2,1},{3,2},{4,3},{5,4},{6,5},{7,6},{8,15},{9,8},{10,9... | collective-permute-start | bytes 3342344 | tf_op jit(solution)/shard_map/ppermute | solution.py:371
  174.9 44.4 %collective-permute-start.23 = (f32[17,128,128]{2,1,0:T(8,128)}, f32[17,128,128]{2,1,0:T(8,128)}, u32[]{:S(2)}, u32[]{:S(2)}) collective-permute-start(f32[17,128,128]{2,1,0:T(8,128)} %broadcast_select_fusion), channel_id=1, source_target_pairs={{0,7},{1,0},{2,1},{3,2},{4,3},{5,4},{6,5},{7,6},{8,15},{9,8},{10,9... | collective-permute-start | bytes 3342344 | tf_op jit(solution)/shard_map/ppermute | solution.py:371
  187.6 31.8 %collective-permute-start.24 = (f32[17,128,128]{2,1,0:T(8,128)}, f32[17,128,128]{2,1,0:T(8,128)}, u32[]{:S(2)}, u32[]{:S(2)}) collective-permute-start(f32[17,128,128]{2,1,0:T(8,128)} %collective-permute-done.22.refs_7_), channel_id=1, source_target_pairs={{1,0},{2,1},{3,2},{4,3},{5,4},{6,5},{7,6},{8,7},{9,8},{10,9},{11,1... | collective-permute-start | bytes 3342344 | tf_op jit(solution)/shard_map/ppermute | solution.py:364
  189.7 13.5 %copy-start.4 = (f32[9,128,128]{2,1,0:T(8,128)}, f32[9,128,128]{2,1,0:T(8,128)S(1)}, u32[]{:S(2)}) copy-start(f32[9,128,128]{2,1,0:T(8,128)S(1)} %fusion.2.e0) | copy-start | bytes 1769476
  189.7 17.9 %copy-start.12 = (f32[1,2,17,17,4,4]{3,5,4,2,1,0:T(4,128)S(1)}, f32[1,2,17,17,4,4]{3,5,4,2,1,0:T(4,128)}, u32[]{:S(2)}) copy-start(f32[1,2,17,17,4,4]{3,5,4,2,1,0:T(4,128)} %param.16) | copy-start | bytes 110980
  198.7 27.4 %collective-permute-start.11 = (f32[9,128,128]{2,1,0:T(8,128)S(1)}, f32[9,128,128]{2,1,0:T(8,128)}, u32[]{:S(2)}, u32[]{:S(2)}) collective-permute-start(f32[9,128,128]{2,1,0:T(8,128)S(1)} %fusion.2.e0), channel_id=1, source_target_pairs={{0,32},{32,64},{64,96},{1,33},{33,65},{65,97},{2,34},{34,66},{66,9... | collective-permute-start | bytes 1769480 | tf_op jit(solution)/shard_map/ppermute | solution.py:364
  203.1 6.6 %copy-start.5 = (f32[8,128,128]{2,1,0:T(8,128)}, f32[8,128,128]{2,1,0:T(8,128)S(1)}, u32[]{:S(2)}) copy-start(f32[8,128,128]{2,1,0:T(8,128)S(1)} %fusion.5.e1) | copy-start | bytes 1572868
  203.2 1.0 copy-start.11
  204.2 22.0 %collective-permute-start.12 = (f32[8,128,128]{2,1,0:T(8,128)S(1)}, f32[8,128,128]{2,1,0:T(8,128)}, u32[]{:S(2)}, u32[]{:S(2)}) collective-permute-start(f32[8,128,128]{2,1,0:T(8,128)S(1)} %fusion.5.e1), channel_id=1, source_target_pairs={{0,32},{32,64},{64,96},{1,33},{33,65},{65,97},{2,34},{34,66},{66,9... | collective-permute-start | bytes 1572872 | tf_op jit(solution)/shard_map/ppermute | solution.py:364

commit v4 on v3

--- a/solution.py
+++ b/solution.py
@@ -432,16 +432,19 @@
     keep = (width[:, None] < count[:, None, None]) & (width < own)
     parts = []
     passed = []
-    for lo, hi in ((0, 9), (9, NW)):
+    for n, (lo, hi) in enumerate(((0, 9), (9, NW))):
         partial = fetch(upper[lo:hi], -ND)
         second = jnp.where(keep[lo:hi], h0[lo:hi] + below2[lo:hi] + partial, 0.0)
         second = jnp.where(region_sites[0] > 1, second, first[lo:hi])
+        if n == 0:
+            split = split_kets(sector, kets)
+            rules = (flat_rule(mpo_pair[0, 0]), flat_rule(mpo_pair[0, 1]))
+            second, split, *rules = lax.optimization_barrier((second, split, *rules))
         parts.append(second)
         passed.append(fetch(second, -1, "region"))
 
     environment = turned(parts)
-    split = split_kets(sector, kets)
-    scalars = (sector, region, channel_class, live_rows, *tables, flat_rule(mpo_pair[0, 0]), flat_rule(mpo_pair[0, 1]))
+    scalars = (sector, region, channel_class, live_rows, *tables, *rules)
     images = pair(scalars, start, passed, split, [rights[u, d] for u in range(3) for d in range(3)])
     return environment[None, :, None], images[None, :, None]
 

time: 279 us -> 258 us (0.925)
  waiting for transfers between devices: 99.3 us -> 67.4 us
  starting transfers between devices: 60.2 us -> 64.8 us
  other arithmetic: 16.4 us -> 20.3 us
    ppermute x20, waiting for transfers between devices: 99.3 us -> 67.4 us  [fetch(): return lax.ppermute(blocks, axis, pairs)]
    ppermute x5, starting transfers between devices: 3.08 us -> 8.33 us  [fetch_next(): return lax.ppermute(given, 'block', pairs)]
  transfers between devices with their start and end apart: 25 -> 25, of which waited for: 10 -> 9; matrix products, arithmetic and copies ran while one was open for 11% -> 13% of each run, Pallas kernels for 13% -> 14%
where the time goes in v4:
time: 258 us; the launch traced here: 255 us
  Pallas kernels  85.5 us (33%)
  waiting for transfers between devices  67.4 us (26%)
  starting transfers between devices  64.8 us (25%)
  other arithmetic  20.3 us (8%)
  local copies, waits for them, and re-layouts  14.7 us (6%)
    ppermute x20, waiting for transfers between devices, fetch(): return lax.ppermute(blocks, axis, pairs)  67.4 us
    ppermute x20, starting transfers between devices, fetch(): return lax.ppermute(blocks, axis, pairs)  56.5 us
    pallas_call x1, Pallas kernels, pair(): pl.pallas_call(pair_kernel, out_shape=jax.ShapeDtypeStruct((16, TILE, TIL...  50.4 us
    pallas_call x2, Pallas kernels, site(): pl.pallas_call(functools.partial(site_kernel, number), grid=(1,), out_sha...  26.6 us
    ppermute x5, starting transfers between devices, fetch_next(): return lax.ppermute(given, 'block', pairs)  8.33 us
    select_n x5, other arithmetic, fetch_next(): given = jnp.where(sector[0] % ND == 0, above, blocks)  8.16 us
    pallas_call x1, Pallas kernels, split_kets(): pl.pallas_call(kets_kernel, grid=(4,), out_shape=jax.ShapeDtypeStruct((4,...  5.89 us
  transfers between devices with their start and end apart: 25, of which 9 were waited for; matrix products, arithmetic and copies ran while one was open for 13% of the time, Pallas kernels for 14%

profile of v4, /device:TPU:32, one launch (start us, length us, event | category | flops | bytes accessed | tf_op | source)
XLA Modules:
  0.0 254.6 jit_solution(13006558305931858605)
XLA Ops:
  0.6 3.9 %collective-permute-start = (f32[2,4,128,128]{3,2,1,0:T(8,128)}, f32[2,4,128,128]{3,2,1,0:T(8,128)S(1)}, u32[]{:S(2)}, u32[]{:S(2)}) collective-permute-start(f32[2,4,128,128]{3,2,1,0:T(8,128)} %bitcast.35), channel_id=1, source_target_pairs={{1,0},{2,1},{3,2},{4,3},{5,4},{6,5},{7,6},{8,7},{9,8},{10,9},{11,1... | collective-permute-start | bytes 1572872 | tf_op jit(solution)/shard_map/ppermute | solution.py:364
  4.5 1.9 collective-permute-start.1
  6.5 1.9 collective-permute-start.2
  8.4 3.9 %collective-permute-start.3 = (f32[2,4,128,128]{3,2,1,0:T(8,128)}, f32[2,4,128,128]{3,2,1,0:T(8,128)}, u32[]{:S(2)}, u32[]{:S(2)}) collective-permute-start(f32[2,4,128,128]{3,2,1,0:T(8,128)} %bitcast.38), channel_id=1, source_target_pairs={{0,8},{1,9},{2,10},{3,11},{4,12},{5,13},{6,14},{7,15},{8,16},{9,17... | collective-permute-start | bytes 1572872 | tf_op jit(solution)/shard_map/ppermute | solution.py:364
  12.3 2.7 %collective-permute-start.17 = (f32[17,128,128]{2,1,0:T(8,128)}, f32[17,128,128]{2,1,0:T(8,128)S(1)}, u32[]{:S(2)}, u32[]{:S(2)}) collective-permute-start(f32[17,128,128]{2,1,0:T(8,128)} %bitcast.29), channel_id=1, source_target_pairs={{8,0},{9,1},{10,2},{11,3},{12,4},{13,5},{14,6},{15,7},{16,8},{17,9... | collective-permute-start | bytes 3342344 | tf_op jit(solution)/shard_map/ppermute | solution.py:364
  21.6 1.3 copy.53.live_ref
  22.9 1.0 fusion.12
  26.2 2.5 collective-permute-done.3.refs_5_.refs_7_
  28.7 13.5 %shard_map.122 = (f32[17,128,128]{2,1,0:T(8,128)}, f32[17,128,128]{2,1,0:T(8,128)}, f32[17,128,128]{2,1,0:T(8,128)}, f32[17,128,128]{2,1,0:T(8,128)}) custom-call(s32[1]{0:T(128)} %bitcast.2.sector_ref, s32[17]{0:T(128)} %class_ref.5, s32[1,3,32]{2,1,0:T(4,128)} %copy.53.live_ref, s32[4,17]{1,0:T(4,128)} %copy.54.out_ref, s32[20,11]{1,0:T(8,128)} %copy.55.block_ref, ...), custom_call_target="tpu_custom_call" | custom-call | flops 4000000000 | bytes 10000000 | tf_op jit(solution)/shard_map/pallas_call | solution.py:161
  42.2 1.9 collective-permute-start.5
  44.1 1.9 collective-permute-start.10
  46.2 2.0 collective-permute-start.19
  48.2 1.9 collective-permute-start.4
  50.1 11.2 %collective-permute-done.5 = f32[17,128,128]{2,1,0:T(8,128)S(1)} collective-permute-done((f32[17,128,128]{2,1,0:T(8,128)}, f32[17,128,128]{2,1,0:T(8,128)S(1)}, u32[]{:S(2)}, u32[]{:S(2)}) %collective-permute-start.5) | collective-permute-done | bytes 1114144 | tf_op jit(solution)/shard_map/ppermute | solution.py:364
  61.3 2.4 add.155
  63.7 3.8 %collective-permute-start.6 = (f32[17,128,128]{2,1,0:T(8,128)}, f32[17,128,128]{2,1,0:T(8,128)}, u32[]{:S(2)}, u32[]{:S(2)}) collective-permute-start(f32[17,128,128]{2,1,0:T(8,128)} %add.155), channel_id=1, source_target_pairs={{0,8},{1,9},{2,10},{3,11},{4,12},{5,13},{6,14},{7,15},{8,16},{9,17... | collective-permute-start | bytes 3342344 | tf_op jit(solution)/shard_map/ppermute | solution.py:364
  67.5 3.8 %collective-permute-start.13 = (f32[16,128,128]{2,1,0:T(8,128)S(1)}, f32[16,128,128]{2,1,0:T(8,128)}, u32[]{:S(2)}, u32[]{:S(2)}) collective-permute-start(f32[16,128,128]{2,1,0:T(8,128)S(1)} %bitcast.24), channel_id=1, source_target_pairs={{0,8},{1,9},{2,10},{3,11},{4,12},{5,13},{6,14},{7,15},{8,16},{9,17... | collective-permute-start | bytes 3145736 | tf_op jit(solution)/shard_map/ppermute | solution.py:364
  71.4 1.3 copy.48
  72.7 1.6 reshape_squeeze.15
  74.9 2.2 collective-permute-start.12
  77.1 1.1 broadcast_select_fusion.4
  78.2 1.1 broadcast_select_fusion.3
  79.4 15.9 %collective-permute-done.19.refs_6_ = f32[17,128,128]{2,1,0:T(8,128)} collective-permute-done((f32[17,128,128]{2,1,0:T(8,128)S(1)}, f32[17,128,128]{2,1,0:T(8,128)}, u32[]{:S(2)}, u32[]{:S(2)}) %collective-permute-start.19) | collective-permute-done | bytes 1114144 | tf_op jit(solution)/shard_map/ppermute | solution.py:364
  95.3 3.1 %collective-permute-start.11 = (f32[16,128,128]{2,1,0:T(8,128)}, f32[16,128,128]{2,1,0:T(8,128)S(1)}, u32[]{:S(2)}, u32[]{:S(2)}) collective-permute-start(f32[16,128,128]{2,1,0:T(8,128)} %broadcast_select_fusion.4), channel_id=1, source_target_pairs={{0,7},{1,0},{2,1},{3,2},{4,3},{5,4},{6,5},{7,6},{8,15},{9,8},{10,9... | collective-permute-start | bytes 3145736 | tf_op jit(solution)/shard_map/ppermute | solution.py:371
  98.3 2.4 broadcast_select_fusion.2
  100.7 7.9 %collective-permute-done.6.refs_2_ = f32[17,128,128]{2,1,0:T(8,128)} collective-permute-done((f32[17,128,128]{2,1,0:T(8,128)}, f32[17,128,128]{2,1,0:T(8,128)}, u32[]{:S(2)}, u32[]{:S(2)}) %collective-permute-start.6) | collective-permute-done | bytes 1114144 | tf_op jit(solution)/shard_map/ppermute | solution.py:364
  108.6 13.1 %shard_map.123 = (f32[17,128,128]{2,1,0:T(8,128)}, f32[17,128,128]{2,1,0:T(8,128)}, f32[17,128,128]{2,1,0:T(8,128)}, f32[17,128,128]{2,1,0:T(8,128)}, f32[17,128,128]{2,1,0:T(8,128)}) custom-call(s32[1]{0:T(128)} %bitcast.2.sector_ref, s32[17]{0:T(128)} %class_ref.5, s32[1,3,32]{2,1,0:T(4,128)} %copy.53.live_ref, s32[4,17]{1,0:T(4,128)} %copy.54.out_ref, ...), custom_call_target="tpu_custom_call" | custom-call | flops 4000000000 | bytes 10000000 | tf_op jit(solution)/shard_map/pallas_call | solution.py:161
  121.7 9.2 %collective-permute-done.13 = f32[16,128,128]{2,1,0:T(8,128)} collective-permute-done((f32[16,128,128]{2,1,0:T(8,128)S(1)}, f32[16,128,128]{2,1,0:T(8,128)}, u32[]{:S(2)}, u32[]{:S(2)}) %collective-permute-start.13) | collective-permute-done | bytes 1048608 | tf_op jit(solution)/shard_map/ppermute | solution.py:364
  131.0 1.9 collective-permute-start.8
  133.1 5.7 %collective-permute-start.22 = (f32[17,128,128]{2,1,0:T(8,128)}, f32[17,128,128]{2,1,0:T(8,128)}, u32[]{:S(2)}, u32[]{:S(2)}) collective-permute-start(f32[17,128,128]{2,1,0:T(8,128)} %collective-permute-done.19.refs_6_), channel_id=1, source_target_pairs={{1,0},{2,1},{3,2},{4,3},{5,4},{6,5},{7,6},{8,7},{9,8},{10,9},{11,1... | collective-permute-start | bytes 3342344 | tf_op jit(solution)/shard_map/ppermute | solution.py:364
  139.5 1.0 copy-done.9
  140.5 1.9 collective-permute-start.7
  147.6 5.9 %split_kets.1.kets_hbm = bf16[4,5,512,256]{3,2,1,0:T(8,128)(2,1)} custom-call(s32[1]{0:T(128)} %bitcast.2.sector_ref, f32[4,4,128,128]{3,2,1,0:T(8,128)} %bitcast.22, f32[4,4,128,128]{3,2,1,0:T(8,128)} %bitcast.32, f32[4,4,128,128]{3,2,1,0:T(8,128)} %bitcast.8.k2, f32[4,4,128,128]{3,2,1,0:T(8,128)} %bitcast.27, f32[4,4,128,128]{3,2,1,0:T(8,128)} %bitcast.10.k4), custom_call_target="tpu_custom_call" | custom-call | flops 5000000 | bytes 10000000 | tf_op jit(solution)/shard_map/split_kets/pallas_call | solution.py:190
  153.5 2.1 add.157
  155.7 3.8 %collective-permute-start.9 = (f32[9,128,128]{2,1,0:T(8,128)S(1)}, f32[9,128,128]{2,1,0:T(8,128)S(1)}, u32[]{:S(2)}, u32[]{:S(2)}) collective-permute-start(f32[9,128,128]{2,1,0:T(8,128)S(1)} %slice.63), channel_id=1, source_target_pairs={{0,8},{1,9},{2,10},{3,11},{4,12},{5,13},{6,14},{7,15},{8,16},{9,17... | collective-permute-start | bytes 1769480 | tf_op jit(solution)/shard_map/ppermute | solution.py:364
  159.5 1.1 broadcast_select_fusion.1
  160.6 5.2 %collective-permute-start.21 = (f32[17,128,128]{2,1,0:T(8,128)}, f32[17,128,128]{2,1,0:T(8,128)}, u32[]{:S(2)}, u32[]{:S(2)}) collective-permute-start(f32[17,128,128]{2,1,0:T(8,128)} %broadcast_select_fusion.1), channel_id=1, source_target_pairs={{0,7},{1,0},{2,1},{3,2},{4,3},{5,4},{6,5},{7,6},{8,15},{9,8},{10,9... | collective-permute-start | bytes 3342344 | tf_op jit(solution)/shard_map/ppermute | solution.py:371
  165.9 2.3 collective-permute-start.14
  168.3 2.4 broadcast_select_fusion
  170.7 1.9 collective-permute-start.24
  172.6 2.1 collective-permute-done.9
  175.0 3.4 %collective-permute-start.15 = (f32[9,128,128]{2,1,0:T(8,128)S(1)}, f32[9,128,128]{2,1,0:T(8,128)S(1)}, u32[]{:S(2)}, u32[]{:S(2)}) collective-permute-start(f32[9,128,128]{2,1,0:T(8,128)S(1)} %fusion.2.e0), channel_id=1, source_target_pairs={{0,32},{32,64},{64,96},{1,33},{33,65},{65,97},{2,34},{34,66},{66,9... | collective-permute-start | bytes 1769480 | tf_op jit(solution)/shard_map/ppermute | solution.py:364
  178.4 7.5 %collective-permute-done.14 = f32[8,128,128]{2,1,0:T(8,128)S(1)} collective-permute-done((f32[8,128,128]{2,1,0:T(8,128)S(1)}, f32[8,128,128]{2,1,0:T(8,128)S(1)}, u32[]{:S(2)}, u32[]{:S(2)}) %collective-permute-start.14) | collective-permute-done | bytes 524320 | tf_op jit(solution)/shard_map/ppermute | solution.py:364
  186.1 3.4 %collective-permute-start.16 = (f32[8,128,128]{2,1,0:T(8,128)S(1)}, f32[8,128,128]{2,1,0:T(8,128)S(1)}, u32[]{:S(2)}, u32[]{:S(2)}) collective-permute-start(f32[8,128,128]{2,1,0:T(8,128)S(1)} %fusion.5.e1), channel_id=1, source_target_pairs={{0,32},{32,64},{64,96},{1,33},{33,65},{65,97},{2,34},{34,66},{66,9... | collective-permute-start | bytes 1572872 | tf_op jit(solution)/shard_map/ppermute | solution.py:364
  189.5 2.6 %turn.1 = f32[17,128,128]{2,1,0:T(8,128)} custom-call(f32[9,128,128]{2,1,0:T(8,128)} %copy-done.4, f32[8,128,128]{2,1,0:T(8,128)} %copy-done.5), custom_call_target="tpu_custom_call" | custom-call | flops 1000000 | bytes 2228224 | tf_op jit(solution)/shard_map/turn/pallas_call | solution.py:351
  192.1 11.0 %collective-permute-done.24.refs_8_ = f32[17,128,128]{2,1,0:T(8,128)} collective-permute-done((f32[17,128,128]{2,1,0:T(8,128)}, f32[17,128,128]{2,1,0:T(8,128)}, u32[]{:S(2)}, u32[]{:S(2)}) %collective-permute-start.24) | collective-permute-done | bytes 1114144 | tf_op jit(solution)/shard_map/ppermute | solution.py:364
  203.1 0.8 copy-done.15
  204.1 50.4 %pair.1 = f32[16,128,128]{2,1,0:T(8,128)} custom-call(s32[1]{0:T(128)} %bitcast.2.sector_ref, s32[1]{0:T(128)} %bitcast.13.region_ref, s32[17]{0:T(128)} %class_ref.5, s32[1,3,32]{2,1,0:T(4,128)} %copy.53.live_ref, s32[4,17]{1,0:T(4,128)} %copy.54.out_ref, s32[20,11]{1,0:T(8,128)} %copy.55.block_ref, s32[20,11]{1,0:T(8,128)} %broadcast_add_fusion.place_ref, ...), custom_call_target="tpu_custom_call" | custom-call | flops 20000000000 | bytes 18000000 | tf_op jit(solution)/shard_map/pair/pallas_call | solution.py:321
  (93 shorter events, 15.6 us)
Async XLA Ops:
  0.6 25.6 %collective-permute-start = (f32[2,4,128,128]{3,2,1,0:T(8,128)}, f32[2,4,128,128]{3,2,1,0:T(8,128)S(1)}, u32[]{:S(2)}, u32[]{:S(2)}) collective-permute-start(f32[2,4,128,128]{3,2,1,0:T(8,128)} %bitcast.35), channel_id=1, source_target_pairs={{1,0},{2,1},{3,2},{4,3},{5,4},{6,5},{7,6},{8,7},{9,8},{10,9},{11,1... | collective-permute-start | bytes 1572872 | tf_op jit(solution)/shard_map/ppermute | solution.py:364
  4.5 21.7 %collective-permute-start.1 = (f32[2,4,128,128]{3,2,1,0:T(8,128)}, f32[2,4,128,128]{3,2,1,0:T(8,128)S(1)}, u32[]{:S(2)}, u32[]{:S(2)}) collective-permute-start(f32[2,4,128,128]{3,2,1,0:T(8,128)} %bitcast.36), channel_id=1, source_target_pairs={{0,1},{1,2},{2,3},{3,4},{4,5},{5,6},{6,7},{7,8},{8,9},{9,10},{10,1... | collective-permute-start | bytes 1572872 | tf_op jit(solution)/shard_map/ppermute | solution.py:364
  6.5 19.7 %collective-permute-start.2 = (f32[2,4,128,128]{3,2,1,0:T(8,128)}, f32[2,4,128,128]{3,2,1,0:T(8,128)}, u32[]{:S(2)}, u32[]{:S(2)}) collective-permute-start(f32[2,4,128,128]{3,2,1,0:T(8,128)} %bitcast.37), channel_id=1, source_target_pairs={{8,0},{9,1},{10,2},{11,3},{12,4},{13,5},{14,6},{15,7},{16,8},{17,9... | collective-permute-start | bytes 1572872 | tf_op jit(solution)/shard_map/ppermute | solution.py:364
  8.4 20.3 %collective-permute-start.3 = (f32[2,4,128,128]{3,2,1,0:T(8,128)}, f32[2,4,128,128]{3,2,1,0:T(8,128)}, u32[]{:S(2)}, u32[]{:S(2)}) collective-permute-start(f32[2,4,128,128]{3,2,1,0:T(8,128)} %bitcast.38), channel_id=1, source_target_pairs={{0,8},{1,9},{2,10},{3,11},{4,12},{5,13},{6,14},{7,15},{8,16},{9,17... | collective-permute-start | bytes 1572872 | tf_op jit(solution)/shard_map/ppermute | solution.py:364
  12.3 33.8 %collective-permute-start.17 = (f32[17,128,128]{2,1,0:T(8,128)}, f32[17,128,128]{2,1,0:T(8,128)S(1)}, u32[]{:S(2)}, u32[]{:S(2)}) collective-permute-start(f32[17,128,128]{2,1,0:T(8,128)} %bitcast.29), channel_id=1, source_target_pairs={{8,0},{9,1},{10,2},{11,3},{12,4},{13,5},{14,6},{15,7},{16,8},{17,9... | collective-permute-start | bytes 3342344 | tf_op jit(solution)/shard_map/ppermute | solution.py:364
  26.2 2.5 copy-start.13
  26.2 2.5 copy-start.14
  28.7 15.4 %copy-start.2 = (f32[1,16,1,128,128]{4,3,2,1,0:T(8,128)S(1)}, f32[1,16,1,128,128]{4,3,2,1,0:T(8,128)}, u32[]{:S(2)}) copy-start(f32[1,16,1,128,128]{4,3,2,1,0:T(8,128)} %param.14) | copy-start | bytes 3145732
  42.2 19.1 %collective-permute-start.5 = (f32[17,128,128]{2,1,0:T(8,128)}, f32[17,128,128]{2,1,0:T(8,128)S(1)}, u32[]{:S(2)}, u32[]{:S(2)}) collective-permute-start(f32[17,128,128]{2,1,0:T(8,128)} %get-tuple-element.28), channel_id=1, source_target_pairs={{0,1},{1,2},{2,3},{3,4},{4,5},{5,6},{6,7},{7,8},{8,9},{9,10},{10,1... | collective-permute-start | bytes 3342344 | tf_op jit(solution)/shard_map/ppermute | solution.py:364
  44.1 30.8 %collective-permute-start.10 = (f32[16,128,128]{2,1,0:T(8,128)S(1)}, f32[16,128,128]{2,1,0:T(8,128)S(1)}, u32[]{:S(2)}, u32[]{:S(2)}) collective-permute-start(f32[16,128,128]{2,1,0:T(8,128)S(1)} %bitcast.23), channel_id=1, source_target_pairs={{8,0},{9,1},{10,2},{11,3},{12,4},{13,5},{14,6},{15,7},{16,8},{17,9... | collective-permute-start | bytes 3145736 | tf_op jit(solution)/shard_map/ppermute | solution.py:364
  46.2 52.2 %copy-start = (f32[17,128,128]{2,1,0:T(8,128)}, f32[17,128,128]{2,1,0:T(8,128)S(1)}, u32[]{:S(2)}) copy-start(f32[17,128,128]{2,1,0:T(8,128)S(1)} %collective-permute-done.17.refs_3_) | copy-start | bytes 3342340
  46.2 49.1 %collective-permute-start.19 = (f32[17,128,128]{2,1,0:T(8,128)S(1)}, f32[17,128,128]{2,1,0:T(8,128)}, u32[]{:S(2)}, u32[]{:S(2)}) collective-permute-start(f32[17,128,128]{2,1,0:T(8,128)S(1)} %collective-permute-done.17.refs_3_), channel_id=1, source_target_pairs={{8,0},{9,1},{10,2},{11,3},{12,4},{13,5},{14,6},{15,7},{16,8},{17,9... | collective-permute-start | bytes 3342344 | tf_op jit(solution)/shard_map/ppermute | solution.py:364
  48.2 52.5 %collective-permute-start.4 = (f32[17,128,128]{2,1,0:T(8,128)}, f32[17,128,128]{2,1,0:T(8,128)}, u32[]{:S(2)}, u32[]{:S(2)}) collective-permute-start(f32[17,128,128]{2,1,0:T(8,128)} %get-tuple-element.26), channel_id=1, source_target_pairs={{0,1},{1,2},{2,3},{3,4},{4,5},{5,6},{6,7},{7,8},{8,9},{9,10},{10,1... | collective-permute-start | bytes 3342344 | tf_op jit(solution)/shard_map/ppermute | solution.py:364
  63.7 44.9 %collective-permute-start.6 = (f32[17,128,128]{2,1,0:T(8,128)}, f32[17,128,128]{2,1,0:T(8,128)}, u32[]{:S(2)}, u32[]{:S(2)}) collective-permute-start(f32[17,128,128]{2,1,0:T(8,128)} %add.155), channel_id=1, source_target_pairs={{0,8},{1,9},{2,10},{3,11},{4,12},{5,13},{6,14},{7,15},{8,16},{9,17... | collective-permute-start | bytes 3342344 | tf_op jit(solution)/shard_map/ppermute | solution.py:364
  67.5 63.4 %collective-permute-start.13 = (f32[16,128,128]{2,1,0:T(8,128)S(1)}, f32[16,128,128]{2,1,0:T(8,128)}, u32[]{:S(2)}, u32[]{:S(2)}) collective-permute-start(f32[16,128,128]{2,1,0:T(8,128)S(1)} %bitcast.24), channel_id=1, source_target_pairs={{0,8},{1,9},{2,10},{3,11},{4,12},{5,13},{6,14},{7,15},{8,16},{9,17... | collective-permute-start | bytes 3145736 | tf_op jit(solution)/shard_map/ppermute | solution.py:364
  74.9 3.4 %copy-start.8 = (f32[1,17,1,128,128]{4,3,2,1,0:T(8,128)S(1)}, f32[1,17,1,128,128]{4,3,2,1,0:T(8,128)}, u32[]{:S(2)}) copy-start(f32[1,17,1,128,128]{4,3,2,1,0:T(8,128)} %param.12) | copy-start | bytes 3342340
  74.9 3.3 %copy-start.3 = (f32[16,128,128]{2,1,0:T(8,128)}, f32[16,128,128]{2,1,0:T(8,128)S(1)}, u32[]{:S(2)}) copy-start(f32[16,128,128]{2,1,0:T(8,128)S(1)} %collective-permute-done.10) | copy-start | bytes 3145732
  74.9 58.2 %collective-permute-start.12 = (f32[16,128,128]{2,1,0:T(8,128)S(1)}, f32[16,128,128]{2,1,0:T(8,128)}, u32[]{:S(2)}, u32[]{:S(2)}) collective-permute-start(f32[16,128,128]{2,1,0:T(8,128)S(1)} %bitcast.25), channel_id=1, source_target_pairs={{0,1},{1,2},{2,3},{3,4},{4,5},{5,6},{6,7},{7,8},{8,9},{9,10},{10,1... | collective-permute-start | bytes 3145736 | tf_op jit(solution)/shard_map/ppermute | solution.py:364
  95.3 44.2 %collective-permute-start.11 = (f32[16,128,128]{2,1,0:T(8,128)}, f32[16,128,128]{2,1,0:T(8,128)S(1)}, u32[]{:S(2)}, u32[]{:S(2)}) collective-permute-start(f32[16,128,128]{2,1,0:T(8,128)} %broadcast_select_fusion.4), channel_id=1, source_target_pairs={{0,7},{1,0},{2,1},{3,2},{4,3},{5,4},{6,5},{7,6},{8,15},{9,8},{10,9... | collective-permute-start | bytes 3145736 | tf_op jit(solution)/shard_map/ppermute | solution.py:371
  100.7 52.8 %collective-permute-start.18 = (f32[17,128,128]{2,1,0:T(8,128)}, f32[17,128,128]{2,1,0:T(8,128)}, u32[]{:S(2)}, u32[]{:S(2)}) collective-permute-start(f32[17,128,128]{2,1,0:T(8,128)} %broadcast_select_fusion.3), channel_id=1, source_target_pairs={{0,7},{1,0},{2,1},{3,2},{4,3},{5,4},{6,5},{7,6},{8,15},{9,8},{10,9... | collective-permute-start | bytes 3342344 | tf_op jit(solution)/shard_map/ppermute | solution.py:371
  108.6 44.9 %collective-permute-start.20 = (f32[17,128,128]{2,1,0:T(8,128)}, f32[17,128,128]{2,1,0:T(8,128)S(1)}, u32[]{:S(2)}, u32[]{:S(2)}) collective-permute-start(f32[17,128,128]{2,1,0:T(8,128)} %broadcast_select_fusion.2), channel_id=1, source_target_pairs={{0,7},{1,0},{2,1},{3,2},{4,3},{5,4},{6,5},{7,6},{8,15},{9,8},{10,9... | collective-permute-start | bytes 3342344 | tf_op jit(solution)/shard_map/ppermute | solution.py:371
  108.6 24.3 %copy-start.11 = (s32[1,3,32]{2,0,1:T(1,128)S(1)}, s32[1,3,32]{2,0,1:T(1,128)}, u32[]{:S(2)}) copy-start(s32[1,3,32]{2,0,1:T(1,128)} %param.18) | copy-start | bytes 1156
  108.6 30.9 %copy-start.10 = (f32[1,2,17,17,4,4]{3,5,4,2,1,0:T(4,128)S(1)}, f32[1,2,17,17,4,4]{3,5,4,2,1,0:T(4,128)}, u32[]{:S(2)}) copy-start(f32[1,2,17,17,4,4]{3,5,4,2,1,0:T(4,128)} %param.16) | copy-start | bytes 110980
  131.0 22.5 %collective-permute-start.8 = (f32[17,128,128]{2,1,0:T(8,128)}, f32[17,128,128]{2,1,0:T(8,128)}, u32[]{:S(2)}, u32[]{:S(2)}) collective-permute-start(f32[17,128,128]{2,1,0:T(8,128)} %get-tuple-element.32), channel_id=1, source_target_pairs={{0,1},{1,2},{2,3},{3,4},{4,5},{5,6},{6,7},{7,8},{8,9},{9,10},{10,1... | collective-permute-start | bytes 3342344 | tf_op jit(solution)/shard_map/ppermute | solution.py:364
  133.1 32.8 %collective-permute-start.22 = (f32[17,128,128]{2,1,0:T(8,128)}, f32[17,128,128]{2,1,0:T(8,128)}, u32[]{:S(2)}, u32[]{:S(2)}) collective-permute-start(f32[17,128,128]{2,1,0:T(8,128)} %collective-permute-done.19.refs_6_), channel_id=1, source_target_pairs={{1,0},{2,1},{3,2},{4,3},{5,4},{6,5},{7,6},{8,7},{9,8},{10,9},{11,1... | collective-permute-start | bytes 3342344 | tf_op jit(solution)/shard_map/ppermute | solution.py:364
  139.5 1.0 copy-start.9
  140.5 30.2 %collective-permute-start.7 = (f32[17,128,128]{2,1,0:T(8,128)}, f32[17,128,128]{2,1,0:T(8,128)S(1)}, u32[]{:S(2)}, u32[]{:S(2)}) collective-permute-start(f32[17,128,128]{2,1,0:T(8,128)} %get-tuple-element.30), channel_id=1, source_target_pairs={{0,1},{1,2},{2,3},{3,4},{4,5},{5,6},{6,7},{7,8},{8,9},{9,10},{10,1... | collective-permute-start | bytes 3342344 | tf_op jit(solution)/shard_map/ppermute | solution.py:364
  153.5 14.8 %copy-start.1 = (f32[17,128,128]{2,1,0:T(8,128)}, f32[17,128,128]{2,1,0:T(8,128)S(1)}, u32[]{:S(2)}) copy-start(f32[17,128,128]{2,1,0:T(8,128)S(1)} %collective-permute-done.20.refs_4_) | copy-start | bytes 3342340
  155.7 19.1 %collective-permute-start.9 = (f32[9,128,128]{2,1,0:T(8,128)S(1)}, f32[9,128,128]{2,1,0:T(8,128)S(1)}, u32[]{:S(2)}, u32[]{:S(2)}) collective-permute-start(f32[9,128,128]{2,1,0:T(8,128)S(1)} %slice.63), channel_id=1, source_target_pairs={{0,8},{1,9},{2,10},{3,11},{4,12},{5,13},{6,14},{7,15},{8,16},{9,17... | collective-permute-start | bytes 1769480 | tf_op jit(solution)/shard_map/ppermute | solution.py:364
  160.6 31.5 %collective-permute-start.21 = (f32[17,128,128]{2,1,0:T(8,128)}, f32[17,128,128]{2,1,0:T(8,128)}, u32[]{:S(2)}, u32[]{:S(2)}) collective-permute-start(f32[17,128,128]{2,1,0:T(8,128)} %broadcast_select_fusion.1), channel_id=1, source_target_pairs={{0,7},{1,0},{2,1},{3,2},{4,3},{5,4},{6,5},{7,6},{8,15},{9,8},{10,9... | collective-permute-start | bytes 3342344 | tf_op jit(solution)/shard_map/ppermute | solution.py:371
  165.9 8.8 %copy-start.6 = (f32[17,128,128]{2,1,0:T(8,128)S(1)}, f32[17,128,128]{2,1,0:T(8,128)}, u32[]{:S(2)}) copy-start(f32[17,128,128]{2,1,0:T(8,128)} %get-tuple-element.29) | copy-start | bytes 3342340
  165.9 8.8 %copy-start.7 = (f32[17,128,128]{2,1,0:T(8,128)S(1)}, f32[17,128,128]{2,1,0:T(8,128)}, u32[]{:S(2)}) copy-start(f32[17,128,128]{2,1,0:T(8,128)} %get-tuple-element.33) | copy-start | bytes 3342340
  165.9 20.0 %collective-permute-start.14 = (f32[8,128,128]{2,1,0:T(8,128)S(1)}, f32[8,128,128]{2,1,0:T(8,128)S(1)}, u32[]{:S(2)}, u32[]{:S(2)}) collective-permute-start(f32[8,128,128]{2,1,0:T(8,128)S(1)} %slice.66), channel_id=1, source_target_pairs={{0,8},{1,9},{2,10},{3,11},{4,12},{5,13},{6,14},{7,15},{8,16},{9,17... | collective-permute-start | bytes 1572872 | tf_op jit(solution)/shard_map/ppermute | solution.py:364
  170.7 21.4 %collective-permute-start.23 = (f32[17,128,128]{2,1,0:T(8,128)}, f32[17,128,128]{2,1,0:T(8,128)}, u32[]{:S(2)}, u32[]{:S(2)}) collective-permute-start(f32[17,128,128]{2,1,0:T(8,128)} %broadcast_select_fusion), channel_id=1, source_target_pairs={{0,7},{1,0},{2,1},{3,2},{4,3},{5,4},{6,5},{7,6},{8,15},{9,8},{10,9... | collective-permute-start | bytes 3342344 | tf_op jit(solution)/shard_map/ppermute | solution.py:371
  170.7 32.4 %collective-permute-start.24 = (f32[17,128,128]{2,1,0:T(8,128)}, f32[17,128,128]{2,1,0:T(8,128)}, u32[]{:S(2)}, u32[]{:S(2)}) collective-permute-start(f32[17,128,128]{2,1,0:T(8,128)} %collective-permute-done.22.refs_7_), channel_id=1, source_target_pairs={{1,0},{2,1},{3,2},{4,3},{5,4},{6,5},{7,6},{8,7},{9,8},{10,9},{11,1... | collective-permute-start | bytes 3342344 | tf_op jit(solution)/shard_map/ppermute | solution.py:364
  174.9 11.1 %copy-start.4 = (f32[9,128,128]{2,1,0:T(8,128)}, f32[9,128,128]{2,1,0:T(8,128)S(1)}, u32[]{:S(2)}) copy-start(f32[9,128,128]{2,1,0:T(8,128)S(1)} %fusion.2.e0) | copy-start | bytes 1769476
  175.0 28.1 %collective-permute-start.15 = (f32[9,128,128]{2,1,0:T(8,128)S(1)}, f32[9,128,128]{2,1,0:T(8,128)S(1)}, u32[]{:S(2)}, u32[]{:S(2)}) collective-permute-start(f32[9,128,128]{2,1,0:T(8,128)S(1)} %fusion.2.e0), channel_id=1, source_target_pairs={{0,32},{32,64},{64,96},{1,33},{33,65},{65,97},{2,34},{34,66},{66,9... | collective-permute-start | bytes 1769480 | tf_op jit(solution)/shard_map/ppermute | solution.py:364
  186.1 3.5 %copy-start.5 = (f32[8,128,128]{2,1,0:T(8,128)}, f32[8,128,128]{2,1,0:T(8,128)S(1)}, u32[]{:S(2)}) copy-start(f32[8,128,128]{2,1,0:T(8,128)S(1)} %fusion.5.e1) | copy-start | bytes 1572868
  186.1 17.0 %collective-permute-start.16 = (f32[8,128,128]{2,1,0:T(8,128)S(1)}, f32[8,128,128]{2,1,0:T(8,128)S(1)}, u32[]{:S(2)}, u32[]{:S(2)}) collective-permute-start(f32[8,128,128]{2,1,0:T(8,128)S(1)} %fusion.5.e1), channel_id=1, source_target_pairs={{0,32},{32,64},{64,96},{1,33},{33,65},{65,97},{2,34},{34,66},{66,9... | collective-permute-start | bytes 1572872 | tf_op jit(solution)/shard_map/ppermute | solution.py:364
  203.1 0.8 copy-start.15
  203.1 1.0 copy-start.12

commit v5 on v3

--- a/solution.py
+++ b/solution.py
@@ -97,12 +97,13 @@
     if number == 0:
         env_ref, *refs = refs
     else:
-        low_ref, below_ref, above_ref, *refs = refs
+        low_ref, *below_refs = refs[:3]
+        above_refs, refs = refs[3:5], refs[5:]
     kets_refs, refs = refs[:5], refs[5:]
-    closed_refs, refs = refs[:4], refs[4:]
+    closed_hbm, refs = refs[:6], refs[6:]
     if number > 0:
         first_ref, *refs = refs
-    kets, product, bras, _ = refs
+    kets, product, bras, closed, sems = refs
     sector = sector_ref[0]
 
     for c, ref in enumerate(kets_refs):
@@ -117,36 +118,49 @@
     rows = lax.broadcasted_iota(jnp.int32, (TILE, TILE), 1)
     columns = lax.broadcasted_iota(jnp.int32, (TILE, TILE), 0)
 
-    def environment(w):
+    def environment(w, n):
         ket = sector + class_shift(class_ref[w])
         keep = inside(ket)
         if number == 0:
             return (env_ref[w] * keep).T
         count = jnp.where(keep > 0, live_ref[0, number - 1, jnp.clip(ket, 0, NSEC - 1)], 0)
         own = live_ref[0, number - 1, sector]
-        total = low_ref[w] + below_ref[w] + above_ref[w]
+        below = jnp.where(sector % ND == 0, 0.0, below_refs[n][w - CHUNKS[n][0]])
+        total = low_ref[w] + below + above_refs[n][w - CHUNKS[n][0]]
         total = jnp.where((rows < own) & (columns < count), total, 0.0)
         first_ref[w] = total
         return total
 
-    def form(w):
-        result = folded(dot(kets[class_ref[w]], stacked(environment(w))))
+    def form(n, w):
+        result = folded(dot(kets[class_ref[w]], stacked(environment(w, n))))
         product[pl.ds(4 * w, 4)] = result.reshape(4, TILE, TILE)
 
-    loop(0, NW, form, 1)
-
+    for n, (start, stop) in enumerate(CHUNKS):
+        loop(start, stop, functools.partial(form, n), 1)
+
+    copies = []
     for s in (3, 2, 1, 0):
 
         def close(terms, i):
             v = out_ref[s, i]
             total = mix(product, 0, block_ref, place_ref, rule_ref, v, class_ref[v], s, terms)
             result = folded(dot(jnp.concatenate(split(total), axis=1), bras[s]))
-            closed_refs[s][v] = result
+            closed[s, v] = result
 
         loop(0, LONG, functools.partial(close, LONG), UNROLL_LONG)
         loop(LONG, NW, functools.partial(close, SHORT), UNROLL_SHORT)
-
-
+        for start, stop in CHUNKS if s >= 2 else ((0, NW),):
+            n = len(copies)
+            copy = pltpu.make_async_copy(
+                closed.at[s, pl.ds(start, stop - start)], closed_hbm[n], sems.at[n]
+            )
+            copy.start()
+            copies.append(copy)
+    for copy in copies:
+        copy.wait()
+
+
+CHUNKS = ((0, 9), (9, NW))
 UNROLL_LONG = 11
 UNROLL_SHORT = 6
 SMEM_SPEC = pl.BlockSpec(memory_space=pltpu.SMEM)
@@ -155,20 +169,22 @@
 
 
 def site(number, scalars, envs, kets):
-    block = jax.ShapeDtypeStruct((NW, TILE, TILE), F32)
-    count = 4 if number == 0 else 5
+    sizes = [stop - start for start, stop in CHUNKS]
+    blocks = [jax.ShapeDtypeStruct((n, TILE, TILE), F32) for n in (*sizes, *sizes, NW, NW, NW)]
+    count = 6 if number == 0 else 7
     ket_spec = pl.BlockSpec((1, 4, TILE, TILE), lambda i: (number, 0, 0, 0))
     return pl.pallas_call(
         functools.partial(site_kernel, number),
         grid=(1,),
-        out_shape=[block] * count,
+        out_shape=blocks[:count],
         in_specs=[SMEM_SPEC] * 7 + [VMEM_SPEC] * len(envs) + [ket_spec] * 5,
-        out_specs=[VMEM_SPEC] * count,
+        out_specs=([HBM_SPEC] * 6 + [VMEM_SPEC])[:count],
         scratch_shapes=[
             pltpu.VMEM((5, 4 * TILE, 2 * TILE), BF16),
             pltpu.VMEM((4 * NW, TILE, TILE), F32),
             pltpu.VMEM((4, 2 * TILE, 2 * TILE), BF16),
-            pltpu.VMEM((2 * TILE, 2 * TILE), BF16),
+            pltpu.VMEM((4, NW, TILE, TILE), F32),
+            pltpu.SemaphoreType.DMA((6,)),
         ],
         compiler_params=pltpu.CompilerParams(vmem_limit_bytes=60 * 2**20),
         cost_estimate=pl.CostEstimate(flops=4 * 10**9, bytes_accessed=10**7, transcendentals=0),
@@ -371,6 +387,23 @@
     return lax.ppermute(given, "block", pairs)
 
 
+def fetch_before(blocks):
+    pairs = [(i, i // ND * ND + (i + 1) % ND) for i in range(NSEC)]
+    return lax.ppermute(blocks, "block", pairs)
+
+
+def moved(sector, h1, threes, twos):
+    below = []
+    above = []
+    for n, (lo, hi) in enumerate(CHUNKS):
+        three = fetch(threes[n], -1)
+        two = fetch_before(twos[n])
+        upper = h1[lo:hi] + three + jnp.where(sector[0] % ND == 0, two, 0.0)
+        below.append(two)
+        above.append(fetch(upper, -ND))
+    return below, above
+
+
 def flat_rule(rule):
     return jnp.pad(rule.reshape(RULE), (0, PADDED - RULE))
 
@@ -415,15 +448,13 @@
 
     tables = mix_tables(channel_class)
     scalars = (sector, channel_class, live_rows, *tables)
-    h0, h1, h2, h3 = site(0, (*scalars, flat_rule(mpo_sites[0, 0])), [start], near)
-    below3 = fetch(h3, -1)
-    below2 = fetch(h2, -1)
-    partial = fetch(h1 + below3, -ND)
-
-    h0, h1, h2, h3, first = site(1, (*scalars, flat_rule(mpo_sites[0, 1])), [h0, below2, partial], near)
-    below3 = fetch(h3, -1)
-    below2 = fetch(h2, -1)
-    upper = h1 + below3
+    *parts, h1, h0 = site(0, (*scalars, flat_rule(mpo_sites[0, 0])), [start], near)
+    below, above = moved(sector, h1, parts[:2], parts[2:])
+    second_rule, below[1] = lax.optimization_barrier((mpo_sites[0, 1], below[1]))
+    terms = [h0, *below, *above]
+    *parts, h1, h0, first = site(1, (*scalars, flat_rule(second_rule)), terms, near)
+    below, above = moved(sector, h1, parts[:2], parts[2:])
+    pair_rules, below[1] = lax.optimization_barrier((mpo_pair[0], below[1]))
     ket = sector + class_shift(channel_class)
     sectors = jnp.arange(NSEC, dtype=jnp.int32)
     width = jnp.arange(TILE, dtype=jnp.int32)
@@ -432,16 +463,16 @@
     keep = (width[:, None] < count[:, None, None]) & (width < own)
     parts = []
     passed = []
-    for lo, hi in ((0, 9), (9, NW)):
-        partial = fetch(upper[lo:hi], -ND)
-        second = jnp.where(keep[lo:hi], h0[lo:hi] + below2[lo:hi] + partial, 0.0)
+    for n, (lo, hi) in enumerate(CHUNKS):
+        under = jnp.where(sector[0] % ND == 0, 0.0, below[n])
+        second = jnp.where(keep[lo:hi], h0[lo:hi] + under + above[n], 0.0)
         second = jnp.where(region_sites[0] > 1, second, first[lo:hi])
         parts.append(second)
         passed.append(fetch(second, -1, "region"))
 
     environment = turned(parts)
     split = split_kets(sector, kets)
-    scalars = (sector, region, channel_class, live_rows, *tables, flat_rule(mpo_pair[0, 0]), flat_rule(mpo_pair[0, 1]))
+    scalars = (sector, region, channel_class, live_rows, *tables, flat_rule(pair_rules[0]), flat_rule(pair_rules[1]))
     images = pair(scalars, start, passed, split, [rights[u, d] for u in range(3) for d in range(3)])
     return environment[None, :, None], images[None, :, None]
 

time: 279 us -> 278 us (level)
  waiting for transfers between devices: 99.3 us -> 90.9 us
  starting transfers between devices: 60.2 us -> 67.3 us
    ppermute x20 -> x21, waiting for transfers between devices: 99.3 us -> 86.6 us  [fetch(): return lax.ppermute(blocks, axis, pairs)]
    ppermute x5, starting transfers between devices: 3.08 us -> 10.8 us  [fetch_next(): return lax.ppermute(given, 'block', pairs)]
    ppermute x0 -> x4, waiting for transfers between devices: none -> 4.31 us  [fetch_before(): return lax.ppermute(blocks, 'block', pairs)]
    ppermute x20 -> x21, starting transfers between devices: 57.1 us -> 56.5 us  [fetch(): return lax.ppermute(blocks, axis, pairs)]
  transfers between devices with their start and end apart: 25 -> 30, of which waited for: 10 -> 14; matrix products, arithmetic and copies ran while one was open for 11% -> 11% of each run, Pallas kernels for 13% -> 8%
where the time goes in v5:
time: 278 us; the launch traced here: 276 us
  waiting for transfers between devices  90.9 us (33%)
  Pallas kernels  84.2 us (30%)
  starting transfers between devices  67.3 us (24%)
  other arithmetic  16.6 us (6%)
  local copies, waits for them, and re-layouts  15.4 us (6%)
    ppermute x21, waiting for transfers between devices, fetch(): return lax.ppermute(blocks, axis, pairs)  86.6 us
    ppermute x21, starting transfers between devices, fetch(): return lax.ppermute(blocks, axis, pairs)  56.5 us
    pallas_call x1, Pallas kernels, pair(): pl.pallas_call(pair_kernel, out_shape=jax.ShapeDtypeStruct((16, TILE, TIL...  50.4 us
    pallas_call x2, Pallas kernels, site(): pl.pallas_call(functools.partial(site_kernel, number), grid=(1,), out_sha...  25.3 us
    ppermute x5, starting transfers between devices, fetch_next(): return lax.ppermute(given, 'block', pairs)  10.8 us
    pallas_call x1, Pallas kernels, split_kets(): pl.pallas_call(kets_kernel, grid=(4,), out_shape=jax.ShapeDtypeStruct((4,...  5.92 us
  transfers between devices with their start and end apart: 30, of which 14 were waited for; matrix products, arithmetic and copies ran while one was open for 11% of the time, Pallas kernels for 8%

profile of v5, /device:TPU:32, one launch (start us, length us, event | category | flops | bytes accessed | tf_op | source)
XLA Modules:
  0.0 276.5 jit_solution(15473649625923548742)
XLA Ops:
  0.6 3.9 %collective-permute-start = (f32[2,4,128,128]{3,2,1,0:T(8,128)}, f32[2,4,128,128]{3,2,1,0:T(8,128)S(1)}, u32[]{:S(2)}, u32[]{:S(2)}) collective-permute-start(f32[2,4,128,128]{3,2,1,0:T(8,128)} %bitcast.38), channel_id=1, source_target_pairs={{1,0},{2,1},{3,2},{4,3},{5,4},{6,5},{7,6},{8,7},{9,8},{10,9},{11,1... | collective-permute-start | bytes 1572872 | tf_op jit(solution)/shard_map/ppermute | solution.py:380
  4.5 1.9 collective-permute-start.1
  6.5 1.9 collective-permute-start.2
  8.4 3.9 %collective-permute-start.3 = (f32[2,4,128,128]{3,2,1,0:T(8,128)}, f32[2,4,128,128]{3,2,1,0:T(8,128)S(1)}, u32[]{:S(2)}, u32[]{:S(2)}) collective-permute-start(f32[2,4,128,128]{3,2,1,0:T(8,128)} %bitcast.41), channel_id=1, source_target_pairs={{0,8},{1,9},{2,10},{3,11},{4,12},{5,13},{6,14},{7,15},{8,16},{9,17... | collective-permute-start | bytes 1572872 | tf_op jit(solution)/shard_map/ppermute | solution.py:380
  23.5 5.1 %collective-permute-done.3.refs_5_.refs_9_ = f32[2,4,128,128]{3,2,1,0:T(8,128)S(1)} collective-permute-done((f32[2,4,128,128]{3,2,1,0:T(8,128)}, f32[2,4,128,128]{3,2,1,0:T(8,128)S(1)}, u32[]{:S(2)}, u32[]{:S(2)}) %collective-permute-start.3) | collective-permute-done | bytes 524320 | tf_op jit(solution)/shard_map/ppermute | solution.py:380
  29.4 12.6 %shard_map.122 = (f32[9,128,128]{2,1,0:T(8,128)}, f32[8,128,128]{2,1,0:T(8,128)}, f32[9,128,128]{2,1,0:T(8,128)}, f32[8,128,128]{2,1,0:T(8,128)}, f32[17,128,128]{2,1,0:T(8,128)}, /*index=5*/f32[17,128,128]{2,1,0:T(8,128)}) custom-call(s32[1]{0:T(128)} %bitcast.2.sector_ref, s32[17]{0:T(128)} %class_ref.5, s32[1,3,32]{2,1,0:T(4,128)} %copy.53.live_ref, ...), custom_call_target="tpu_custom_call" | custom-call | flops 4000000000 | bytes 10000000 | tf_op jit(solution)/shard_map/pallas_call | solution.py:176
  42.1 1.9 collective-permute-start.8
  44.0 2.3 collective-permute-start.22
  46.4 1.9 collective-permute-start.6
  48.3 3.7 %collective-permute-done.4.refs_2_ = f32[8,128,128]{2,1,0:T(8,128)S(1)} collective-permute-done((f32[8,128,128]{2,1,0:T(8,128)}, f32[8,128,128]{2,1,0:T(8,128)S(1)}, u32[]{:S(2)}, u32[]{:S(2)}) %collective-permute-start.4) | collective-permute-done | bytes 524320 | tf_op jit(solution)/shard_map/ppermute | solution.py:392
  52.9 1.9 collective-permute-start.18
  54.8 2.1 collective-permute-done.8
  56.9 2.3 select_add_fusion.3
  59.1 4.4 %collective-permute-start.9 = (f32[8,128,128]{2,1,0:T(8,128)}, f32[8,128,128]{2,1,0:T(8,128)}, u32[]{:S(2)}, u32[]{:S(2)}) collective-permute-start(f32[8,128,128]{2,1,0:T(8,128)} %select_add_fusion.3), channel_id=1, source_target_pairs={{0,8},{1,9},{2,10},{3,11},{4,12},{5,13},{6,14},{7,15},{8,16},{9,17... | collective-permute-start | bytes 1572872 | tf_op jit(solution)/shard_map/ppermute | solution.py:380
  64.1 5.5 %collective-permute-done.6 = f32[9,128,128]{2,1,0:T(8,128)} collective-permute-done((f32[9,128,128]{2,1,0:T(8,128)}, f32[9,128,128]{2,1,0:T(8,128)}, u32[]{:S(2)}, u32[]{:S(2)}) %collective-permute-start.6) | collective-permute-done | bytes 589856 | tf_op jit(solution)/shard_map/ppermute | solution.py:380
  69.6 2.2 select_add_fusion.1
  71.8 4.3 %collective-permute-start.7 = (f32[9,128,128]{2,1,0:T(8,128)}, f32[9,128,128]{2,1,0:T(8,128)}, u32[]{:S(2)}, u32[]{:S(2)}) collective-permute-start(f32[9,128,128]{2,1,0:T(8,128)} %select_add_fusion.1), channel_id=1, source_target_pairs={{0,8},{1,9},{2,10},{3,11},{4,12},{5,13},{6,14},{7,15},{8,16},{9,17... | collective-permute-start | bytes 1769480 | tf_op jit(solution)/shard_map/ppermute | solution.py:380
  76.1 2.5 collective-permute-start.24
  79.6 1.3 copy.52
  80.9 1.6 reshape.396
  83.1 8.2 %collective-permute-done.7.refs_3_ = f32[9,128,128]{2,1,0:T(8,128)} collective-permute-done((f32[9,128,128]{2,1,0:T(8,128)}, f32[9,128,128]{2,1,0:T(8,128)}, u32[]{:S(2)}, u32[]{:S(2)}) %collective-permute-start.7) | collective-permute-done | bytes 589856 | tf_op jit(solution)/shard_map/ppermute | solution.py:380
  91.3 12.7 %shard_map.123 = (f32[9,128,128]{2,1,0:T(8,128)}, f32[8,128,128]{2,1,0:T(8,128)}, f32[9,128,128]{2,1,0:T(8,128)}, f32[8,128,128]{2,1,0:T(8,128)}, f32[17,128,128...) custom-call(s32[1]{0:T(128)} %bitcast.2.sector_ref, s32[17]{0:T(128)} %class_ref.5, ...), custom_call_target="tpu_custom_call" | custom-call | flops 4000000000 | bytes 10000000 | tf_op jit(solution)/shard_map/pallas_call | solution.py:176
  104.2 4.2 %collective-permute-start.23 = (f32[17,128,128]{2,1,0:T(8,128)S(1)}, f32[17,128,128]{2,1,0:T(8,128)S(1)}, u32[]{:S(2)}, u32[]{:S(2)}) collective-permute-start(f32[17,128,128]{2,1,0:T(8,128)S(1)} %broadcast_select_fusion.3), channel_id=1, source_target_pairs={{0,7},{1,0},{2,1},{3,2},{4,3},{5,4},{6,5},{7,6},{8,15},{9,8},{10,9... | collective-permute-start | bytes 3342344 | tf_op jit(solution)/shard_map/ppermute | solution.py:387
  108.4 10.8 %collective-permute-done.24.refs_6_ = f32[17,128,128]{2,1,0:T(8,128)} collective-permute-done((f32[17,128,128]{2,1,0:T(8,128)S(1)}, f32[17,128,128]{2,1,0:T(8,128)}, u32[]{:S(2)}, u32[]{:S(2)}) %collective-permute-start.24) | collective-permute-done | bytes 1114144 | tf_op jit(solution)/shard_map/ppermute | solution.py:380
  119.2 2.0 collective-permute-start.14
  121.3 1.4 broadcast_select_fusion.2
  122.7 1.9 collective-permute-start.11
  124.7 4.1 %collective-permute-start.25 = (f32[17,128,128]{2,1,0:T(8,128)S(1)}, f32[17,128,128]{2,1,0:T(8,128)S(1)}, u32[]{:S(2)}, u32[]{:S(2)}) collective-permute-start(f32[17,128,128]{2,1,0:T(8,128)S(1)} %broadcast_select_fusion.2), channel_id=1, source_target_pairs={{0,7},{1,0},{2,1},{3,2},{4,3},{5,4},{6,5},{7,6},{8,15},{9,8},{10,9... | collective-permute-start | bytes 3342344 | tf_op jit(solution)/shard_map/ppermute | solution.py:387
  130.6 1.4 collective-permute-done.14
  132.0 1.9 collective-permute-start.27
  134.1 2.4 collective-permute-start.20
  136.5 1.8 collective-permute-done.11
  138.3 3.6 %collective-permute-start.21 = (f32[16,128,128]{2,1,0:T(8,128)S(1)}, f32[16,128,128]{2,1,0:T(8,128)S(1)}, u32[]{:S(2)}, u32[]{:S(2)}) collective-permute-start(f32[16,128,128]{2,1,0:T(8,128)S(1)} %bitcast.29), channel_id=1, source_target_pairs={{0,8},{1,9},{2,10},{3,11},{4,12},{5,13},{6,14},{7,15},{8,16},{9,17... | collective-permute-start | bytes 3145736 | tf_op jit(solution)/shard_map/ppermute | solution.py:380
  143.3 2.2 collective-permute-start.12
  145.7 8.2 %collective-permute-done.27.refs_7_ = f32[17,128,128]{2,1,0:T(8,128)} collective-permute-done((f32[17,128,128]{2,1,0:T(8,128)}, f32[17,128,128]{2,1,0:T(8,128)}, u32[]{:S(2)}, u32[]{:S(2)}) %collective-permute-start.27) | collective-permute-done | bytes 1114144 | tf_op jit(solution)/shard_map/ppermute | solution.py:380
  153.9 1.9 collective-permute-start.15
  155.8 2.4 broadcast_select_fusion
  158.2 1.3 collective-permute-start.26
  159.6 15.3 %collective-permute-done.21 = f32[16,128,128]{2,1,0:T(8,128)S(1)} collective-permute-done((f32[16,128,128]{2,1,0:T(8,128)S(1)}, f32[16,128,128]{2,1,0:T(8,128)S(1)}, u32[]{:S(2)}, u32[]{:S(2)}) %collective-permute-start.21) | collective-permute-done | bytes 1048608 | tf_op jit(solution)/shard_map/ppermute | solution.py:380
  174.9 12.6 %collective-permute-done.12 = f32[9,128,128]{2,1,0:T(8,128)S(1)} collective-permute-done((f32[9,128,128]{2,1,0:T(8,128)S(1)}, f32[9,128,128]{2,1,0:T(8,128)S(1)}, u32[]{:S(2)}, u32[]{:S(2)}) %collective-permute-start.12) | collective-permute-done | bytes 589856 | tf_op jit(solution)/shard_map/ppermute | solution.py:380
  187.5 1.9 collective-permute-start.29
  189.6 8.9 %collective-permute-done.15 = f32[8,128,128]{2,1,0:T(8,128)S(1)} collective-permute-done((f32[8,128,128]{2,1,0:T(8,128)S(1)}, f32[8,128,128]{2,1,0:T(8,128)S(1)}, u32[]{:S(2)}, u32[]{:S(2)}) %collective-permute-start.15) | collective-permute-done | bytes 524320 | tf_op jit(solution)/shard_map/ppermute | solution.py:380
  198.6 4.2 %collective-permute-start.16 = (f32[9,128,128]{2,1,0:T(8,128)S(1)}, f32[9,128,128]{2,1,0:T(8,128)}, u32[]{:S(2)}, u32[]{:S(2)}) collective-permute-start(f32[9,128,128]{2,1,0:T(8,128)S(1)} %slice_select_fusion.e0), channel_id=1, source_target_pairs={{0,32},{32,64},{64,96},{1,33},{33,65},{65,97},{2,34},{34,66},{66,9... | collective-permute-start | bytes 1769480 | tf_op jit(solution)/shard_map/ppermute | solution.py:380
  204.0 3.3 %collective-permute-start.17 = (f32[8,128,128]{2,1,0:T(8,128)S(1)}, f32[8,128,128]{2,1,0:T(8,128)}, u32[]{:S(2)}, u32[]{:S(2)}) collective-permute-start(f32[8,128,128]{2,1,0:T(8,128)S(1)} %slice_select_fusion.1.e1), channel_id=1, source_target_pairs={{0,32},{32,64},{64,96},{1,33},{33,65},{65,97},{2,34},{34,66},{66,9... | collective-permute-start | bytes 1572872 | tf_op jit(solution)/shard_map/ppermute | solution.py:380
  207.3 5.9 %split_kets.1.kets_hbm = bf16[4,5,512,256]{3,2,1,0:T(8,128)(2,1)} custom-call(s32[1]{0:T(128)} %bitcast.2.sector_ref, f32[4,4,128,128]{3,2,1,0:T(8,128)} %bitcast.25, f32[4,4,128,128]{3,2,1,0:T(8,128)} %bitcast.34, f32[4,4,128,128]{3,2,1,0:T(8,128)} %bitcast.32, f32[4,4,128,128]{3,2,1,0:T(8,128)} %bitcast.30, f32[4,4,128,128]{3,2,1,0:T(8,128)} %bitcast.33), custom_call_target="tpu_custom_call" | custom-call | flops 5000000 | bytes 10000000 | tf_op jit(solution)/shard_map/split_kets/pallas_call | solution.py:206
  216.6 2.6 turn.1
  219.2 6.7 %collective-permute-done.17.passed1_ref = f32[8,128,128]{2,1,0:T(8,128)} collective-permute-done((f32[8,128,128]{2,1,0:T(8,128)S(1)}, f32[8,128,128]{2,1,0:T(8,128)}, u32[]{:S(2)}, u32[]{:S(2)}) %collective-permute-start.17) | collective-permute-done | bytes 524320 | tf_op jit(solution)/shard_map/ppermute | solution.py:380
  225.9 50.4 %pair.1 = f32[16,128,128]{2,1,0:T(8,128)} custom-call(s32[1]{0:T(128)} %bitcast.2.sector_ref, s32[1]{0:T(128)} %bitcast.9.region_ref, s32[17]{0:T(128)} %class_ref.5, s32[1,3,32]{2,1,0:T(4,128)} %copy.53.live_ref, s32[4,17]{1,0:T(4,128)} %copy.54.out_ref, s32[20,11]{1,0:T(8,128)} %copy.55.block_ref, s32[20,11]{1,0:T(8,128)} %broadcast_add_fusion.place_ref, ...), custom_call_target="tpu_custom_call" | custom-call | flops 20000000000 | bytes 18000000 | tf_op jit(solution)/shard_map/pair/pallas_call | solution.py:337
  (119 shorter events, 22.5 us)
Async XLA Ops:
  0.6 22.8 %collective-permute-start = (f32[2,4,128,128]{3,2,1,0:T(8,128)}, f32[2,4,128,128]{3,2,1,0:T(8,128)S(1)}, u32[]{:S(2)}, u32[]{:S(2)}) collective-permute-start(f32[2,4,128,128]{3,2,1,0:T(8,128)} %bitcast.38), channel_id=1, source_target_pairs={{1,0},{2,1},{3,2},{4,3},{5,4},{6,5},{7,6},{8,7},{9,8},{10,9},{11,1... | collective-permute-start | bytes 1572872 | tf_op jit(solution)/shard_map/ppermute | solution.py:380
  4.5 18.9 %collective-permute-start.1 = (f32[2,4,128,128]{3,2,1,0:T(8,128)}, f32[2,4,128,128]{3,2,1,0:T(8,128)S(1)}, u32[]{:S(2)}, u32[]{:S(2)}) collective-permute-start(f32[2,4,128,128]{3,2,1,0:T(8,128)} %bitcast.39), channel_id=1, source_target_pairs={{0,1},{1,2},{2,3},{3,4},{4,5},{5,6},{6,7},{7,8},{8,9},{9,10},{10,1... | collective-permute-start | bytes 1572872 | tf_op jit(solution)/shard_map/ppermute | solution.py:380
  6.5 17.0 %collective-permute-start.2 = (f32[2,4,128,128]{3,2,1,0:T(8,128)}, f32[2,4,128,128]{3,2,1,0:T(8,128)S(1)}, u32[]{:S(2)}, u32[]{:S(2)}) collective-permute-start(f32[2,4,128,128]{3,2,1,0:T(8,128)} %bitcast.40), channel_id=1, source_target_pairs={{8,0},{9,1},{10,2},{11,3},{12,4},{13,5},{14,6},{15,7},{16,8},{17,9... | collective-permute-start | bytes 1572872 | tf_op jit(solution)/shard_map/ppermute | solution.py:380
  8.4 20.2 %collective-permute-start.3 = (f32[2,4,128,128]{3,2,1,0:T(8,128)}, f32[2,4,128,128]{3,2,1,0:T(8,128)S(1)}, u32[]{:S(2)}, u32[]{:S(2)}) collective-permute-start(f32[2,4,128,128]{3,2,1,0:T(8,128)} %bitcast.41), channel_id=1, source_target_pairs={{0,8},{1,9},{2,10},{3,11},{4,12},{5,13},{6,14},{7,15},{8,16},{9,17... | collective-permute-start | bytes 1572872 | tf_op jit(solution)/shard_map/ppermute | solution.py:380
  23.4 5.2 %copy-start.19 = (f32[2,4,128,128]{3,2,1,0:T(8,128)}, f32[2,4,128,128]{3,2,1,0:T(8,128)S(1)}, u32[]{:S(2)}) copy-start(f32[2,4,128,128]{3,2,1,0:T(8,128)S(1)} %collective-permute-done.refs_2_.refs_6_) | copy-start | bytes 1572868
  23.5 5.2 %copy-start.20 = (f32[2,4,128,128]{3,2,1,0:T(8,128)}, f32[2,4,128,128]{3,2,1,0:T(8,128)S(1)}, u32[]{:S(2)}) copy-start(f32[2,4,128,128]{3,2,1,0:T(8,128)S(1)} %collective-permute-done.1.refs_3_.refs_7_) | copy-start | bytes 1572868
  23.5 5.1 %copy-start.21 = (f32[2,4,128,128]{3,2,1,0:T(8,128)}, f32[2,4,128,128]{3,2,1,0:T(8,128)S(1)}, u32[]{:S(2)}) copy-start(f32[2,4,128,128]{3,2,1,0:T(8,128)S(1)} %collective-permute-done.2.refs_4_.refs_8_) | copy-start | bytes 1572868
  29.4 23.5 %copy-start.2 = (f32[1,16,1,128,128]{4,3,2,1,0:T(8,128)S(1)}, f32[1,16,1,128,128]{4,3,2,1,0:T(8,128)}, u32[]{:S(2)}) copy-start(f32[1,16,1,128,128]{4,3,2,1,0:T(8,128)} %param.14) | copy-start | bytes 3145732
  42.0 10.0 %collective-permute-start.4 = (f32[8,128,128]{2,1,0:T(8,128)}, f32[8,128,128]{2,1,0:T(8,128)S(1)}, u32[]{:S(2)}, u32[]{:S(2)}) collective-permute-start(f32[8,128,128]{2,1,0:T(8,128)} %get-tuple-element.29), channel_id=1, source_target_pairs={{0,1},{1,2},{2,3},{3,4},{4,5},{5,6},{6,7},{7,0},{8,9},{9,10},{10,1... | collective-permute-start | bytes 1572872 | tf_op jit(solution)/shard_map/ppermute | solution.py:392
  42.1 14.8 %collective-permute-start.8 = (f32[8,128,128]{2,1,0:T(8,128)}, f32[8,128,128]{2,1,0:T(8,128)}, u32[]{:S(2)}, u32[]{:S(2)}) collective-permute-start(f32[8,128,128]{2,1,0:T(8,128)} %get-tuple-element.36), channel_id=1, source_target_pairs={{0,1},{1,2},{2,3},{3,4},{4,5},{5,6},{6,7},{7,8},{8,9},{9,10},{10,1... | collective-permute-start | bytes 1572872 | tf_op jit(solution)/shard_map/ppermute | solution.py:380
  44.0 32.1 %collective-permute-start.22 = (f32[17,128,128]{2,1,0:T(8,128)}, f32[17,128,128]{2,1,0:T(8,128)S(1)}, u32[]{:S(2)}, u32[]{:S(2)}) collective-permute-start(f32[17,128,128]{2,1,0:T(8,128)} %bitcast.16.refs_0_), channel_id=1, source_target_pairs={{8,0},{9,1},{10,2},{11,3},{12,4},{13,5},{14,6},{15,7},{16,8},{17,9... | collective-permute-start | bytes 3342344 | tf_op jit(solution)/shard_map/ppermute | solution.py:380
  46.3 17.8 %collective-permute-start.5 = (f32[9,128,128]{2,1,0:T(8,128)}, f32[9,128,128]{2,1,0:T(8,128)}, u32[]{:S(2)}, u32[]{:S(2)}) collective-permute-start(f32[9,128,128]{2,1,0:T(8,128)} %get-tuple-element.32), channel_id=1, source_target_pairs={{0,1},{1,2},{2,3},{3,4},{4,5},{5,6},{6,7},{7,0},{8,9},{9,10},{10,1... | collective-permute-start | bytes 1769480 | tf_op jit(solution)/shard_map/ppermute | solution.py:392
  46.4 23.2 %collective-permute-start.6 = (f32[9,128,128]{2,1,0:T(8,128)}, f32[9,128,128]{2,1,0:T(8,128)}, u32[]{:S(2)}, u32[]{:S(2)}) collective-permute-start(f32[9,128,128]{2,1,0:T(8,128)} %get-tuple-element.35), channel_id=1, source_target_pairs={{0,1},{1,2},{2,3},{3,4},{4,5},{5,6},{6,7},{7,8},{8,9},{9,10},{10,1... | collective-permute-start | bytes 1769480 | tf_op jit(solution)/shard_map/ppermute | solution.py:380
  48.3 21.3 %copy-start.7 = (f32[17,128,128]{2,1,0:T(8,128)S(1)}, f32[17,128,128]{2,1,0:T(8,128)}, u32[]{:S(2)}) copy-start(f32[17,128,128]{2,1,0:T(8,128)} %get-tuple-element.34) | copy-start | bytes 3342340
  52.9 69.8 %collective-permute-start.18 = (f32[16,128,128]{2,1,0:T(8,128)S(1)}, f32[16,128,128]{2,1,0:T(8,128)S(1)}, u32[]{:S(2)}, u32[]{:S(2)}) collective-permute-start(f32[16,128,128]{2,1,0:T(8,128)S(1)} %bitcast.26), channel_id=1, source_target_pairs={{8,0},{9,1},{10,2},{11,3},{12,4},{13,5},{14,6},{15,7},{16,8},{17,9... | collective-permute-start | bytes 3145736 | tf_op jit(solution)/shard_map/ppermute | solution.py:380
  59.1 16.9 %copy-start.16 = (s32[1,3,32]{2,0,1:T(1,128)S(1)}, s32[1,3,32]{2,0,1:T(1,128)}, u32[]{:S(2)}) copy-start(s32[1,3,32]{2,0,1:T(1,128)} %param.18) | copy-start | bytes 1156
  59.1 24.0 %collective-permute-start.9 = (f32[8,128,128]{2,1,0:T(8,128)}, f32[8,128,128]{2,1,0:T(8,128)}, u32[]{:S(2)}, u32[]{:S(2)}) collective-permute-start(f32[8,128,128]{2,1,0:T(8,128)} %select_add_fusion.3), channel_id=1, source_target_pairs={{0,8},{1,9},{2,10},{3,11},{4,12},{5,13},{6,14},{7,15},{8,16},{9,17... | collective-permute-start | bytes 1572872 | tf_op jit(solution)/shard_map/ppermute | solution.py:380
  71.8 19.5 %collective-permute-start.7 = (f32[9,128,128]{2,1,0:T(8,128)}, f32[9,128,128]{2,1,0:T(8,128)}, u32[]{:S(2)}, u32[]{:S(2)}) collective-permute-start(f32[9,128,128]{2,1,0:T(8,128)} %select_add_fusion.1), channel_id=1, source_target_pairs={{0,8},{1,9},{2,10},{3,11},{4,12},{5,13},{6,14},{7,15},{8,16},{9,17... | collective-permute-start | bytes 1769480 | tf_op jit(solution)/shard_map/ppermute | solution.py:380
  76.1 45.2 %copy-start = (f32[17,128,128]{2,1,0:T(8,128)}, f32[17,128,128]{2,1,0:T(8,128)S(1)}, u32[]{:S(2)}) copy-start(f32[17,128,128]{2,1,0:T(8,128)S(1)} %collective-permute-done.22.refs_3_) | copy-start | bytes 3342340
  76.1 43.1 %collective-permute-start.24 = (f32[17,128,128]{2,1,0:T(8,128)S(1)}, f32[17,128,128]{2,1,0:T(8,128)}, u32[]{:S(2)}, u32[]{:S(2)}) collective-permute-start(f32[17,128,128]{2,1,0:T(8,128)S(1)} %collective-permute-done.22.refs_3_), channel_id=1, source_target_pairs={{8,0},{9,1},{10,2},{11,3},{12,4},{13,5},{14,6},{15,7},{16,8},{17,9... | collective-permute-start | bytes 3342344 | tf_op jit(solution)/shard_map/ppermute | solution.py:380
  104.1 15.2 %copy-start.23 = (f32[8,128,128]{2,1,0:T(8,128)S(1)}, f32[8,128,128]{2,1,0:T(8,128)}, u32[]{:S(2)}) copy-start(f32[8,128,128]{2,1,0:T(8,128)} %get-tuple-element.44) | copy-start | bytes 1572868
  104.1 20.6 %collective-permute-start.13 = (f32[8,128,128]{2,1,0:T(8,128)}, f32[8,128,128]{2,1,0:T(8,128)S(1)}, u32[]{:S(2)}, u32[]{:S(2)}) collective-permute-start(f32[8,128,128]{2,1,0:T(8,128)} %get-tuple-element.42), channel_id=1, source_target_pairs={{0,1},{1,2},{2,3},{3,4},{4,5},{5,6},{6,7},{7,0},{8,9},{9,10},{10,1... | collective-permute-start | bytes 1572872 | tf_op jit(solution)/shard_map/ppermute | solution.py:392
  104.2 37.9 %collective-permute-start.23 = (f32[17,128,128]{2,1,0:T(8,128)S(1)}, f32[17,128,128]{2,1,0:T(8,128)S(1)}, u32[]{:S(2)}, u32[]{:S(2)}) collective-permute-start(f32[17,128,128]{2,1,0:T(8,128)S(1)} %broadcast_select_fusion.3), channel_id=1, source_target_pairs={{0,7},{1,0},{2,1},{3,2},{4,3},{5,4},{6,5},{7,6},{8,15},{9,8},{10,9... | collective-permute-start | bytes 3342344 | tf_op jit(solution)/shard_map/ppermute | solution.py:387
  108.4 25.6 %collective-permute-start.10 = (f32[9,128,128]{2,1,0:T(8,128)S(1)}, f32[9,128,128]{2,1,0:T(8,128)S(1)}, u32[]{:S(2)}, u32[]{:S(2)}) collective-permute-start(f32[9,128,128]{2,1,0:T(8,128)S(1)} %copy-done.18), channel_id=1, source_target_pairs={{0,1},{1,2},{2,3},{3,4},{4,5},{5,6},{6,7},{7,0},{8,9},{9,10},{10,1... | collective-permute-start | bytes 1769480 | tf_op jit(solution)/shard_map/ppermute | solution.py:392
  119.2 12.7 %collective-permute-start.14 = (f32[8,128,128]{2,1,0:T(8,128)S(1)}, f32[8,128,128]{2,1,0:T(8,128)S(1)}, u32[]{:S(2)}, u32[]{:S(2)}) collective-permute-start(f32[8,128,128]{2,1,0:T(8,128)S(1)} %copy-done.23), channel_id=1, source_target_pairs={{0,1},{1,2},{2,3},{3,4},{4,5},{5,6},{6,7},{7,8},{8,9},{9,10},{10,1... | collective-permute-start | bytes 1572872 | tf_op jit(solution)/shard_map/ppermute | solution.py:380
  122.7 11.3 %copy-start.3 = (f32[16,128,128]{2,1,0:T(8,128)}, f32[16,128,128]{2,1,0:T(8,128)S(1)}, u32[]{:S(2)}) copy-start(f32[16,128,128]{2,1,0:T(8,128)S(1)} %collective-permute-done.18) | copy-start | bytes 3145732
  122.7 15.5 %collective-permute-start.11 = (f32[9,128,128]{2,1,0:T(8,128)S(1)}, f32[9,128,128]{2,1,0:T(8,128)S(1)}, u32[]{:S(2)}, u32[]{:S(2)}) collective-permute-start(f32[9,128,128]{2,1,0:T(8,128)S(1)} %copy-done.17), channel_id=1, source_target_pairs={{0,1},{1,2},{2,3},{3,4},{4,5},{5,6},{6,7},{7,8},{8,9},{9,10},{10,1... | collective-permute-start | bytes 1769480 | tf_op jit(solution)/shard_map/ppermute | solution.py:380
  124.7 18.7 %collective-permute-start.25 = (f32[17,128,128]{2,1,0:T(8,128)S(1)}, f32[17,128,128]{2,1,0:T(8,128)S(1)}, u32[]{:S(2)}, u32[]{:S(2)}) collective-permute-start(f32[17,128,128]{2,1,0:T(8,128)S(1)} %broadcast_select_fusion.2), channel_id=1, source_target_pairs={{0,7},{1,0},{2,1},{3,2},{4,3},{5,4},{6,5},{7,6},{8,15},{9,8},{10,9... | collective-permute-start | bytes 3342344 | tf_op jit(solution)/shard_map/ppermute | solution.py:387
  130.6 11.3 %copy-start.6 = (f32[17,128,128]{2,1,0:T(8,128)S(1)}, f32[17,128,128]{2,1,0:T(8,128)}, u32[]{:S(2)}) copy-start(f32[17,128,128]{2,1,0:T(8,128)} %get-tuple-element.39) | copy-start | bytes 3342340
  132.0 21.9 %collective-permute-start.27 = (f32[17,128,128]{2,1,0:T(8,128)}, f32[17,128,128]{2,1,0:T(8,128)}, u32[]{:S(2)}, u32[]{:S(2)}) collective-permute-start(f32[17,128,128]{2,1,0:T(8,128)} %collective-permute-done.24.refs_6_), channel_id=1, source_target_pairs={{1,0},{2,1},{3,2},{4,3},{5,4},{6,5},{7,6},{8,7},{9,8},{10,9},{11,1... | collective-permute-start | bytes 3342344 | tf_op jit(solution)/shard_map/ppermute | solution.py:380
  134.1 24.2 %collective-permute-start.20 = (f32[16,128,128]{2,1,0:T(8,128)S(1)}, f32[16,128,128]{2,1,0:T(8,128)S(1)}, u32[]{:S(2)}, u32[]{:S(2)}) collective-permute-start(f32[16,128,128]{2,1,0:T(8,128)S(1)} %bitcast.28), channel_id=1, source_target_pairs={{0,1},{1,2},{2,3},{3,4},{4,5},{5,6},{6,7},{7,8},{8,9},{9,10},{10,1... | collective-permute-start | bytes 3145736 | tf_op jit(solution)/shard_map/ppermute | solution.py:380
  138.3 36.6 %collective-permute-start.21 = (f32[16,128,128]{2,1,0:T(8,128)S(1)}, f32[16,128,128]{2,1,0:T(8,128)S(1)}, u32[]{:S(2)}, u32[]{:S(2)}) collective-permute-start(f32[16,128,128]{2,1,0:T(8,128)S(1)} %bitcast.29), channel_id=1, source_target_pairs={{0,8},{1,9},{2,10},{3,11},{4,12},{5,13},{6,14},{7,15},{8,16},{9,17... | collective-permute-start | bytes 3145736 | tf_op jit(solution)/shard_map/ppermute | solution.py:380
  142.2 60.7 %collective-permute-start.19 = (f32[16,128,128]{2,1,0:T(8,128)S(1)}, f32[16,128,128]{2,1,0:T(8,128)S(1)}, u32[]{:S(2)}, u32[]{:S(2)}) collective-permute-start(f32[16,128,128]{2,1,0:T(8,128)S(1)} %broadcast_select_fusion.4), channel_id=1, source_target_pairs={{0,7},{1,0},{2,1},{3,2},{4,3},{5,4},{6,5},{7,6},{8,15},{9,8},{10,9... | collective-permute-start | bytes 3145736 | tf_op jit(solution)/shard_map/ppermute | solution.py:387
  143.3 12.5 %copy-start.1 = (f32[17,128,128]{2,1,0:T(8,128)}, f32[17,128,128]{2,1,0:T(8,128)S(1)}, u32[]{:S(2)}) copy-start(f32[17,128,128]{2,1,0:T(8,128)S(1)} %collective-permute-done.25.refs_4_) | copy-start | bytes 3342340
  143.3 44.2 %collective-permute-start.12 = (f32[9,128,128]{2,1,0:T(8,128)S(1)}, f32[9,128,128]{2,1,0:T(8,128)S(1)}, u32[]{:S(2)}, u32[]{:S(2)}) collective-permute-start(f32[9,128,128]{2,1,0:T(8,128)S(1)} %select_add_fusion), channel_id=1, source_target_pairs={{0,8},{1,9},{2,10},{3,11},{4,12},{5,13},{6,14},{7,15},{8,16},{9,17... | collective-permute-start | bytes 1769480 | tf_op jit(solution)/shard_map/ppermute | solution.py:380
  145.7 43.7 %copy-start.8 = (f32[17,128,128]{2,1,0:T(8,128)S(1)}, f32[17,128,128]{2,1,0:T(8,128)}, u32[]{:S(2)}) copy-start(f32[17,128,128]{2,1,0:T(8,128)} %get-tuple-element.37) | copy-start | bytes 3342340
  145.7 43.7 %copy-start.9 = (f32[17,128,128]{2,1,0:T(8,128)S(1)}, f32[17,128,128]{2,1,0:T(8,128)}, u32[]{:S(2)}) copy-start(f32[17,128,128]{2,1,0:T(8,128)} %get-tuple-element.41) | copy-start | bytes 3342340
  153.9 44.7 %collective-permute-start.15 = (f32[8,128,128]{2,1,0:T(8,128)S(1)}, f32[8,128,128]{2,1,0:T(8,128)S(1)}, u32[]{:S(2)}, u32[]{:S(2)}) collective-permute-start(f32[8,128,128]{2,1,0:T(8,128)S(1)} %select_add_fusion.2), channel_id=1, source_target_pairs={{0,8},{1,9},{2,10},{3,11},{4,12},{5,13},{6,14},{7,15},{8,16},{9,17... | collective-permute-start | bytes 1572872 | tf_op jit(solution)/shard_map/ppermute | solution.py:380
  158.2 31.4 %copy-start.11 = (f32[16,128,128]{2,1,0:T(8,128)}, f32[16,128,128]{2,1,0:T(8,128)S(1)}, u32[]{:S(2)}) copy-start(f32[16,128,128]{2,1,0:T(8,128)S(1)} %collective-permute-done.20) | copy-start | bytes 3145732
  158.2 67.6 %collective-permute-start.26 = (f32[17,128,128]{2,1,0:T(8,128)S(1)}, f32[17,128,128]{2,1,0:T(8,128)}, u32[]{:S(2)}, u32[]{:S(2)}) collective-permute-start(f32[17,128,128]{2,1,0:T(8,128)S(1)} %broadcast_select_fusion.1), channel_id=1, source_target_pairs={{0,7},{1,0},{2,1},{3,2},{4,3},{5,4},{6,5},{7,6},{8,15},{9,8},{10,9... | collective-permute-start | bytes 3342344 | tf_op jit(solution)/shard_map/ppermute | solution.py:387
  174.8 14.8 %copy-start.12 = (f32[16,128,128]{2,1,0:T(8,128)}, f32[16,128,128]{2,1,0:T(8,128)S(1)}, u32[]{:S(2)}) copy-start(f32[16,128,128]{2,1,0:T(8,128)S(1)} %collective-permute-done.21) | copy-start | bytes 3145732
  174.9 51.0 %collective-permute-start.28 = (f32[17,128,128]{2,1,0:T(8,128)}, f32[17,128,128]{2,1,0:T(8,128)}, u32[]{:S(2)}, u32[]{:S(2)}) collective-permute-start(f32[17,128,128]{2,1,0:T(8,128)} %broadcast_select_fusion), channel_id=1, source_target_pairs={{0,7},{1,0},{2,1},{3,2},{4,3},{5,4},{6,5},{7,6},{8,15},{9,8},{10,9... | collective-permute-start | bytes 3342344 | tf_op jit(solution)/shard_map/ppermute | solution.py:387
  187.5 38.4 %collective-permute-start.29 = (f32[17,128,128]{2,1,0:T(8,128)}, f32[17,128,128]{2,1,0:T(8,128)}, u32[]{:S(2)}, u32[]{:S(2)}) collective-permute-start(f32[17,128,128]{2,1,0:T(8,128)} %collective-permute-done.27.refs_7_), channel_id=1, source_target_pairs={{1,0},{2,1},{3,2},{4,3},{5,4},{6,5},{7,6},{8,7},{9,8},{10,9},{11,1... | collective-permute-start | bytes 3342344 | tf_op jit(solution)/shard_map/ppermute | solution.py:380
  189.6 13.3 %copy-start.4 = (f32[9,128,128]{2,1,0:T(8,128)}, f32[9,128,128]{2,1,0:T(8,128)S(1)}, u32[]{:S(2)}) copy-start(f32[9,128,128]{2,1,0:T(8,128)S(1)} %slice_select_fusion.e0) | copy-start | bytes 1769476
  198.6 27.3 %collective-permute-start.16 = (f32[9,128,128]{2,1,0:T(8,128)S(1)}, f32[9,128,128]{2,1,0:T(8,128)}, u32[]{:S(2)}, u32[]{:S(2)}) collective-permute-start(f32[9,128,128]{2,1,0:T(8,128)S(1)} %slice_select_fusion.e0), channel_id=1, source_target_pairs={{0,32},{32,64},{64,96},{1,33},{33,65},{65,97},{2,34},{34,66},{66,9... | collective-permute-start | bytes 1769480 | tf_op jit(solution)/shard_map/ppermute | solution.py:380
  202.9 10.3 %copy-start.5 = (f32[8,128,128]{2,1,0:T(8,128)}, f32[8,128,128]{2,1,0:T(8,128)S(1)}, u32[]{:S(2)}) copy-start(f32[8,128,128]{2,1,0:T(8,128)S(1)} %slice_select_fusion.1.e1) | copy-start | bytes 1572868
  204.0 21.9 %collective-permute-start.17 = (f32[8,128,128]{2,1,0:T(8,128)S(1)}, f32[8,128,128]{2,1,0:T(8,128)}, u32[]{:S(2)}, u32[]{:S(2)}) collective-permute-start(f32[8,128,128]{2,1,0:T(8,128)S(1)} %slice_select_fusion.1.e1), channel_id=1, source_target_pairs={{0,32},{32,64},{64,96},{1,33},{33,65},{65,97},{2,34},{34,66},{66,9... | collective-permute-start | bytes 1572872 | tf_op jit(solution)/shard_map/ppermute | solution.py:380
  207.3 5.9 %copy-start.15 = (f32[1,2,17,17,4,4]{3,5,4,2,1,0:T(4,128)S(1)}, f32[1,2,17,17,4,4]{3,5,4,2,1,0:T(4,128)}, u32[]{:S(2)}) copy-start(f32[1,2,17,17,4,4]{3,5,4,2,1,0:T(4,128)} %param.16) | copy-start | bytes 110980
  (6 other events, 13.9 us)
